TPU v7x, 32 devices: a whole 2x2x4 slice. The times are simulated.
32 devices in a mesh: ctx: 16 (over z, y, core), wsh: 2 (over x).
Axes of the slice: x: 2, y: 2, z: 4, core: 2. Of those that a mesh axis runs over, the one named last changes fastest.
Arguments:
- tokens: bfloat16 [2, 3, 1024, 1024], P('wsh', None, 'ctx'), may hold values from -6 to 6
- cotangent: bfloat16 [2, 3, 1024, 1024], P('wsh', None, 'ctx'), may hold values from -6 to 6
- lengths: int32 [2, 3, 2], P('wsh'), may hold values from 1 to 512, 768 in all within a row
- dealing: int32 [2, 3, 16], P('wsh'), may hold values from 0 to 15, each once within a row
- w_query: bfloat16 [1024, 1024], P('wsh'), may hold values from -0.1875 to 0.1875
- w_key: bfloat16 [1024, 1024], P('wsh'), may hold values from -0.1875 to 0.1875
- w_value: bfloat16 [1024, 1024], P('wsh'), may hold values from -0.1875 to 0.1875
- w_out: bfloat16 [1024, 1024], P('wsh'), may hold values from -1.5 to 1.5
- w_up: bfloat16 [1024, 4096], P('wsh'), may hold values from -0.1875 to 0.1875
- w_down: bfloat16 [4096, 1024], P('wsh'), may hold values from -0.09375 to 0.09375
- b_query: bfloat16 [1024], P('wsh'), may hold values from -2 to 2
- b_value: bfloat16 [1024], P('wsh'), may hold values from -2 to 2
- b_out: bfloat16 [1024], P('wsh'), may hold values from -2 to 2
- b_up: bfloat16 [4096], P('wsh'), may hold values from -2 to 2
- b_down: bfloat16 [1024], P('wsh'), may hold values from -2 to 2
- gain_one: bfloat16 [1024], P('wsh'), may hold values from 0.5 to 1.5
- shift_one: bfloat16 [1024], P('wsh'), may hold values from -2 to 2
- gain_two: bfloat16 [1024], P('wsh'), may hold values from 0.5 to 1.5
- shift_two: bfloat16 [1024], P('wsh'), may hold values from -2 to 2
Outputs:
- output: bfloat16 [2, 3, 1024, 1024], P('wsh', None, 'ctx')
- grad_tokens: bfloat16 [2, 3, 1024, 1024], P('wsh', None, 'ctx')
- grad_w_query: float32 [1024, 1024], P('wsh')
- grad_w_key: float32 [1024, 1024], P('wsh')
- grad_w_value: float32 [1024, 1024], P('wsh')
- grad_w_out: float32 [1024, 1024], P('wsh')
- grad_w_up: float32 [1024, 4096], P('wsh')
- grad_w_down: float32 [4096, 1024], P('wsh')
- grad_b_query: float32 [1024], P('wsh')
- grad_b_value: float32 [1024], P('wsh')
- grad_b_out: float32 [1024], P('wsh')
- grad_b_up: float32 [4096], P('wsh')
- grad_b_down: float32 [1024], P('wsh')
- grad_gain_one: float32 [1024], P('wsh')
- grad_shift_one: float32 [1024], P('wsh')
- grad_gain_two: float32 [1024], P('wsh')
- grad_shift_two: float32 [1024], P('wsh')
Inputs may be any that keep to these rules, and one draw needn't show every extreme that they name: The 2 lengths of one group add up to 768. `dealing`: for each wsh index and micro-batch, a permutation of the 16 block numbers.
All inputs are finite; a program needn't handle non-finite values.
Results may differ from a plain program's by a relative error of at most 0.023.
Values may be sent and summed in bfloat16 or wider, within the bound.
A program may use at most 192 MiB of HBM per device.

v0:
```python
import math

import jax
import jax.numpy as jnp
from jax import lax
from jax.sharding import PartitionSpec as P

HEADS = 16
BPS = 8
MB = 3
BLK = 64


EPSILON = 1e-12
NEG_FILL = -1e30


def as_sent(x):
    return jax.tree.map(lambda a: a.astype(jnp.bfloat16) if a.dtype == jnp.float32 else a, x)


def layer_norm(summed, gain_vec, shift_vec):
    row_mean = jnp.mean(summed, axis=-1, keepdims=True)
    centred = summed - row_mean
    row_var = jnp.mean(centred * centred, axis=-1, keepdims=True)
    return centred * lax.rsqrt(row_var + EPSILON) * gain_vec + shift_vec


def gelu_exact(values):
    return jax.nn.gelu(values, approximate=False)


def row_labels(dealt_order, seq_lengths):
    blocks_of_rows = jnp.repeat(dealt_order, BLK)
    within = jnp.tile(jnp.arange(BLK, dtype=jnp.int32), dealt_order.shape[0])
    seq_ids = blocks_of_rows // BPS
    places = blocks_of_rows % BPS * BLK + within
    numbers = jnp.arange(seq_lengths.shape[0], dtype=jnp.int32)
    seq_bound = jnp.sum(
        jnp.where(seq_ids[:, None] == numbers[None, :], seq_lengths[None, :], 0), axis=1
    )
    return (seq_ids, places < seq_bound)


def blockwise(carried, total_rows, step_rows, visit_block):
    return lax.fori_loop(
        0,
        total_rows // step_rows,
        lambda turn_index, running: visit_block(running, turn_index * step_rows),
        carried,
    )


def masked_scores(query_blk, key_blk, query_seq, key_seq, key_valid, scale_factor):
    allowed = (query_seq[:, None] == key_seq[None, :]) & key_valid[None, :]
    scores = (
        jnp.einsum("qhd,khd->hqk", query_blk, key_blk, preferred_element_type=jnp.float32)
        * scale_factor
    )
    return (jnp.where(allowed[None], scores, NEG_FILL), allowed[None].astype(jnp.float32))


def attention_grads(
    query_blk,
    grad_blk,
    key_blk,
    value_blk,
    query_seq,
    key_seq,
    key_valid,
    row_total,
    row_delta,
    scale_factor,
):
    scores, allowed = masked_scores(query_blk, key_blk, query_seq, key_seq, key_valid, scale_factor)
    probs = jnp.exp(scores - row_total[:, :, None]) * allowed
    grad_probs = jnp.einsum("qhd,khd->hqk", grad_blk, value_blk, preferred_element_type=jnp.float32)
    grad_scores = (probs * (grad_probs - row_delta[:, :, None])).astype(jnp.bfloat16)
    return (probs.astype(jnp.bfloat16), grad_scores)


def gather_params(params):
    return (
        lax.all_gather(params[0], "wsh", axis=0, tiled=True),
        lax.all_gather(params[1], "wsh", axis=0, tiled=True),
        lax.all_gather(params[2], "wsh", axis=0, tiled=True),
        lax.all_gather(params[3], "wsh", axis=0, tiled=True),
        lax.all_gather(params[4], "wsh", axis=0, tiled=True),
        lax.all_gather(params[5], "wsh", axis=0, tiled=True),
        lax.all_gather(params[6], "wsh", axis=0, tiled=True),
        lax.all_gather(params[7], "wsh", axis=0, tiled=True),
        lax.all_gather(params[8], "wsh", axis=0, tiled=True),
        lax.all_gather(params[9], "wsh", axis=0, tiled=True),
        lax.all_gather(params[10], "wsh", axis=0, tiled=True),
        lax.all_gather(params[11], "wsh", axis=0, tiled=True),
        lax.all_gather(params[12], "wsh", axis=0, tiled=True),
        lax.all_gather(params[13], "wsh", axis=0, tiled=True),
        lax.all_gather(params[14], "wsh", axis=0, tiled=True),
    )


def per_device(
    tokens,
    cotangent,
    lengths,
    dealing,
    w_query,
    w_key,
    w_value,
    w_out,
    w_up,
    w_down,
    b_query,
    b_value,
    b_out,
    b_up,
    b_down,
    gain_one,
    shift_one,
    gain_two,
    shift_two,
):
    params = (
        w_query,
        w_key,
        w_value,
        w_out,
        w_up,
        w_down,
        b_query,
        b_value,
        b_out,
        b_up,
        b_down,
        gain_one,
        shift_one,
        gain_two,
        shift_two,
    )
    own_rows = tokens.shape[2]
    width = tokens.shape[3]
    head_size = width // HEADS
    scale_factor = 1.0 / math.sqrt(head_size)
    my_start = lax.axis_index("ctx") * own_rows
    wsh_count = lax.axis_size("wsh")
    grads = tuple(
        (jnp.zeros((item.shape[0] * wsh_count,) + item.shape[1:], jnp.float32) for item in params)
    )
    results = []
    input_grads = []
    for micro in range(MB):
        whole = gather_params(params)
        query_weight, key_weight, value_weight, out_weight, up_weight, down_weight = whole[:6]
        (
            bias_query,
            bias_value,
            bias_out,
            bias_up,
            bias_down,
            gain_first,
            shift_first,
            gain_second,
            shift_second,
        ) = tuple((item.astype(jnp.float32) for item in whole[6:]))
        token_rows = tokens[0, micro]
        seq_all, valid_all = row_labels(dealing[0, micro], lengths[0, micro])
        my_seq = lax.dynamic_slice_in_dim(seq_all, my_start, own_rows)
        my_valid = lax.dynamic_slice_in_dim(valid_all, my_start, own_rows)
        query_low = (
            jnp.dot(token_rows, query_weight, preferred_element_type=jnp.float32) + bias_query
        ).astype(jnp.bfloat16)
        key_low = jnp.dot(token_rows, key_weight, preferred_element_type=jnp.float32).astype(
            jnp.bfloat16
        )
        value_low = (
            jnp.dot(token_rows, value_weight, preferred_element_type=jnp.float32) + bias_value
        ).astype(jnp.bfloat16)
        query_heads = query_low.reshape(own_rows, HEADS, head_size)
        my_key_heads = key_low.reshape(own_rows, HEADS, head_size)
        my_value_heads = value_low.reshape(own_rows, HEADS, head_size)
        start_state = (
            jnp.full((HEADS, own_rows), NEG_FILL, jnp.float32),
            jnp.zeros((HEADS, own_rows), jnp.float32),
            jnp.zeros((own_rows, HEADS, head_size), jnp.float32),
        )
        key_piece = lax.all_gather(key_low, "ctx", axis=0, tiled=True)
        value_piece = lax.all_gather(value_low, "ctx", axis=0, tiled=True)
        piece_rows = key_piece.shape[0]
        step_rows = math.gcd(piece_rows, 512)

        def visit_block(running, offset):
            run_max, run_sum, run_acc = running
            key_blk = lax.dynamic_slice_in_dim(key_piece, offset, step_rows).reshape(
                step_rows, HEADS, head_size
            )
            value_blk = lax.dynamic_slice_in_dim(value_piece, offset, step_rows).reshape(
                step_rows, HEADS, head_size
            )
            key_seq = lax.dynamic_slice_in_dim(seq_all, offset, step_rows)
            key_valid = lax.dynamic_slice_in_dim(valid_all, offset, step_rows)
            scores, allowed = masked_scores(
                query_heads, key_blk, my_seq, key_seq, key_valid, scale_factor
            )
            new_max = jnp.maximum(run_max, jnp.max(scores, axis=-1))
            rescale = jnp.exp(run_max - new_max)
            weights = jnp.exp(scores - new_max[:, :, None]) * allowed
            run_sum = run_sum * rescale + jnp.sum(weights, axis=-1)
            run_acc = run_acc * rescale.T[:, :, None] + jnp.einsum(
                "hqk,khd->qhd",
                weights.astype(jnp.bfloat16),
                value_blk,
                preferred_element_type=jnp.float32,
            )
            return (new_max, run_sum, run_acc)

        final_max, final_sum, final_acc = blockwise(start_state, piece_rows, step_rows, visit_block)
        attended = final_acc / final_sum.T[:, :, None]
        log_total = final_max + jnp.log(final_sum)
        attended_low = attended.reshape(own_rows, width).astype(jnp.bfloat16)
        out_proj = jnp.dot(attended_low, out_weight, preferred_element_type=jnp.float32) + bias_out
        first_sum = token_rows.astype(jnp.float32) + out_proj
        norm_one, norm_one_back = jax.vjp(layer_norm, first_sum, gain_first, shift_first)
        mlp_input = norm_one.astype(jnp.bfloat16)
        up_pre = jnp.dot(mlp_input, up_weight, preferred_element_type=jnp.float32) + bias_up
        activated, gelu_back = jax.vjp(gelu_exact, up_pre)
        activated_low = activated.astype(jnp.bfloat16)
        down_out = (
            jnp.dot(activated_low, down_weight, preferred_element_type=jnp.float32) + bias_down
        )
        result, norm_two_back = jax.vjp(layer_norm, norm_one + down_out, gain_second, shift_second)
        results.append(result.astype(jnp.bfloat16))
        grad_second, grad_gain_b, grad_shift_b = norm_two_back(
            cotangent[0, micro].astype(jnp.float32)
        )
        grad_down_low = grad_second.astype(jnp.bfloat16)
        grad_activated = jnp.einsum(
            "rd,fd->rf", grad_down_low, down_weight, preferred_element_type=jnp.float32
        )
        (grad_up_pre,) = gelu_back(grad_activated)
        grad_up_low = grad_up_pre.astype(jnp.bfloat16)
        grad_norm_one = (
            jnp.einsum("rf,df->rd", grad_up_low, up_weight, preferred_element_type=jnp.float32)
            + grad_second
        )
        grad_first, grad_gain_a, grad_shift_a = norm_one_back(grad_norm_one)
        grad_out_low = grad_first.astype(jnp.bfloat16)
        grad_att_low = jnp.einsum(
            "rd,ed->re", grad_out_low, out_weight, preferred_element_type=jnp.float32
        ).astype(jnp.bfloat16)
        grad_heads = grad_att_low.reshape(own_rows, HEADS, head_size)
        row_delta = jnp.sum(grad_heads.astype(jnp.float32) * attended, axis=-1).T
        empty_heads = jnp.zeros((own_rows, HEADS, head_size), jnp.float32)
        query_key_piece = lax.all_gather(key_low, "ctx", axis=0, tiled=True)
        query_value_piece = lax.all_gather(value_low, "ctx", axis=0, tiled=True)
        query_piece_rows = query_key_piece.shape[0]
        query_step_rows = math.gcd(query_piece_rows, 512)

        def query_visit_block(running, offset):
            key_blk = lax.dynamic_slice_in_dim(query_key_piece, offset, query_step_rows).reshape(
                query_step_rows, HEADS, head_size
            )
            value_blk = lax.dynamic_slice_in_dim(
                query_value_piece, offset, query_step_rows
            ).reshape(query_step_rows, HEADS, head_size)
            key_seq = lax.dynamic_slice_in_dim(seq_all, offset, query_step_rows)
            key_valid = lax.dynamic_slice_in_dim(valid_all, offset, query_step_rows)
            probs_low, grad_scores = attention_grads(
                query_heads,
                grad_heads,
                key_blk,
                value_blk,
                my_seq,
                key_seq,
                key_valid,
                log_total,
                row_delta,
                scale_factor,
            )
            return running + jnp.einsum(
                "hqk,khd->qhd", grad_scores, key_blk, preferred_element_type=jnp.float32
            )

        grad_query_sum = blockwise(
            empty_heads, query_piece_rows, query_step_rows, query_visit_block
        )
        total_all, delta_all = (
            lax.all_gather(log_total.T, "ctx", axis=0, tiled=True),
            lax.all_gather(row_delta.T, "ctx", axis=0, tiled=True),
        )
        query_piece = lax.all_gather(query_low, "ctx", axis=0, tiled=True)
        grad_piece = lax.all_gather(grad_att_low, "ctx", axis=0, tiled=True)
        key_piece_rows = query_piece.shape[0]
        key_step_rows = math.gcd(key_piece_rows, 512)

        def key_visit_block(running, offset):
            grad_key_run, grad_value_run = running
            query_blk = lax.dynamic_slice_in_dim(query_piece, offset, key_step_rows).reshape(
                key_step_rows, HEADS, head_size
            )
            grad_blk = lax.dynamic_slice_in_dim(grad_piece, offset, key_step_rows).reshape(
                key_step_rows, HEADS, head_size
            )
            total_blk = lax.dynamic_slice_in_dim(total_all, offset, key_step_rows)
            delta_blk = lax.dynamic_slice_in_dim(delta_all, offset, key_step_rows)
            query_seq = lax.dynamic_slice_in_dim(seq_all, offset, key_step_rows)
            probs_low, grad_scores = attention_grads(
                query_blk,
                grad_blk,
                my_key_heads,
                my_value_heads,
                query_seq,
                my_seq,
                my_valid,
                total_blk.T,
                delta_blk.T,
                scale_factor,
            )
            grad_key_run = grad_key_run + jnp.einsum(
                "hqk,qhd->khd", grad_scores, query_blk, preferred_element_type=jnp.float32
            )
            grad_value_run = grad_value_run + jnp.einsum(
                "hqk,qhd->khd", probs_low, grad_blk, preferred_element_type=jnp.float32
            )
            return (grad_key_run, grad_value_run)

        grad_key_sum, grad_value_sum = blockwise(
            (empty_heads, empty_heads), key_piece_rows, key_step_rows, key_visit_block
        )
        grad_key_flat = grad_key_sum.reshape(own_rows, width)
        grad_value_flat = grad_value_sum.reshape(own_rows, width)
        grad_query_low = (
            (grad_query_sum * scale_factor).reshape(own_rows, width).astype(jnp.bfloat16)
        )
        grad_key_low = (grad_key_flat * scale_factor).astype(jnp.bfloat16)
        grad_value_low = grad_value_flat.astype(jnp.bfloat16)
        terms = (
            jnp.einsum("rd,re->de", token_rows, grad_query_low, preferred_element_type=jnp.float32),
            jnp.einsum("rd,re->de", token_rows, grad_key_low, preferred_element_type=jnp.float32),
            jnp.einsum("rd,re->de", token_rows, grad_value_low, preferred_element_type=jnp.float32),
            jnp.einsum("rd,re->de", attended_low, grad_out_low, preferred_element_type=jnp.float32),
            jnp.einsum("rd,rf->df", mlp_input, grad_up_low, preferred_element_type=jnp.float32),
            jnp.einsum(
                "rf,rd->fd", activated_low, grad_down_low, preferred_element_type=jnp.float32
            ),
            jnp.sum(grad_query_low.astype(jnp.float32), axis=0),
            jnp.sum(grad_value_low.astype(jnp.float32), axis=0),
            jnp.sum(grad_out_low.astype(jnp.float32), axis=0),
            jnp.sum(grad_up_low.astype(jnp.float32), axis=0),
            jnp.sum(grad_down_low.astype(jnp.float32), axis=0),
            grad_gain_a,
            grad_shift_a,
            grad_gain_b,
            grad_shift_b,
        )
        grads = tuple((total_now + fresh for total_now, fresh in zip(grads, terms)))
        grad_rows = (
            grad_first
            + jnp.einsum(
                "re,de->rd", grad_query_low, query_weight, preferred_element_type=jnp.float32
            )
            + jnp.einsum("re,de->rd", grad_key_low, key_weight, preferred_element_type=jnp.float32)
            + jnp.einsum(
                "re,de->rd", grad_value_low, value_weight, preferred_element_type=jnp.float32
            )
        )
        input_grads.append(grad_rows.astype(jnp.bfloat16))
    shards = jax.tree.map(
        lambda part: part.astype(jnp.float32),
        lax.psum_scatter(as_sent(grads), "wsh", scatter_dimension=0, tiled=True),
    )
    summed = jax.tree.map(lambda part: part.astype(jnp.float32), lax.psum(as_sent(shards), "ctx"))
    return (jnp.stack(results)[None], jnp.stack(input_grads)[None]) + tuple(summed)


def solution(mesh):
    placed = (
        P("wsh", None, "ctx", None),
        P("wsh", None, "ctx", None),
        P("wsh", None, None),
        P("wsh", None, None),
        P("wsh", None),
        P("wsh", None),
        P("wsh", None),
        P("wsh", None),
        P("wsh", None),
        P("wsh", None),
        P("wsh"),
        P("wsh"),
        P("wsh"),
        P("wsh"),
        P("wsh"),
        P("wsh"),
        P("wsh"),
        P("wsh"),
        P("wsh"),
    )
    return jax.shard_map(
        per_device,
        mesh=mesh,
        in_specs=placed,
        out_specs=(
            P("wsh", None, "ctx", None),
            P("wsh", None, "ctx", None),
            P("wsh", None),
            P("wsh", None),
            P("wsh", None),
            P("wsh", None),
            P("wsh", None),
            P("wsh", None),
            P("wsh"),
            P("wsh"),
            P("wsh"),
            P("wsh"),
            P("wsh"),
            P("wsh"),
            P("wsh"),
            P("wsh"),
            P("wsh"),
        ),
        check_vma=False,
    )
```

profile of v0, /device:TPU:0, one launch (start us, length us, event | category | flops | bytes accessed | tf_op | source)
XLA Modules:
  0.0 1500.0 jit_solution(13445184941101564481)
XLA Ops:
  9.5 35.9 %all-gather.33.cloned.1.call-done = bf16[1024,1024]{1,0:T(8,128)(2,1)} async-done(((bf16[512,1024]{1,0:T(8,128)(2,1)}), bf16[1024,1024]{1,0:T(8,128)(2,1)}) %all-gather.33.cloned.1.call-update) | async-done | bytes 2097168 | tf_op jit(solution)/shard_map/all_gather | solution.py:85
  52.7 27.4 %all-gather.39.cloned.1.call-done = bf16[1024,1024]{1,0:T(8,128)(2,1)} async-done(((bf16[512,1024]{1,0:T(8,128)(2,1)}), bf16[1024,1024]{1,0:T(8,128)(2,1)}) %all-gather.39.cloned.1.call-update) | async-done | bytes 2097168 | tf_op jit(solution)/shard_map/all_gather | solution.py:86
  162.5 38.3 %all-gather.55.cloned.1.call-done = bf16[1024,1024]{1,0:T(8,128)(2,1)} async-done(((bf16[64,1024]{1,0:T(8,128)(2,1)}), bf16[1024,1024]{1,0:T(8,128)(2,1)}) %all-gather.55.cloned.1.call-update) | async-done | bytes 2097168 | tf_op jit(solution)/shard_map/all_gather | solution.py:187
  237.0 40.6 %all-gather.49.cloned.1.call-done = bf16[1024,1024]{1,0:T(8,128)(2,1)} async-done(((bf16[64,1024]{1,0:T(8,128)(2,1)}), bf16[1024,1024]{1,0:T(8,128)(2,1)}) %all-gather.49.cloned.1.call-update) | async-done | bytes 2097168 | tf_op jit(solution)/shard_map/all_gather | solution.py:186
  281.6 38.4 %all-gather.51.cloned.1.call-done = bf16[1024,1024]{1,0:T(8,128)(2,1)} async-done(((bf16[64,1024]{1,0:T(8,128)(2,1)}), bf16[1024,1024]{1,0:T(8,128)(2,1)}) %all-gather.51.cloned.1.call-update) | async-done | bytes 2097168 | tf_op jit(solution)/shard_map/all_gather | solution.py:187
  341.3 21.2 %all-gather.35.cloned.1.call-done = bf16[1024,1024]{1,0:T(8,128)(2,1)} async-done(((bf16[64,1024]{1,0:T(8,128)(2,1)}), bf16[1024,1024]{1,0:T(8,128)(2,1)}) %all-gather.35.cloned.1.call-update) | async-done | bytes 2097168 | tf_op jit(solution)/shard_map/all_gather | solution.py:186
  366.4 38.2 %all-gather.41.cloned.1.call-done = bf16[1024,1024]{1,0:T(8,128)(2,1)} async-done(((bf16[64,1024]{1,0:T(8,128)(2,1)}), bf16[1024,1024]{1,0:T(8,128)(2,1)}) %all-gather.41.cloned.1.call-update) | async-done | bytes 2097168 | tf_op jit(solution)/shard_map/all_gather | solution.py:187
  408.6 18.9 %while.144 = (s32[]{:T(128)}, f32[16,64]{1,0:T(8,128)S(1)}, f32[16,64]{1,0:T(8,128)}, f32[64,16,64]{0,2,1:T(8,128)}, s32[64]{0:T(128)}, /*index=5*/s32[1024]{0:T...) while((s32[]{:T(128)}, f32[16,64]{1,0:T(8,128)S(1)}, ...), condition=%wide.region_4.5_spmd.clone, body=%wide.region_1.4_spmd.clone.sunk | while | flops 141334528 | bytes 16228475 | solution.py:46
  431.3 77.7 %all-gather.45.cloned.1.call-done = bf16[1024,4096]{1,0:T(8,128)(2,1)} async-done(((bf16[512,4096]{1,0:T(8,128)(2,1)}), bf16[1024,4096]{1,0:T(8,128)(2,1)}) %all-gather.45.cloned.1.call-update) | async-done | bytes 8388624 | tf_op jit(solution)/shard_map/all_gather | solution.py:88
  517.1 97.4 %all-gather.47.cloned.1.call-done = bf16[4096,1024]{1,0:T(8,128)(2,1)} async-done(((bf16[2048,1024]{1,0:T(8,128)(2,1)}), bf16[4096,1024]{1,0:T(8,128)(2,1)}) %all-gather.47.cloned.1.call-update) | async-done | bytes 8388624 | tf_op jit(solution)/shard_map/all_gather | solution.py:89
  676.6 19.5 %while.151 = (s32[]{:T(128)}, f32[64,16,64]{0,2,1:T(8,128)}, bf16[1024,1024]{0,1:T(8,128)(2,1)}, s32[64]{0:T(128)}, s32[1024]{0:T(1024)S(1)}, /*index=5*/pred[10...) while((s32[]{:T(128)}, f32[64,16,64]{0,2,1:T(8,128)}, ...), condition=%wide.region_51.52_spmd.clone, body=%wide.region_50.51_spmd.clone.sunk | while | flops 205225984 | bytes 12664793 | solution.py:46
  719.6 18.5 %while.147 = (s32[]{:T(128)}, f32[64,16,64]{0,2,1:T(8,128)}, bf16[1024,1024]{0,1:T(8,128)(2,1)}, s32[64]{0:T(128)}, s32[1024]{0:T(1024)}, /*index=5*/pred[1024]{...) while((s32[]{:T(128)}, f32[64,16,64]{0,2,1:T(8,128)}, ...), condition=%wide.region_33.34_spmd.clone, body=%wide.region_32.33_spmd.clone.sunk | while | flops 205225984 | bytes 12664793 | solution.py:46
  754.0 21.9 %all-gather.12 = f32[16,64,16]{1,2,0:T(8,128)S(1)} all-gather(f32[1,64,16]{1,2,0:T(8,128)S(1)} %bitcast.786), channel_id=1, replica_groups=mesh['ctx'=16,'wsh'=2] {'ctx'}, dimensions={0}, use_global_device_ids=true | all-gather | bytes 69632 | tf_op jit(solution)/shard_map/all_gather | solution.py:287
  795.3 19.2 %all-gather.8 = f32[16,64,16]{1,2,0:T(8,128)S(1)} all-gather(f32[1,64,16]{1,2,0:T(8,128)S(1)} %bitcast.784), channel_id=1, replica_groups=mesh['ctx'=16,'wsh'=2] {'ctx'}, dimensions={0}, use_global_device_ids=true | all-gather | bytes 69632 | tf_op jit(solution)/shard_map/all_gather | solution.py:287
  815.6 17.8 %all-gather.13 = f32[16,64,16]{1,2,0:T(8,128)S(1)} all-gather(f32[1,64,16]{1,2,0:T(8,128)S(1)} %copy.258), channel_id=1, replica_groups=mesh['ctx'=16,'wsh'=2] {'ctx'}, dimensions={0}, use_global_device_ids=true | all-gather | bytes 69632 | tf_op jit(solution)/shard_map/all_gather | solution.py:288
  834.2 19.1 %all-gather.11 = f32[16,64,16]{1,2,0:T(8,128)S(1)} all-gather(f32[1,64,16]{1,2,0:T(8,128)S(1)} %copy.244), channel_id=1, replica_groups=mesh['ctx'=16,'wsh'=2] {'ctx'}, dimensions={0}, use_global_device_ids=true | all-gather | bytes 69632 | tf_op jit(solution)/shard_map/all_gather | solution.py:288
  854.2 18.3 %all-gather.9 = f32[16,64,16]{1,2,0:T(8,128)S(1)} all-gather(f32[1,64,16]{1,2,0:T(8,128)S(1)} %copy.230), channel_id=1, replica_groups=mesh['ctx'=16,'wsh'=2] {'ctx'}, dimensions={0}, use_global_device_ids=true | all-gather | bytes 69632 | tf_op jit(solution)/shard_map/all_gather | solution.py:288
  877.3 26.6 %while.152 = (s32[]{:T(128)}, f32[64,16,64]{0,2,1:T(8,128)}, f32[64,16,64]{0,2,1:T(8,128)}, bf16[1024,1024]{1,0:T(8,128)(2,1)}, s32[1024]{0:T(1024)S(1)}, /*inde...) while((s32[]{:T(128)}, f32[64,16,64]{0,2,1:T(8,128)}, ...), condition=%wide.region_53.54_spmd.clone, body=%wide.region_52.53_spmd.clone.sunk | while | flops 272990208 | bytes 24910396 | solution.py:46
  905.8 24.3 %while.150 = (s32[]{:T(128)}, f32[64,16,64]{0,2,1:T(8,128)}, f32[64,16,64]{0,2,1:T(8,128)}, bf16[1024,1024]{1,0:T(8,128)(2,1)}, s32[1024]{0:T(1024)S(1)}, /*inde...) while((s32[]{:T(128)}, f32[64,16,64]{0,2,1:T(8,128)}, ...), condition=%wide.region_44.45_spmd.clone, body=%wide.region_43.44_spmd.clone.sunk | while | flops 272990208 | bytes 25435024 | solution.py:46
  931.9 26.3 %while.148 = (s32[]{:T(128)}, f32[64,16,64]{0,2,1:T(8,128)}, f32[64,16,64]{0,2,1:T(8,128)}, bf16[1024,1024]{1,0:T(8,128)(2,1)}, s32[1024]{0:T(1024)}, /*index=5*...) while((s32[]{:T(128)}, f32[64,16,64]{0,2,1:T(8,128)}, ...), condition=%wide.region_35.36_spmd.clone, body=%wide.region_34.35_spmd.clone.sunk | while | flops 272990208 | bytes 25434740 | solution.py:46
  1036.5 93.2 %reduce-scatter.15.cloned.1.call-done = bf16[512,4096]{1,0:T(8,128)(2,1)} async-done(((bf16[1024,4096]{1,0:T(8,128)(2,1)}), bf16[512,4096]{1,0:T(8,128)(2,1)}) %reduce-scatter.15.cloned.1.call-update) | async-done | bytes 4194320 | tf_op jit(solution)/shard_map/reduce_scatter | solution.py:369
  1129.6 102.1 %reduce-scatter.17.cloned.1.call-done = bf16[2048,1024]{1,0:T(8,128)(2,1)} async-done(((bf16[4096,1024]{1,0:T(8,128)(2,1)}), bf16[2048,1024]{1,0:T(8,128)(2,1)}) %reduce-scatter.17.cloned.1.call-update) | async-done | bytes 4194320 | tf_op jit(solution)/shard_map/reduce_scatter | solution.py:369
  1258.6 64.5 %all-reduce.9 = (bf16[512]{0:T(512)(128)(2,1)S(1)}, bf16[512]{0:T(512)(128)(2,1)S(1)}, bf16[512]{0:T(512)(128)(2,1)S(1)}, bf16[2048]{0:T(1024)(128)(2,1)S(1)}, b...) all-reduce(bf16[512]{0:T(512)(128)(2,1)S(1)} %dynamic-slice.1, ...), channel_id=1, replica_groups=mesh['ctx'=16,'wsh'=2] {'ctx'}, use_global_device_ids=true, to_apply=%region_70.71 | all-reduce | flops 6144 | bytes 24576 | tf_op jit(solution)/shard_map/psum | solution.py:371
  1334.7 139.6 %all-reduce.14.cloned.1.call-done = (bf16[512,1024]{0,1:T(8,128)(2,1)}, bf16[512,1024]{0,1:T(8,128)(2,1)}, bf16[512,1024]{0,1:T(8,128)(2,1)}, bf16[512,1024]{1,0...) async-done(((bf16[512,1024]{0,1:T(8,128)(2,1)}, bf16[512,1024]{0,1:T(8,128)(2,1)}, bf16[512,1024]{0,1:T(8,128)(2,1)}, bf16[512,1024]{1,0:T(8,128)(2,1)}, ...) | async-done | bytes 12582928 | tf_op jit(solution)/shard_map/psum | solution.py:371
  (934 shorter events, 615.3 us)
Async XLA Ops:
  7.9 72.2 %all-gather.39.cloned.1.call-start = ((), (), s32[]{:S(2)}) async-start(), calls=%async_computation.9 | async-start | bytes 3145728 | tf_op jit(solution)/shard_map/all_gather | solution.py:86
  8.7 127.7 %all-gather.37.cloned.1.call-start = ((), (), s32[]{:S(2)}) async-start(), calls=%async_computation.8 | async-start | bytes 3145728 | tf_op jit(solution)/shard_map/all_gather | solution.py:84
  9.4 149.1 %all-gather.53.cloned.1.call-start = ((), (), s32[]{:S(2)}) async-start(), calls=%async_computation.16 | async-start | bytes 2228224 | tf_op jit(solution)/shard_map/all_gather | solution.py:186
  48.2 152.6 %all-gather.55.cloned.1.call-start = ((), (), s32[]{:S(2)}) async-start(), calls=%async_computation.17 | async-start | bytes 2228224 | tf_op jit(solution)/shard_map/all_gather | solution.py:187
  82.9 151.2 %all-gather.43.cloned.1.call-start = ((), (), s32[]{:S(2)}) async-start(), calls=%async_computation.11 | async-start | bytes 3145728 | tf_op jit(solution)/shard_map/all_gather | solution.py:87
  83.5 194.2 %all-gather.49.cloned.1.call-start = ((), (), s32[]{:S(2)}) async-start(), calls=%async_computation.14 | async-start | bytes 2228224 | tf_op jit(solution)/shard_map/all_gather | solution.py:186
  84.7 235.3 %all-gather.51.cloned.1.call-start = ((), (), s32[]{:S(2)}) async-start(), calls=%async_computation.15 | async-start | bytes 2228224 | tf_op jit(solution)/shard_map/all_gather | solution.py:187
  87.5 275.0 %all-gather.35.cloned.1.call-start = ((), (), s32[]{:S(2)}) async-start(), calls=%async_computation.7 | async-start | bytes 2228224 | tf_op jit(solution)/shard_map/all_gather | solution.py:186
  88.7 316.0 %all-gather.41.cloned.1.call-start = ((), (), s32[]{:S(2)}) async-start(), calls=%async_computation.10 | async-start | bytes 2228224 | tf_op jit(solution)/shard_map/all_gather | solution.py:187
  91.6 417.3 %all-gather.45.cloned.1.call-start = ((), (), s32[]{:S(2)}) async-start(), calls=%async_computation.12 | async-start | bytes 12582912 | tf_op jit(solution)/shard_map/all_gather | solution.py:88
  92.5 521.9 %all-gather.47.cloned.1.call-start = ((), (), s32[]{:S(2)}) async-start(), calls=%async_computation.13 | async-start | bytes 12582912 | tf_op jit(solution)/shard_map/all_gather | solution.py:89
  93.1 784.2 %all-gather.65.cloned.1.call-start = ((), (), s32[]{:S(2)}) async-start(), calls=%async_computation.22 | async-start | bytes 2228224 | tf_op jit(solution)/shard_map/all_gather | solution.py:290
  141.8 735.5 %all-gather.67.cloned.1.call-start = ((), (), s32[]{:S(2)}) async-start(), calls=%async_computation.23 | async-start | bytes 2228224 | tf_op jit(solution)/shard_map/all_gather | solution.py:291
  659.7 246.1 %all-gather.61.cloned.1.call-start = ((), (), s32[]{:S(2)}) async-start(), calls=%async_computation.20 | async-start | bytes 2228224 | tf_op jit(solution)/shard_map/all_gather | solution.py:290
  660.3 245.5 %all-gather.63.cloned.1.call-start = ((), (), s32[]{:S(2)}) async-start(), calls=%async_computation.21 | async-start | bytes 2228224 | tf_op jit(solution)/shard_map/all_gather | solution.py:291
  663.2 268.7 %all-gather.57.cloned.1.call-start = ((), (), s32[]{:S(2)}) async-start(), calls=%async_computation.18 | async-start | bytes 2228224 | tf_op jit(solution)/shard_map/all_gather | solution.py:290
  663.7 268.1 %all-gather.59.cloned.1.call-start = ((), (), s32[]{:S(2)}) async-start(), calls=%async_computation.19 | async-start | bytes 2228224 | tf_op jit(solution)/shard_map/all_gather | solution.py:291
  713.6 322.8 %reduce-scatter.7.cloned.1.call-start = ((), (), s32[]{:S(2)}) async-start(), calls=%async_computation.24 | async-start | bytes 3145728 | tf_op jit(solution)/shard_map/reduce_scatter | solution.py:369
  744.7 291.7 %reduce-scatter.13.cloned.1.call-start = ((), (), s32[]{:S(2)}) async-start(), calls=%async_computation.27 | async-start | bytes 3145728 | tf_op jit(solution)/shard_map/reduce_scatter | solution.py:369
  877.2 159.2 %reduce-scatter.9.cloned.1.call-start = ((), (), s32[]{:S(2)}) async-start(), calls=%async_computation.25 | async-start | bytes 3145728 | tf_op jit(solution)/shard_map/reduce_scatter | solution.py:369
  963.3 73.2 %reduce-scatter.11.cloned.1.call-start = ((), (), s32[]{:S(2)}) async-start(), calls=%async_computation.26 | async-start | bytes 3145728 | tf_op jit(solution)/shard_map/reduce_scatter | solution.py:369
  970.2 159.4 %reduce-scatter.15.cloned.1.call-start = ((), (), s32[]{:S(2)}) async-start(), calls=%async_computation.28 | async-start | bytes 12582912 | tf_op jit(solution)/shard_map/reduce_scatter | solution.py:369
  1003.4 228.3 %reduce-scatter.17.cloned.1.call-start = ((), (), s32[]{:S(2)}) async-start(), calls=%async_computation.29 | async-start | bytes 12582912 | tf_op jit(solution)/shard_map/reduce_scatter | solution.py:369
  1036.3 437.9 %all-reduce.14.cloned.1.call-start = ((), (), s32[]{:S(2)}) async-start(), calls=%async_computation.30 | async-start | bytes 25165824 | tf_op jit(solution)/shard_map/psum | solution.py:371
  (225 other events, 4126.4 us)
Sparse Core Ops, SparseCore 0:
  9.6 35.7 all-gather.32
  47.0 33.1 all-gather.38
  81.7 33.3 all-gather.36
  117.1 41.3 all-gather.52
  160.5 40.1 all-gather.54
  202.1 31.8 all-gather.42
  236.2 41.3 all-gather.48
  279.8 40.1 all-gather.50
  322.2 40.2 all-gather.34
  364.4 40.1 all-gather.40
  406.2 102.7 all-gather.44
  510.4 103.9 all-gather.46
  616.6 41.5 all-gather.64
  660.2 41.0 all-gather.66
  703.2 40.1 all-gather.60
  745.5 40.1 all-gather.62
  787.7 40.6 all-gather.56
  830.4 40.9 all-gather.58
  874.2 30.6 reduce-scatter.6
  907.6 31.8 reduce-scatter.12
  995.6 31.8 reduce-scatter.10
  1030.4 99.2 reduce-scatter.14
  1132.5 99.2 reduce-scatter.16
  1236.9 237.3 all-reduce.13
  (1 shorter events, 29.2 us)
where the time goes:
time: 1510 us; the launch traced here: 1500 us
  waiting for transfers between devices  782 us (52%)
  matrix products  231 us (15%)
  blocking collectives  225 us (15%)
  local copies, waits for them, and re-layouts  151 us (10%)
  other arithmetic  90 us (6%)
  between operations  17.9 us (1%)
    reduce_scatter x6, waiting for transfers between devices, per_device(): lax.psum_scatter(as_sent(grads), 'wsh', scatter_dimension=0, tiled=True)  195 us
    psum x1, waiting for transfers between devices, per_device(): lax.psum(as_sent(shards), 'ctx')  140 us
    all_gather x3, waiting for transfers between devices, per_device(): value_piece = lax.all_gather(value_low, 'ctx', axis=0, tiled=True)  115 us
    all_gather x1, waiting for transfers between devices, gather_params(): lax.all_gather(params[5], 'wsh', axis=0, tiled=True)  97.4 us
    all_gather x3, waiting for transfers between devices, per_device(): key_piece = lax.all_gather(key_low, 'ctx', axis=0, tiled=True)  78.3 us
    all_gather x1, waiting for transfers between devices, gather_params(): lax.all_gather(params[4], 'wsh', axis=0, tiled=True)  77.7 us
    psum x1, blocking collectives, per_device(): lax.psum(as_sent(shards), 'ctx')  64.5 us
    all_gather x3, blocking collectives, per_device(): lax.all_gather(log_total.T, 'ctx', axis=0, tiled=True)  58.9 us
  transfers between devices with their start and end apart: 25, of which 14 were waited for; matrix products, arithmetic and copies ran while one was open for 29% of the time, Pallas kernels for 0%

commit v1 on v0

--- a/solution.py
+++ b/solution.py
@@ -1,8 +1,11 @@
+import functools
 import math
 
 import jax
 import jax.numpy as jnp
 from jax import lax
+from jax.experimental import pallas as pl
+from jax.experimental.pallas import tpu as pltpu
 from jax.sharding import PartitionSpec as P
 
 HEADS = 16
@@ -372,6 +375,771 @@
     return (jnp.stack(results)[None], jnp.stack(input_grads)[None]) + tuple(summed)
 
 
+MESH_IDS = pl.DeviceIdType.MESH
+F32 = jnp.float32
+BF16 = jnp.bfloat16
+HD = 64
+VMEM_BYTES = 60 * 1024 * 1024
+
+
+def flip(index, bit):
+    return index + bit * (1 - 2 * lax.rem(lax.div(index, bit), 2))
+
+
+def bit_of(index, bit):
+    return lax.rem(lax.div(index, bit), 2)
+
+
+def greet(peers):
+    barrier = pltpu.get_barrier_semaphore()
+    for peer in peers:
+        pl.semaphore_signal(barrier, inc=1, device_id=peer, device_id_type=MESH_IDS)
+    pl.semaphore_wait(barrier, len(peers))
+
+
+def send(src, dst, send_sem, recv_sem, peer):
+    copy = pltpu.make_async_remote_copy(
+        src_ref=src,
+        dst_ref=dst,
+        send_sem=send_sem,
+        recv_sem=recv_sem,
+        device_id=peer,
+        device_id_type=MESH_IDS,
+    )
+    copy.start()
+    return copy
+
+
+def gather_kernel(plan, n_weights, *refs):
+    shards, small = refs[:n_weights], refs[n_weights]
+    wholes, small_whole = refs[n_weights + 1 : 2 * n_weights + 1], refs[2 * n_weights + 1]
+    send_sem, recv_sem, small_sems, local_sem = refs[2 * n_weights + 2 :]
+    c, w = lax.axis_index("ctx"), lax.axis_index("wsh")
+    o = 1 - w
+    by_x, by_y, by_z, by_core = (c, o), (flip(c, 2), w), (flip(c, 4), w), (flip(c, 1), w)
+    core, y, z = bit_of(c, 1), bit_of(c, 2), bit_of(c, 4)
+    mine = core * 4 + z * 2 + y
+    from_y, from_z = core * 4 + z * 2 + (1 - y), core * 4 + (1 - z) * 2 + y
+    locals_ = []
+    for index, (shard, whole) in enumerate(zip(shards, wholes)):
+        rows = shard.shape[0]
+        copy = pltpu.make_async_copy(
+            shard, whole.at[pl.ds(pl.multiple_of(w * rows, rows), rows)], local_sem.at[index]
+        )
+        copy.start()
+        locals_.append(copy)
+    copy = pltpu.make_async_copy(small, small_whole.at[w], local_sem.at[n_weights])
+    copy.start()
+    locals_.append(copy)
+    greet((by_x, by_y, by_z, by_core))
+    sent = [send(small, small_whole.at[w], small_sems.at[0], small_sems.at[1], by_x)]
+
+    def part(chunk, side, piece, start, count):
+        tensor, first, rows = plan[chunk]
+        size = rows // 8
+        half = shards[tensor].shape[0]
+        at = side * half + first + piece * size + start
+        return wholes[tensor].at[pl.ds(pl.multiple_of(at, 8), count)]
+
+    steps = {}
+    for chunk, (tensor, first, rows) in enumerate(plan):
+        size = rows // 8
+        src = shards[tensor].at[pl.ds(pl.multiple_of(first + mine * size, 8), size)]
+        steps[chunk, 0] = send(
+            src, part(chunk, w, mine, 0, size), send_sem.at[0, chunk], recv_sem.at[0, chunk], by_x
+        )
+
+    def second(chunk):
+        size = plan[chunk][2] // 8
+        steps[chunk, 0].wait_recv()
+        for kind, peer in ((1, by_y), (2, by_z)):
+            ref = part(chunk, o, mine, 0, size)
+            steps[chunk, kind] = send(
+                ref, ref, send_sem.at[kind, chunk], recv_sem.at[kind, chunk], peer
+            )
+
+    def third(chunk):
+        size = plan[chunk][2] // 8
+        steps[chunk, 1].wait_recv()
+        steps[chunk, 2].wait_recv()
+        ref = part(chunk, o, from_z, 0, size // 2)
+        steps[chunk, 3] = send(ref, ref, send_sem.at[3, chunk], recv_sem.at[3, chunk], by_y)
+        ref = part(chunk, o, from_y, size // 2, size // 2)
+        steps[chunk, 4] = send(ref, ref, send_sem.at[4, chunk], recv_sem.at[4, chunk], by_z)
+
+    def fourth(chunk):
+        size = plan[chunk][2] // 8
+        steps[chunk, 3].wait_recv()
+        steps[chunk, 4].wait_recv()
+        ref = part(chunk, o, core * 4, 0, 4 * size)
+        steps[chunk, 5] = send(ref, ref, send_sem.at[5, chunk], recv_sem.at[5, chunk], by_core)
+
+    count = len(plan)
+    for turn in range(count + 2):
+        if turn < count:
+            second(turn)
+        if 0 <= turn - 1 < count:
+            third(turn - 1)
+        if 0 <= turn - 2 < count:
+            fourth(turn - 2)
+    for chunk in range(count):
+        steps[chunk, 5].wait_recv()
+        for kind in range(6):
+            steps[chunk, kind].wait_send()
+    sent[0].wait()
+    for copy in locals_:
+        copy.wait()
+
+
+def gather_weights(shards, small):
+    plan = []
+    for index, shard in enumerate(shards):
+        rows = shard.shape[0]
+        parts = max(1, shard.shape[0] * shard.shape[1] // (1024 * 1024))
+        for piece in range(parts):
+            plan.append((index, piece * (rows // parts), rows // parts))
+    count = len(shards)
+    shapes = [jax.ShapeDtypeStruct((2 * s.shape[0],) + s.shape[1:], s.dtype) for s in shards]
+    shapes.append(jax.ShapeDtypeStruct((2,) + small.shape, small.dtype))
+    anywhere = pl.BlockSpec(memory_space=pl.ANY)
+    return pl.pallas_call(
+        functools.partial(gather_kernel, plan, count),
+        out_shape=shapes,
+        in_specs=[anywhere] * (count + 1),
+        out_specs=[anywhere] * (count + 1),
+        scratch_shapes=[
+            pltpu.SemaphoreType.DMA((6, len(plan))),
+            pltpu.SemaphoreType.DMA((6, len(plan))),
+            pltpu.SemaphoreType.DMA((2,)),
+            pltpu.SemaphoreType.DMA((count + 1,)),
+        ],
+        compiler_params=pltpu.CompilerParams(collective_id=0, has_side_effects=True),
+        name="gather_weights",
+    )(*shards, small)
+
+
+def plane_peers(c, w, count):
+    return [(lax.rem(c + step, count), w) for step in range(1, count)]
+
+
+def pack_three(first, second, third, row, pair, out):
+    cols = pl.ds(pair * 128, 128)
+    a, b, d = (ref[pl.ds(row, BLK), cols] for ref in (first, second, third))
+    half = BLK // 2
+    for head in range(2):
+        lane = slice(head * HD, head * HD + HD)
+        out[2 * pair + head, 0:BLK, :] = jnp.concatenate([a[:, lane], b[:, lane]], axis=1)
+        out[2 * pair + head, BLK : BLK + half, :] = jnp.concatenate(
+            [d[:half, lane], d[half:, lane]], axis=1
+        )
+
+
+def unpack_fold(block):
+    return jnp.concatenate([block[:, :HD], block[:, HD:]], axis=0)
+
+
+def fold(rows):
+    half = rows.shape[0] // 2
+    return jnp.concatenate([rows[:half], rows[half:]], axis=1)
+
+
+def all_bytes(ref, sem, peers):
+    view = ref.at[pl.ds(0, peers)]
+    return pltpu.make_async_copy(view, view, sem)
+
+
+def attend_kernel(
+    heads,
+    lens_ref,
+    slot_ref,
+    block_ref,
+    q_ref,
+    k_ref,
+    v_ref,
+    a_ref,
+    kept_ref,
+    lse_ref,
+    *scratch,
+):
+    in_buf = scratch[:MB]
+    out_buf, back_out, back_in, q_s, k_s, v_s, a_s = scratch[MB : MB + 7]
+    send_sem, recv_sem, back_send, back_recv, keep_sem = scratch[MB + 7 :]
+    c, w = lax.axis_index("ctx"), lax.axis_index("wsh")
+    peers = plane_peers(c, w, heads)
+    greet(peers)
+    blocks = heads
+    for m in range(MB):
+        for pair in range(heads // 2):
+            pack_three(q_ref, k_ref, v_ref, m * BLK, pair, out_buf.at[m])
+        for peer in peers:
+            send(
+                out_buf.at[m, peer[0]], in_buf[m].at[c], send_sem.at[m], recv_sem.at[m], peer
+            )
+        in_buf[m][c] = out_buf[m, c]
+    for m in range(MB):
+        all_bytes(in_buf[m], recv_sem.at[m], heads - 1).wait()
+        keep = pltpu.make_async_copy(in_buf[m], kept_ref.at[m], keep_sem.at[m])
+        keep.start()
+        for b in range(blocks):
+            got = in_buf[m][slot_ref[m, b]]
+            q_s[b * BLK : (b + 1) * BLK, :] = got[:BLK, :HD]
+            k_s[b * BLK : (b + 1) * BLK, :] = got[:BLK, HD:]
+            v_s[b * BLK : (b + 1) * BLK, :] = unpack_fold(got[BLK:])
+        span = BPS * BLK
+        for s in range(blocks // BPS):
+            rows = slice(s * span, (s + 1) * span)
+            scores = lax.dot_general(
+                k_s[rows, :], q_s[rows, :], (((1,), (1,)), ((), ())), preferred_element_type=F32
+            ) * (1.0 / math.sqrt(HD))
+            place = lax.broadcasted_iota(jnp.int32, scores.shape, 0)
+            scores = jnp.where(place < lens_ref[m, s], scores, NEG_FILL)
+            top = jnp.max(scores, axis=0, keepdims=True)
+            weights = jnp.exp(scores - top)
+            total = jnp.sum(weights, axis=0, keepdims=True)
+            out_t = lax.dot_general(
+                v_s[rows, :],
+                weights.astype(BF16),
+                (((0,), (0,)), ((), ())),
+                preferred_element_type=F32,
+            )
+            a_s[s * BPS : (s + 1) * BPS] = (out_t / total).T.reshape(BPS, BLK, HD)
+            lse_ref[pl.ds(m * (blocks // BPS) + s, 1), :] = top + jnp.log(total)
+        for t in range(blocks):
+            back_out[m, t] = fold(a_s[block_ref[m, t]]).astype(BF16)
+        for peer in peers:
+            send(
+                back_out.at[m, peer[0]], back_in.at[m, c], back_send.at[m], back_recv.at[m], peer
+            )
+        back_in[m, c] = back_out[m, c]
+    for m in range(MB):
+        all_bytes(back_in.at[m], back_recv.at[m], heads - 1).wait()
+        for pair in range(heads // 2):
+            a_ref[m * BLK : (m + 1) * BLK, pair * 128 : (pair + 1) * 128] = jnp.concatenate(
+                [unpack_fold(back_in[m, 2 * pair]), unpack_fold(back_in[m, 2 * pair + 1])], axis=1
+            )
+    for m in range(MB):
+        all_bytes(out_buf.at[m], send_sem.at[m], heads - 1).wait()
+        all_bytes(back_out.at[m], back_send.at[m], heads - 1).wait()
+        pltpu.make_async_copy(in_buf[m], kept_ref.at[m], keep_sem.at[m]).wait()
+
+
+def attend(lens, slot_of, block_of, q, k, v, heads):
+    vmem, smem = pl.BlockSpec(memory_space=pltpu.VMEM), pl.BlockSpec(memory_space=pltpu.SMEM)
+    rows, width = q.shape
+    pack_rows = BLK + BLK // 2
+    span = BPS * BLK
+    return pl.pallas_call(
+        functools.partial(attend_kernel, heads),
+        out_shape=[
+            jax.ShapeDtypeStruct((rows, width), BF16),
+            jax.ShapeDtypeStruct((MB, heads, pack_rows, 128), BF16),
+            jax.ShapeDtypeStruct((8, span), F32),
+        ],
+        in_specs=[smem] * 3 + [vmem] * 3,
+        out_specs=[vmem, pl.BlockSpec(memory_space=pl.ANY), vmem],
+        scratch_shapes=[pltpu.VMEM((heads, pack_rows, 128), BF16)] * MB
+        + [
+            pltpu.VMEM((MB, heads, pack_rows, 128), BF16),
+            pltpu.VMEM((MB, heads, BLK // 2, 128), BF16),
+            pltpu.VMEM((MB, heads, BLK // 2, 128), BF16),
+            pltpu.VMEM((heads * BLK, HD), BF16),
+            pltpu.VMEM((heads * BLK, HD), BF16),
+            pltpu.VMEM((heads * BLK, HD), BF16),
+            pltpu.VMEM((heads, BLK, HD), F32),
+            pltpu.SemaphoreType.DMA((MB,)),
+            pltpu.SemaphoreType.DMA((MB,)),
+            pltpu.SemaphoreType.DMA((MB,)),
+            pltpu.SemaphoreType.DMA((MB,)),
+            pltpu.SemaphoreType.DMA((MB,)),
+        ],
+        compiler_params=pltpu.CompilerParams(
+            collective_id=1, has_side_effects=True, vmem_limit_bytes=VMEM_BYTES
+        ),
+        name="attend",
+    )(lens, slot_of, block_of, q, k, v)
+
+
+def attend_back_kernel(heads, *refs):
+    lens_ref, slot_ref, block_ref, da_ref, kept_ref, lse_ref = refs[:6]
+    x_ref, a_ref, n_ref, g_ref, do_ref, du_ref, dm_ref = refs[6:13]
+    dq_ref, dk_ref, dv_ref = refs[13:16]
+    x_all, a_all, n_all, g_all, do_all, du_all, dm_all, dqkv_all = refs[16:24]
+    in_buf = refs[24 : 24 + MB]
+    out_buf, back_out, back_in = refs[24 + MB : 27 + MB]
+    q_s, k_s, v_s, a_s, dq_s, dk_s, dv_s = refs[27 + MB : 34 + MB]
+    send_sem, recv_sem, back_send, back_recv, mate_send, mate_recv, own_sem = refs[34 + MB :]
+    c, w = lax.axis_index("ctx"), lax.axis_index("wsh")
+    core = bit_of(c, 1)
+    mate = (flip(c, 1), w)
+    peers = plane_peers(c, w, heads)
+    blocks = heads
+    rows_own = da_ref.shape[0]
+    greet(peers)
+
+    place = pl.ds(pl.multiple_of(core * rows_own, rows_own), rows_own)
+    moves = []
+
+    def share(src, dst, lanes):
+        for first, size, to, per_core in lanes:
+            index = len(moves)
+            step = size if per_core else 0
+            own_from = pl.ds(pl.multiple_of(first + core * step, 128), size)
+            mate_from = pl.ds(pl.multiple_of(first + (1 - core) * step, 128), size)
+            spot = dst.at[place, pl.ds(to, size)]
+            own = pltpu.make_async_copy(src.at[:, own_from], spot, own_sem.at[index])
+            own.start()
+            gone = send(
+                src.at[:, mate_from], spot, mate_send.at[index], mate_recv.at[index], mate
+            )
+            moves.append((own, gone))
+
+    width = da_ref.shape[1]
+    hidden = g_ref.shape[1]
+    for m in range(MB):
+        row = slice(m * BLK, (m + 1) * BLK)
+        for pair in range(heads // 2):
+            both = da_ref[row, pair * 128 : (pair + 1) * 128]
+            for head in range(2):
+                out_buf[m, 2 * pair + head] = fold(both[:, head * HD : (head + 1) * HD])
+        for peer in peers:
+            send(out_buf.at[m, peer[0]], in_buf[m].at[c], send_sem.at[m], recv_sem.at[m], peer)
+        in_buf[m][c] = out_buf[m, c]
+    for src, dst in ((x_ref, x_all), (a_ref, a_all), (n_ref, n_all), (dm_ref, dm_all)):
+        share(src, dst, ((0, width, 0, False),))
+    share(do_ref, do_all, ((0, width // 2, 0, True),))
+    share(du_ref, du_all, ((0, hidden // 2, 0, True),))
+    share(g_ref, g_all, ((0, hidden // 4, 0, True), (hidden // 2, hidden // 4, hidden // 4, True)))
+    for m in range(MB):
+        all_bytes(in_buf[m], recv_sem.at[m], heads - 1).wait()
+        for b in range(blocks):
+            slot = slot_ref[m, b]
+            got = kept_ref[m, slot]
+            rows = slice(b * BLK, (b + 1) * BLK)
+            q_s[rows, :] = got[:BLK, :HD]
+            k_s[rows, :] = got[:BLK, HD:]
+            v_s[rows, :] = unpack_fold(got[BLK:])
+            a_s[rows, :] = unpack_fold(in_buf[m][slot])
+        span = BPS * BLK
+        for s in range(blocks // BPS):
+            rows = slice(s * span, (s + 1) * span)
+            qq, kk, vv, dd = q_s[rows, :], k_s[rows, :], v_s[rows, :], a_s[rows, :]
+            scale = 1.0 / math.sqrt(HD)
+            minor = (((1,), (1,)), ((), ()))
+            scores = lax.dot_general(kk, qq, minor, preferred_element_type=F32) * scale
+            spot = lax.broadcasted_iota(jnp.int32, scores.shape, 0)
+            total = lse_ref[pl.ds(m * (blocks // BPS) + s, 1), :]
+            probs = jnp.exp(jnp.where(spot < lens_ref[m, s], scores - total, NEG_FILL))
+            dp = lax.dot_general(vv, dd, minor, preferred_element_type=F32)
+            both = probs * dp
+            delta = jnp.sum(both, axis=0, keepdims=True)
+            ds = (both - probs * delta).astype(BF16)
+            here = slice(s * BPS, (s + 1) * BPS)
+            split = (BPS, BLK, HD)
+            dv = jnp.dot(probs.astype(BF16), dd, preferred_element_type=F32)
+            dv_s[here] = dv.reshape(split)
+            dk_s[here] = (jnp.dot(ds, qq, preferred_element_type=F32) * scale).reshape(split)
+            dq_t = lax.dot_general(kk, ds, (((0,), (0,)), ((), ())), preferred_element_type=F32)
+            dq_s[here] = (dq_t.T * scale).reshape(split)
+        for t in range(blocks):
+            at = block_ref[m, t]
+            back_out[m, t, 0:BLK, :] = jnp.concatenate([dq_s[at], dk_s[at]], axis=1).astype(BF16)
+            back_out[m, t, BLK:, :] = fold(dv_s[at]).astype(BF16)
+        for peer in peers:
+            send(
+                back_out.at[m, peer[0]], back_in.at[m, c], back_send.at[m], back_recv.at[m], peer
+            )
+        back_in[m, c] = back_out[m, c]
+    for m in range(MB):
+        all_bytes(back_in.at[m], back_recv.at[m], heads - 1).wait()
+        row = slice(m * BLK, (m + 1) * BLK)
+        for pair in range(heads // 2):
+            lanes = slice(pair * 128, (pair + 1) * 128)
+            one, two = back_in[m, 2 * pair], back_in[m, 2 * pair + 1]
+            dq_ref[row, lanes] = jnp.concatenate([one[:BLK, :HD], two[:BLK, :HD]], axis=1)
+            dk_ref[row, lanes] = jnp.concatenate([one[:BLK, HD:], two[:BLK, HD:]], axis=1)
+            dv_ref[row, lanes] = jnp.concatenate(
+                [unpack_fold(one[BLK:]), unpack_fold(two[BLK:])], axis=1
+            )
+    for index, ref in enumerate((dq_ref, dk_ref, dv_ref)):
+        half = width // 2
+        spot = dqkv_all.at[place, pl.ds(index * half, half)]
+        number = len(moves)
+        own_from = pl.ds(pl.multiple_of(core * half, 128), half)
+        mate_from = pl.ds(pl.multiple_of((1 - core) * half, 128), half)
+        own = pltpu.make_async_copy(ref.at[:, own_from], spot, own_sem.at[number])
+        own.start()
+        gone = send(ref.at[:, mate_from], spot, mate_send.at[number], mate_recv.at[number], mate)
+        moves.append((own, gone))
+    for m in range(MB):
+        all_bytes(out_buf.at[m], send_sem.at[m], heads - 1).wait()
+        all_bytes(back_out.at[m], back_send.at[m], heads - 1).wait()
+    for own, gone in moves:
+        own.wait()
+        gone.wait()
+
+
+def attend_back(lens, slot_of, block_of, da, kept, lse, x, a, n1, g, do, du, dm, heads):
+    vmem, smem = pl.BlockSpec(memory_space=pltpu.VMEM), pl.BlockSpec(memory_space=pltpu.SMEM)
+    anywhere = pl.BlockSpec(memory_space=pl.ANY)
+    rows, width = da.shape
+    hidden = g.shape[1]
+    pack_rows = BLK + BLK // 2
+    both = 2 * rows
+    moves = 11
+    shape = lambda *dims: jax.ShapeDtypeStruct(dims, BF16)
+    return pl.pallas_call(
+        functools.partial(attend_back_kernel, heads),
+        out_shape=[shape(rows, width)] * 3
+        + [
+            shape(both, width),
+            shape(both, width),
+            shape(both, width),
+            shape(both, hidden // 2),
+            shape(both, width // 2),
+            shape(both, hidden // 2),
+            shape(both, width),
+            shape(both, 3 * width // 2),
+        ],
+        in_specs=[smem] * 3 + [vmem] * 3 + [anywhere] * 7,
+        out_specs=[vmem] * 3 + [anywhere] * 8,
+        scratch_shapes=[pltpu.VMEM((heads, BLK // 2, 128), BF16)] * MB
+        + [
+            pltpu.VMEM((MB, heads, BLK // 2, 128), BF16),
+            pltpu.VMEM((MB, heads, pack_rows, 128), BF16),
+            pltpu.VMEM((MB, heads, pack_rows, 128), BF16),
+        ]
+        + [pltpu.VMEM((heads * BLK, HD), BF16)] * 4
+        + [pltpu.VMEM((heads, BLK, HD), F32)] * 3
+        + [pltpu.SemaphoreType.DMA((MB,))] * 4
+        + [pltpu.SemaphoreType.DMA((moves,))] * 3,
+        compiler_params=pltpu.CompilerParams(
+            collective_id=2, has_side_effects=True, vmem_limit_bytes=VMEM_BYTES
+        ),
+        name="attend_back",
+    )(lens, slot_of, block_of, da, kept, lse, x, a, n1, g, do, du, dm)
+
+
+CHUNKS = 2
+
+
+def reduce_kernel(ga1_ref, ga2_ref, gb_ref, gc_ref, vec_ref, *refs):
+    o_a, o_b, o_c, vec_out = refs[:4]
+    s_a, s_b, s_c = refs[4:7]
+    r_bufs = (refs[7:11], refs[11:15], refs[15:19])
+    v_recv, v_sum = refs[19:21]
+    load_sem, rs_send, rs_recv, ag_send, ag_recv, v_send_sem, v_recv_sem, own_sem = refs[21:]
+    c, x = lax.axis_index("ctx"), lax.axis_index("wsh")
+    core, y, z, zz = bit_of(c, 1), bit_of(c, 2), bit_of(c, 4), bit_of(c, 8)
+    by_x, by_y, by_z = (c, 1 - x), (flip(c, 2), x), (flip(c, 4), x)
+    by_zz, by_core = (flip(c, 8), x), (flip(c, 1), x)
+    shards = 8
+    lanes1 = ga1_ref.shape[3]
+    lanes2 = ga2_ref.shape[3]
+    loads = [
+        pltpu.make_async_copy(ga1_ref, s_a.at[:, :, :, pl.ds(0, lanes1)], load_sem.at[0]),
+        pltpu.make_async_copy(ga2_ref, s_a.at[:, :, :, pl.ds(lanes1, lanes2)], load_sem.at[1]),
+        pltpu.make_async_copy(gb_ref, s_b, load_sem.at[2]),
+        pltpu.make_async_copy(gc_ref, s_c, load_sem.at[3]),
+    ]
+    for load in loads:
+        load.start()
+    greet((by_x, by_y, by_z, by_zz, by_core))
+    vec_steps = [
+        send(vec_ref.at[1 - x], v_recv.at[0], v_send_sem.at[0], v_recv_sem.at[0], by_x)
+    ]
+
+    def vec_next(step, peer):
+        vec_steps[step].wait_recv()
+        before = vec_ref[x] if step == 0 else v_sum[step - 1]
+        v_sum[step] = before + v_recv[step]
+        if peer is not None:
+            vec_steps.append(
+                send(
+                    v_sum.at[step],
+                    v_recv.at[step + 1],
+                    v_send_sem.at[step + 1],
+                    v_recv_sem.at[step + 1],
+                    peer,
+                )
+            )
+
+    for load in loads:
+        load.wait()
+    yz, zy = y * 4 + z * 2, z * 4 + y * 2
+    plans = (
+        (
+            (by_x, 1 - x, x, 0, 0, 8),
+            (by_y, x, x, (1 - y) * 4, y * 4, 4),
+            (by_z, x, x, y * 4 + (1 - z) * 2, yz, 2),
+            (by_zz, x, x, yz + 1 - zz, yz + zz, 1),
+        ),
+        (
+            (by_y, None, None, (1 - y) * 4, y * 4, 4),
+            (by_z, None, None, y * 4 + (1 - z) * 2, yz, 2),
+            (by_x, 1 - x, x, yz, yz, 2),
+            (by_zz, x, x, yz + 1 - zz, yz + zz, 1),
+        ),
+        (
+            (by_z, None, None, (1 - z) * 4, z * 4, 4),
+            (by_x, 1 - x, x, z * 4, z * 4, 4),
+            (by_y, x, x, z * 4 + (1 - y) * 2, zy, 2),
+            (by_zz, x, x, zy + 1 - zz, zy + zz, 1),
+        ),
+    )
+    sums = (s_a, s_b, s_c)
+    outs = (o_a, o_b, o_c)
+    flights = {}
+
+    def chunk_rows(part, chunk):
+        rows = sums[part].shape[2] // CHUNKS
+        return pl.ds(chunk * rows, rows)
+
+    def reduce_send(part, step, chunk):
+        peer, side, _, first, _, count = plans[part][step]
+        rows = chunk_rows(part, chunk)
+        if side is None:
+            src = sums[part].at[:, pl.ds(first, count), rows]
+            dst = r_bufs[part][step].at[:, :, rows]
+        else:
+            src = sums[part].at[side, pl.ds(first, count), rows]
+            dst = r_bufs[part][step].at[0, :, rows]
+        flights[part, step, chunk] = send(
+            src, dst, rs_send.at[part, step, chunk], rs_recv.at[part, step, chunk], peer
+        )
+
+    def reduce_add(part, step, chunk):
+        _, _, side, _, first, count = plans[part][step]
+        rows = chunk_rows(part, chunk)
+        flights[part, step, chunk].wait_recv()
+        total, fresh = sums[part], r_bufs[part][step]
+        sides = ((0, 0), (1, 1)) if side is None else ((side, 0),)
+        for here, there in sides:
+
+            def body(index, carry):
+                spot = first + index
+                total[here, spot, rows] = (
+                    total[here, spot, rows].astype(F32) + fresh[there, index, rows].astype(F32)
+                ).astype(BF16)
+                return carry
+
+            lax.fori_loop(0, count, body, 0)
+
+    for chunk in range(CHUNKS):
+        for part in range(3):
+            reduce_send(part, 0, chunk)
+    vec_peers = (by_y, by_z, by_zz, by_core, None)
+    for step in range(1, 4):
+        vec_next(step - 1, vec_peers[step - 1])
+        for chunk in range(CHUNKS):
+            for part in range(3):
+                reduce_add(part, step - 1, chunk)
+                reduce_send(part, step, chunk)
+    gathers = (
+        ((by_zz, yz + zz, 1), (by_z, yz, 2), (by_y, y * 4, 4)),
+        ((by_zz, yz + zz, 1), (by_z, yz, 2), (by_y, y * 4, 4)),
+        ((by_zz, zy + zz, 1), (by_y, zy, 2), (by_z, z * 4, 4)),
+    )
+    news = (
+        (yz + 1 - zz, y * 4 + (1 - z) * 2, (1 - y) * 4),
+        (yz + 1 - zz, y * 4 + (1 - z) * 2, (1 - y) * 4),
+        (zy + 1 - zz, z * 4 + (1 - y) * 2, (1 - z) * 4),
+    )
+    owns, spread = [], {}
+    vec_next(3, by_core)
+    for chunk in range(CHUNKS):
+        for part in range(3):
+            reduce_add(part, 3, chunk)
+            rows = chunk_rows(part, chunk)
+            peer, first, count = gathers[part][0]
+            src = sums[part].at[x, pl.ds(first, 1), rows]
+            dst = outs[part].at[core, pl.ds(first, 1), rows]
+            own = pltpu.make_async_copy(src, dst, own_sem.at[part, chunk])
+            own.start()
+            owns.append(own)
+            sem = lambda kind: (ag_send.at[part, kind, chunk], ag_recv.at[part, kind, chunk])
+            spread[part, 0, chunk] = send(src, dst, *sem(0), peer)
+            spread[part, 3, chunk] = send(src, dst, *sem(3), by_core)
+    vec_next(4, None)
+    vec_out[...] = v_sum[4]
+    for own in owns:
+        own.wait()
+    for step in range(1, 4):
+        for chunk in range(CHUNKS):
+            for part in range(3):
+                rows = chunk_rows(part, chunk)
+                spread[part, step - 1, chunk].wait_recv()
+                sem = lambda kind: (ag_send.at[part, kind, chunk], ag_recv.at[part, kind, chunk])
+                if step < 3:
+                    peer, first, count = gathers[part][step]
+                    ref = outs[part].at[core, pl.ds(first, count), rows]
+                    spread[part, step, chunk] = send(ref, ref, *sem(step), peer)
+                fresh = outs[part].at[
+                    core, pl.ds(news[part][step - 1], gathers[part][step - 1][2]), rows
+                ]
+                spread[part, 3 + step, chunk] = send(fresh, fresh, *sem(3 + step), by_core)
+    for key, flight in spread.items():
+        if key[1] >= 3:
+            flight.wait_recv()
+        flight.wait_send()
+    for flight in flights.values():
+        flight.wait_send()
+    for flight in vec_steps:
+        flight.wait_send()
+
+
+def reduce_grads(ga1, ga2, gb, gc, vec):
+    vmem, anywhere = pl.BlockSpec(memory_space=pltpu.VMEM), pl.BlockSpec(memory_space=pl.ANY)
+    lanes = ga1.shape[3] + ga2.shape[3]
+    a_shape = ga1.shape[:3] + (lanes,)
+    b_shape, c_shape = gb.shape, gc.shape
+    scratch = [pltpu.VMEM(s, BF16) for s in (a_shape, b_shape, c_shape)]
+    halves = (
+        ((1, 8), (1, 4), (1, 2), (1, 1)),
+        ((2, 4), (2, 2), (1, 2), (1, 1)),
+        ((2, 4), (1, 4), (1, 2), (1, 1)),
+    )
+    for shape, steps in zip((a_shape, b_shape, c_shape), halves):
+        scratch += [pltpu.VMEM(lead + shape[2:], BF16) for lead in steps]
+    scratch += [
+        pltpu.VMEM((5,) + vec.shape[1:], F32),
+        pltpu.VMEM((5,) + vec.shape[1:], F32),
+        pltpu.SemaphoreType.DMA((4,)),
+        pltpu.SemaphoreType.DMA((3, 4, CHUNKS)),
+        pltpu.SemaphoreType.DMA((3, 4, CHUNKS)),
+        pltpu.SemaphoreType.DMA((3, 7, CHUNKS)),
+        pltpu.SemaphoreType.DMA((3, 7, CHUNKS)),
+        pltpu.SemaphoreType.DMA((5,)),
+        pltpu.SemaphoreType.DMA((5,)),
+        pltpu.SemaphoreType.DMA((3, CHUNKS)),
+    ]
+    return pl.pallas_call(
+        reduce_kernel,
+        out_shape=[
+            jax.ShapeDtypeStruct(a_shape, BF16),
+            jax.ShapeDtypeStruct(b_shape, BF16),
+            jax.ShapeDtypeStruct(c_shape, BF16),
+            jax.ShapeDtypeStruct(vec.shape[1:], F32),
+        ],
+        in_specs=[anywhere] * 4 + [vmem],
+        out_specs=[anywhere] * 3 + [vmem],
+        scratch_shapes=scratch,
+        compiler_params=pltpu.CompilerParams(
+            collective_id=3, has_side_effects=True, vmem_limit_bytes=VMEM_BYTES
+        ),
+        name="reduce_grads",
+    )(ga1, ga2, gb, gc, vec)
+
+
+def norm_parts(summed):
+    row_mean = jnp.mean(summed, axis=-1, keepdims=True)
+    centred = summed - row_mean
+    row_var = jnp.mean(centred * centred, axis=-1, keepdims=True)
+    scale = lax.rsqrt(row_var + EPSILON)
+    return centred * scale, scale
+
+
+def norm_back(grad, unit, scale, gain):
+    inner = grad * gain
+    mean_one = jnp.mean(inner, axis=-1, keepdims=True)
+    mean_two = jnp.mean(inner * unit, axis=-1, keepdims=True)
+    return scale * (inner - mean_one - unit * mean_two)
+
+
+def dot(a, b, dims):
+    return lax.dot_general(a, b, (dims, ((), ())), preferred_element_type=F32)
+
+
+ROW_COL, COL_COL, ROW_ROW = ((1,), (0,)), ((1,), (1,)), ((0,), (0,))
+
+
+def per_device_heads(tokens, cotangent, lengths, dealing, *params):
+    rows_in = tokens.shape[2]
+    width = tokens.shape[3]
+    rows = MB * rows_in
+    weights, vectors = params[:6], params[6:]
+    sizes = [item.shape[0] for item in vectors]
+    small = jnp.concatenate(vectors).reshape(-1, 128)
+    *wholes, small_whole = gather_weights(weights, small)
+    query_w, key_w, value_w, out_w, up_w, down_w = wholes
+    flat = small_whole.reshape(2, -1).astype(F32)
+    spots = [sum(sizes[:i]) for i in range(len(sizes) + 1)]
+    bias_query, bias_value, bias_out, bias_up, bias_down, gain_one, shift_one, gain_two, shift_two = (
+        flat[:, spots[i] : spots[i + 1]].reshape(1, -1) for i in range(len(sizes))
+    )
+    x = tokens.reshape(rows, width)
+    lens = lengths[0]
+    block_of = dealing[0]
+    slot_of = jnp.argsort(block_of, axis=1).astype(jnp.int32)
+    q = (dot(x, query_w, ROW_COL) + bias_query).astype(BF16)
+    k = dot(x, key_w, ROW_COL).astype(BF16)
+    v = (dot(x, value_w, ROW_COL) + bias_value).astype(BF16)
+    a, kept, lse = attend(lens, slot_of, block_of, q, k, v, HEADS)
+
+    h_one = x.astype(F32) + (dot(a, out_w, ROW_COL) + bias_out)
+    unit_one, scale_one = norm_parts(h_one)
+    n_one = unit_one * gain_one + shift_one
+    n_low = n_one.astype(BF16)
+    u = dot(n_low, up_w, ROW_COL) + bias_up
+    act, act_back = jax.vjp(gelu_exact, u)
+    g = act.astype(BF16)
+    h_two = n_one + (dot(g, down_w, ROW_COL) + bias_down)
+    unit_two, scale_two = norm_parts(h_two)
+    output = (unit_two * gain_two + shift_two).astype(BF16)
+
+    cot = cotangent.reshape(rows, width).astype(F32)
+    dh_two = norm_back(cot, unit_two, scale_two, gain_two)
+    dm = dh_two.astype(BF16)
+    (du_full,) = act_back(dot(dm, down_w, COL_COL))
+    du = du_full.astype(BF16)
+    dn = dot(du, up_w, COL_COL) + dh_two
+    dh_one = norm_back(dn, unit_one, scale_one, gain_one)
+    do = dh_one.astype(BF16)
+    da = dot(do, out_w, COL_COL).astype(BF16)
+
+    dq, dk, dv, x_all, a_all, n_all, g_all, do_all, du_all, dm_all, dqkv_all = attend_back(
+        lens, slot_of, block_of, da, kept, lse, x, a, n_low, g, do, du, dm, HEADS
+    )
+    total = lambda item: jnp.sum(item.astype(F32), axis=0)
+    vec = [
+        total(dq),
+        total(dv),
+        total(do),
+        total(du),
+        total(dm),
+        total(dn * unit_one),
+        total(dn),
+        total(cot * unit_two),
+        total(cot),
+    ]
+    vec = jnp.concatenate([item.reshape(2, -1) for item in vec], axis=1).reshape(2, -1, 128)
+    ga1 = dot(x_all, dqkv_all, ROW_ROW).astype(BF16).reshape(2, 8, -1, dqkv_all.shape[1])
+    ga2 = dot(a_all, do_all, ROW_ROW).astype(BF16).reshape(2, 8, -1, do_all.shape[1])
+    gb = dot(n_all, du_all, ROW_ROW).astype(BF16).reshape(2, 8, -1, du_all.shape[1])
+    gc = dot(g_all, dm_all, ROW_ROW).astype(BF16).reshape(2, 8, -1, dm_all.shape[1])
+    o_a, o_b, o_c, vec_sum = reduce_grads(ga1, ga2, gb, gc, vec)
+    grad_rows = (
+        dh_one + dot(dq, query_w, COL_COL) + dot(dk, key_w, COL_COL) + dot(dv, value_w, COL_COL)
+    )
+    grad_tokens = grad_rows.astype(BF16)
+    half = width // 2
+    o_a = o_a.reshape(2, -1, o_a.shape[3])
+    square = [
+        jnp.concatenate([o_a[0, :, i * half : (i + 1) * half], o_a[1, :, i * half : (i + 1) * half]], axis=1)
+        for i in range(4)
+    ]
+    o_b = o_b.reshape(2, -1, o_b.shape[3])
+    up = jnp.concatenate([o_b[0], o_b[1]], axis=1)
+    down = o_c.reshape(-1, width)
+    vec_sum = vec_sum.reshape(-1)
+    ends = [vec_sum[spots[i] : spots[i + 1]] for i in range(len(sizes))]
+    shape = (1, MB, rows_in, width)
+    return (
+        (output.reshape(shape), grad_tokens.reshape(shape))
+        + tuple(item.astype(F32) for item in square + [up, down])
+        + tuple(ends)
+    )
+
+
 def solution(mesh):
     placed = (
         P("wsh", None, "ctx", None),
@@ -394,8 +1162,9 @@
         P("wsh"),
         P("wsh"),
     )
+    by_heads = mesh.shape["ctx"] == HEADS and mesh.shape["wsh"] == 2
     return jax.shard_map(
-        per_device,
+        per_device_heads if by_heads else per_device,
         mesh=mesh,
         in_specs=placed,
         out_specs=(

time: 1510 us -> 859 us (0.57)
  waiting for transfers between devices: 782 us -> 0 us
  Pallas kernels: 0 us -> 744 us
  blocking collectives: 225 us -> 0 us
  matrix products: 231 us -> 65.1 us
  local copies, waits for them, and re-layouts: 151 us -> 17 us
  other arithmetic: 90 us -> 23.3 us
  between operations: 17.9 us -> 1.41 us
    pallas_call x0 -> x4, Pallas kernels: none -> 744 us  [the longest x1 384 us: gather_weights(): pl.pallas_call(functools.partial(gather_kernel, plan, count), out_shape=s...]
    all_gather x18 -> x0, waiting for transfers between devices: 442 us -> none  [the longest x3 115 us: per_device(): value_piece = lax.all_gather(value_low, 'ctx', axis=0, tiled=True)]
    reduce_scatter x6 -> x0, waiting for transfers between devices: 195 us -> none  [per_device(): lax.psum_scatter(as_sent(grads), 'wsh', scatter_dimension=0, tiled=True)]
    dot_general x96 -> x16, matrix products: 231 us -> 65.1 us  [dot(): return lax.dot_general(a, b, (dims, ((), ())), preferred_element_type=F32)]
    all_gather x15 -> x0, blocking collectives: 153 us -> none  [the longest x3 58.9 us: per_device(): lax.all_gather(log_total.T, 'ctx', axis=0, tiled=True)]
    psum x1 -> x0, waiting for transfers between devices: 140 us -> none  [per_device(): lax.psum(as_sent(shards), 'ctx')]
    dynamic_slice x66 -> x0, local copies, waits for them, and re-layouts: 76.1 us -> none  [the longest x12 25.1 us: key_visit_block(): lax.dynamic_slice_in_dim(grad_piece, offset, key_step_rows)]
    psum x1 -> x0, blocking collectives: 64.5 us -> none  [per_device(): lax.psum(as_sent(shards), 'ctx')]
  transfers between devices with their start and end apart: 25 -> 0, of which waited for: 14 -> 0; matrix products, arithmetic and copies ran while one was open for 29% -> 0% of each run, Pallas kernels for 0% -> 0%
where the time goes in v1:
time: 859 us; the launch traced here: 851 us
  Pallas kernels  744 us (87%)
  matrix products  65.1 us (8%)
  other arithmetic  23.3 us (3%)
  local copies, waits for them, and re-layouts  17 us (2%)
    pallas_call x1, Pallas kernels, gather_weights(): pl.pallas_call(functools.partial(gather_kernel, plan, count), out_shape=s...  384 us
    pallas_call x1, Pallas kernels, reduce_grads(): pl.pallas_call(reduce_kernel, out_shape=[jax.ShapeDtypeStruct(a_shape, BF...  207 us
    pallas_call x1, Pallas kernels, attend_back(): pl.pallas_call(functools.partial(attend_back_kernel, heads), out_shape=[s...  108 us
    dot_general x16, matrix products, dot(): return lax.dot_general(a, b, (dims, ((), ())), preferred_element_type=F32)  65.1 us
    pallas_call x1, Pallas kernels, attend(): pl.pallas_call(functools.partial(attend_kernel, heads), out_shape=[jax.Sh...  44.8 us

profile of v1, /device:TPU:0, one launch (start us, length us, event | category | flops | bytes accessed | tf_op | source)
XLA Modules:
  0.0 850.9 jit_solution(420638313190739917)
XLA Ops:
  12.4 383.6 %gather_weights.1 = (bf16[1024,1024]{1,0:T(8,128)(2,1)}, bf16[1024,1024]{1,0:T(8,128)(2,1)}, bf16[1024,1024]{1,0:T(8,128)(2,1)}, bf16[1024,1024]{1,0:T(8,128)(2,...) custom-call(bf16[512,1024]{1,0:T(8,128)(2,1)} %refs_0_.1, ...), custom_call_target="tpu_custom_call" | custom-call | tf_op jit(solution)/shard_map/gather_weights/pallas_call | solution.py:505
  397.2 2.9 fusion.13.q_ref
  400.2 3.1 fusion.12.v_ref
  403.2 2.9 fusion.11.k_ref
  406.2 44.8 %attend.1 = (bf16[192,1024]{1,0:T(8,128)(2,1)}, bf16[3,16,96,128]{3,2,1,0:T(8,128)(2,1)}, f32[8,512]{1,0:T(8,128)}) custom-call(s32[3,2]{1,0:T(4,128)} %copy.39.lens_ref.refs_0_, s32[3,16]{1,0:T(4,128)} %copy.40.slot_ref.refs_1_, s32[3,16]{1,0:T(4,128)} %bitcast.160, bf16[192,1024]{1,0:T(8,128)(2,1)} %fusion.13.q_ref, bf16[192,1024]{1,0:T(8,128)(2,1)} %fusion.11.k_ref, ...), custom_call_target="tpu_custom_call" | custom-call | tf_op jit(solution)/shard_map/attend/pallas_call | solution.py:631
  450.9 1.7 fusion.19
  453.2 13.1 %multiply_convert_fusion = (bf16[192,4096]{1,0:T(8,128)(2,1)S(1)}, f32[192,4096]{1,0:T(8,128)}, f32[192,4096]{1,0:T(8,128)}) fusion(f32[4096]{0:T(1024)S(1)} %bitcast.166, bf16[192,1024]{1,0:T(8,128)(2,1)S(1)} %fusion.16.refs_8_, bf16[1024,4096]{1,0:T(8,128)(2,1)} %get-tuple-element.50), kind=kOutput, calls=%fused_computation.10 | convolution fusion | flops 1662517248 | bytes 16662528 | tf_op jit(solution)/shard_map/dot_general | solution.py:1049
  466.3 1.9 fusion.20
  469.5 2.5 convert_reduce_fusion.2
  472.0 10.3 %convert_reduce_fusion = (f32[4096]{0:T(1024)S(1)}, bf16[192,4096]{1,0:T(8,128)(2,1)}) fusion(f32[192,4096]{1,0:T(8,128)} %get-tuple-element.86, f32[192,4096]{1,0:T(8,128)} %get-tuple-element.116, bf16[192,1024]{1,0:T(8,128)(2,1)S(1)} %get-tuple-element.78.refs_12_, bf16[4096,1024]{1,0:T(8,128)(2,1)} %get-tuple-element.51), kind=kOutput, calls=%fused_computation.8 | convolution fusion | flops 1623191552 | bytes 16662528 | tf_op jit(solution)/shard_map/dot_general | solution.py:1049
  482.3 7.9 multiply_reduce_fusion
  490.3 2.3 convert_reduce_fusion.3
  492.6 1.6 convolution_convert_fusion.5.refs_3_
  494.2 108.3 %attend_back.1 = (bf16[192,1024]{1,0:T(8,128)(2,1)}, bf16[192,1024]{1,0:T(8,128)(2,1)}, bf16[192,1024]{1,0:T(8,128)(2,1)}, bf16[384,1024]{1,0:T(8,128)(2,1)}, bf...) custom-call(s32[3,2]{1,0:T(4,128)} %copy.39.lens_ref.refs_0_, ...), custom_call_target="tpu_custom_call" | custom-call | tf_op jit(solution)/shard_map/attend_back/pallas_call | solution.py:790
  602.6 2.0 convolution_add_fusion.5
  605.5 1.6 fusion.8
  608.0 2.7 convolution_convert_fusion.3
  610.8 3.5 convolution_convert_fusion.2
  614.3 4.4 convolution_convert_fusion.1
  618.7 4.7 convolution_convert_fusion
  623.4 207.4 %reduce_grads.1 = (bf16[2,8,64,2048]{3,2,1,0:T(8,128)(2,1)}, bf16[2,8,64,2048]{3,2,1,0:T(8,128)(2,1)}, bf16[2,8,128,1024]{3,2,1,0:T(8,128)(2,1)}, f32[48,128]{1,0:T(8,128)}) custom-call(bf16[2,8,64,1536]{3,2,1,0:T(8,128)(2,1)} %bitcast.144, bf16[2,8,64,512]{3,2,1,0:T(8,128)(2,1)} %bitcast.145, bf16[2,8,64,2048]{3,2,1,0:T(8,128)(2,1)} %bitcast.137, ...), custom_call_target="tpu_custom_call" | custom-call | tf_op jit(solution)/shard_map/reduce_grads/pallas_call | solution.py:1015
  830.8 2.5 slice_bitcast_fusion.1
  841.5 4.5 maximum_convert_fusion
  846.0 4.7 bitcast_convert_fusion
  (133 shorter events, 24.7 us)
Async XLA Ops:
  2.7 393.4 %copy-start.18 = (s32[1,3,16]{2,1,0:T(4,128)}, s32[1,3,16]{2,1,0:T(4,128)S(1)}, u32[]{:S(2)}) copy-start(s32[1,3,16]{2,1,0:T(4,128)S(1)} %copy.60) | copy-start | bytes 580
  12.4 384.5 %copy-start.3 = (bf16[1,3,64,1024]{3,2,1,0:T(8,128)(2,1)S(1)}, bf16[1,3,64,1024]{3,2,1,0:T(8,128)(2,1)}, u32[]{:S(2)}) copy-start(bf16[1,3,64,1024]{3,2,1,0:T(8,128)(2,1)} %param.20) | copy-start | bytes 1179652
  12.4 384.8 %copy-start.6 = (bf16[1,3,64,1024]{3,2,1,0:T(8,128)(2,1)S(1)}, bf16[1,3,64,1024]{3,2,1,0:T(8,128)(2,1)}, u32[]{:S(2)}) copy-start(bf16[1,3,64,1024]{3,2,1,0:T(8,128)(2,1)} %param.19) | copy-start | bytes 1179652
  400.2 50.8 %copy-start = (bf16[1024,1024]{1,0:T(8,128)(2,1)S(1)}, bf16[1024,1024]{1,0:T(8,128)(2,1)}, u32[]{:S(2)}) copy-start(bf16[1024,1024]{1,0:T(8,128)(2,1)} %get-tuple-element.49) | copy-start | bytes 6291460
  400.2 50.8 %copy-start.7 = (bf16[1,3,64,1024]{3,2,1,0:T(8,128)(2,1)S(1)}, bf16[1,3,64,1024]{3,2,1,0:T(8,128)(2,1)}, u32[]{:S(2)}) copy-start(bf16[1,3,64,1024]{3,2,1,0:T(8,128)(2,1)} %param.19) | copy-start | bytes 1179652
  453.1 13.2 %copy-start.15 = (bf16[192,1024]{1,0:T(8,128)(2,1)}, bf16[192,1024]{1,0:T(8,128)(2,1)S(1)}, u32[]{:S(2)}) copy-start(bf16[192,1024]{1,0:T(8,128)(2,1)S(1)} %fusion.16.refs_8_) | copy-start | bytes 1179652
  453.1 13.2 %slice-start = ((s8[8388608]{0:T(1024)(128)(4,1)}), s8[4194304]{0:T(1024)(128)(4,1)S(1)}, s32[]{:S(2)}) async-start(s8[8388608]{0:T(1024)(128)(4,1)} %bitcast.172), calls=%async_computation | async-start | bytes 8388608
  453.2 13.1 %slice-start.1 = ((s8[8388608]{0:T(1024)(128)(4,1)}), s8[4194304]{0:T(1024)(128)(4,1)S(1)}, s32[]{:S(2)}) async-start(s8[8388608]{0:T(1024)(128)(4,1)} %bitcast.172), calls=%async_computation.1 | async-start | bytes 8388608
  472.0 10.3 %copy-start.16 = (bf16[192,1024]{1,0:T(8,128)(2,1)}, bf16[192,1024]{1,0:T(8,128)(2,1)S(1)}, u32[]{:S(2)}) copy-start(bf16[192,1024]{1,0:T(8,128)(2,1)S(1)} %get-tuple-element.78.refs_12_) | copy-start | bytes 1179652
  494.2 108.4 %copy-start.9 = (f32[192,1024]{1,0:T(8,128)S(1)}, f32[192,1024]{1,0:T(8,128)}, u32[]{:S(2)}) copy-start(f32[192,1024]{1,0:T(8,128)} %get-tuple-element.84) | copy-start | bytes 2359300
  494.2 108.4 %copy-start.11 = (bf16[1024,1024]{1,0:T(8,128)(2,1)S(1)}, bf16[1024,1024]{1,0:T(8,128)(2,1)}, u32[]{:S(2)}) copy-start(bf16[1024,1024]{1,0:T(8,128)(2,1)} %get-tuple-element.44) | copy-start | bytes 6291460
  602.6 2.9 copy-start.10
  602.6 2.9 copy-start.12
  604.6 2.6 copy-start.14
  605.5 2.5 copy-start.27
  605.5 5.3 copy-start.23
  605.5 5.3 copy-start.26
  610.8 3.5 copy-start.22
  610.8 3.5 copy-start.25
  614.3 4.4 copy-start.21
  614.3 4.4 copy-start.24
  830.8 2.5 copy-start.19
  837.7 3.3 copy-start.5
  841.5 4.5 copy-start.4
  (6 other events, 9.2 us)

commit v2 on v1

--- a/solution.py
+++ b/solution.py
@@ -413,21 +413,19 @@
 def gather_kernel(plan, n_weights, *refs):
     shards, small = refs[:n_weights], refs[n_weights]
     wholes, small_whole = refs[n_weights + 1 : 2 * n_weights + 1], refs[2 * n_weights + 1]
-    send_sem, recv_sem, small_sems, local_sem = refs[2 * n_weights + 2 :]
+    stages = refs[2 * n_weights + 2 : 3 * n_weights + 2]
+    send_sem, recv_sem, small_sems, local_sem, stage_sem = refs[3 * n_weights + 2 :]
     c, w = lax.axis_index("ctx"), lax.axis_index("wsh")
     o = 1 - w
     by_x, by_y, by_z, by_core = (c, o), (flip(c, 2), w), (flip(c, 4), w), (flip(c, 1), w)
     core, y, z = bit_of(c, 1), bit_of(c, 2), bit_of(c, 4)
     mine = core * 4 + z * 2 + y
     from_y, from_z = core * 4 + z * 2 + (1 - y), core * 4 + (1 - z) * 2 + y
-    locals_ = []
-    for index, (shard, whole) in enumerate(zip(shards, wholes)):
-        rows = shard.shape[0]
-        copy = pltpu.make_async_copy(
-            shard, whole.at[pl.ds(pl.multiple_of(w * rows, rows), rows)], local_sem.at[index]
-        )
+    staged, locals_ = [], []
+    for index, (shard, stage) in enumerate(zip(shards, stages)):
+        copy = pltpu.make_async_copy(shard, stage, stage_sem.at[index])
         copy.start()
-        locals_.append(copy)
+        staged.append(copy)
     copy = pltpu.make_async_copy(small, small_whole.at[w], local_sem.at[n_weights])
     copy.start()
     locals_.append(copy)
@@ -448,6 +446,15 @@
         steps[chunk, 0] = send(
             src, part(chunk, w, mine, 0, size), send_sem.at[0, chunk], recv_sem.at[0, chunk], by_x
         )
+
+    for index, (stage, whole) in enumerate(zip(stages, wholes)):
+        rows = stage.shape[0]
+        staged[index].wait()
+        copy = pltpu.make_async_copy(
+            stage, whole.at[pl.ds(pl.multiple_of(w * rows, rows), rows)], local_sem.at[index]
+        )
+        copy.start()
+        locals_.append(copy)
 
     def second(chunk):
         size = plan[chunk][2] // 8
@@ -507,13 +514,17 @@
         out_shape=shapes,
         in_specs=[anywhere] * (count + 1),
         out_specs=[anywhere] * (count + 1),
-        scratch_shapes=[
+        scratch_shapes=[pltpu.VMEM(s.shape, s.dtype) for s in shards]
+        + [
             pltpu.SemaphoreType.DMA((6, len(plan))),
             pltpu.SemaphoreType.DMA((6, len(plan))),
             pltpu.SemaphoreType.DMA((2,)),
             pltpu.SemaphoreType.DMA((count + 1,)),
+            pltpu.SemaphoreType.DMA((count,)),
         ],
-        compiler_params=pltpu.CompilerParams(collective_id=0, has_side_effects=True),
+        compiler_params=pltpu.CompilerParams(
+            collective_id=0, has_side_effects=True, vmem_limit_bytes=VMEM_BYTES
+        ),
         name="gather_weights",
     )(*shards, small)
 
@@ -800,7 +811,7 @@
             shape(both, width),
             shape(both, 3 * width // 2),
         ],
-        in_specs=[smem] * 3 + [vmem] * 3 + [anywhere] * 7,
+        in_specs=[smem] * 3 + [vmem] * 10,
         out_specs=[vmem] * 3 + [anywhere] * 8,
         scratch_shapes=[pltpu.VMEM((heads, BLK // 2, 128), BF16)] * MB
         + [

time: 859 us -> 478 us (0.56)
  Pallas kernels: 744 us -> 365 us
    pallas_call x1, Pallas kernels: 384 us -> 65.8 us  [gather_weights(): pl.pallas_call(functools.partial(gather_kernel, plan, count), out_shape=s...]
    pallas_call x1, Pallas kernels: 108 us -> 43.7 us  [attend_back(): pl.pallas_call(functools.partial(attend_back_kernel, heads), out_shape=[s...]
where the time goes in v2:
time: 478 us; the launch traced here: 471 us
  Pallas kernels  365 us (76%)
  matrix products  65.1 us (14%)
  other arithmetic  23.3 us (5%)
  local copies, waits for them, and re-layouts  17 us (4%)
    pallas_call x1, Pallas kernels, reduce_grads(): pl.pallas_call(reduce_kernel, out_shape=[jax.ShapeDtypeStruct(a_shape, BF...  213 us
    pallas_call x1, Pallas kernels, gather_weights(): pl.pallas_call(functools.partial(gather_kernel, plan, count), out_shape=s...  65.8 us
    dot_general x16, matrix products, dot(): return lax.dot_general(a, b, (dims, ((), ())), preferred_element_type=F32)  65.1 us
    pallas_call x1, Pallas kernels, attend_back(): pl.pallas_call(functools.partial(attend_back_kernel, heads), out_shape=[s...  43.7 us
    pallas_call x1, Pallas kernels, attend(): pl.pallas_call(functools.partial(attend_kernel, heads), out_shape=[jax.Sh...  42.3 us
    convert_element_type x6, other arithmetic, per_device_heads(): item.astype(F32)  15.5 us
    unnamed x90, local copies, waits for them, and re-layouts  9.75 us

profile of v2, /device:TPU:0, one launch (start us, length us, event | category | flops | bytes accessed | tf_op | source)
XLA Modules:
  0.0 471.4 jit_solution(7465012874082639794)
XLA Ops:
  12.4 65.8 %gather_weights.1 = (bf16[1024,1024]{1,0:T(8,128)(2,1)}, bf16[1024,1024]{1,0:T(8,128)(2,1)}, bf16[1024,1024]{1,0:T(8,128)(2,1)}, bf16[1024,1024]{1,0:T(8,128)(2,...) custom-call(bf16[512,1024]{1,0:T(8,128)(2,1)} %refs_0_.1, ...), custom_call_target="tpu_custom_call" | custom-call | tf_op jit(solution)/shard_map/gather_weights/pallas_call | solution.py:512
  79.5 2.9 fusion.13.q_ref
  82.4 3.1 fusion.12.v_ref
  85.5 2.9 fusion.11.k_ref
  88.4 42.3 %attend.1 = (bf16[192,1024]{1,0:T(8,128)(2,1)}, bf16[3,16,96,128]{3,2,1,0:T(8,128)(2,1)}, f32[8,512]{1,0:T(8,128)}) custom-call(s32[3,2]{1,0:T(4,128)} %copy.39.lens_ref.refs_0_, s32[3,16]{1,0:T(4,128)} %copy.40.slot_ref.refs_1_, s32[3,16]{1,0:T(4,128)} %bitcast.160, bf16[192,1024]{1,0:T(8,128)(2,1)} %fusion.13.q_ref, bf16[192,1024]{1,0:T(8,128)(2,1)} %fusion.11.k_ref, ...), custom_call_target="tpu_custom_call" | custom-call | tf_op jit(solution)/shard_map/attend/pallas_call | solution.py:642
  130.8 1.7 fusion.19
  133.0 13.0 %multiply_convert_fusion = (bf16[192,4096]{1,0:T(8,128)(2,1)S(1)}, f32[192,4096]{1,0:T(8,128)}, f32[192,4096]{1,0:T(8,128)}) fusion(f32[4096]{0:T(1024)S(1)} %bitcast.166, bf16[192,1024]{1,0:T(8,128)(2,1)S(1)} %fusion.16.refs_8_, bf16[1024,4096]{1,0:T(8,128)(2,1)} %get-tuple-element.50), kind=kOutput, calls=%fused_computation.10 | convolution fusion | flops 1662517248 | bytes 16662528 | tf_op jit(solution)/shard_map/dot_general | solution.py:1060
  146.1 1.9 fusion.20
  149.3 2.5 convert_reduce_fusion.2
  151.9 10.3 %convert_reduce_fusion = (f32[4096]{0:T(1024)S(1)}, bf16[192,4096]{1,0:T(8,128)(2,1)}) fusion(f32[192,4096]{1,0:T(8,128)} %get-tuple-element.86, f32[192,4096]{1,0:T(8,128)} %get-tuple-element.116, bf16[192,1024]{1,0:T(8,128)(2,1)S(1)} %get-tuple-element.78.refs_12_, bf16[4096,1024]{1,0:T(8,128)(2,1)} %get-tuple-element.51), kind=kOutput, calls=%fused_computation.8 | convolution fusion | flops 1623191552 | bytes 16662528 | tf_op jit(solution)/shard_map/dot_general | solution.py:1060
  162.1 7.9 %multiply_reduce_fusion = (f32[1024]{0:T(1024)S(1)}, f32[192]{0:T(256)S(1)}, f32[192]{0:T(256)S(1)}, f32[1024]{0:T(1024)S(1)}, f32[192,1024]{1,0:T(8,128)}) fusion(f32[192,1024]{1,0:T(8,128)S(1)} %get-tuple-element.115, f32[192]{0:T(256)S(1)} %add_rsqrt_fusion.1, f32[192]{0:T(256)S(1)} %broadcast_multiply_fusion.5, f32[1024]{0:T(1024)S(1)} %bitcast.157, ...), kind=kOutput, calls=%fused_computation.53 | convolution fusion | flops 1612576256 | bytes 12336128 | tf_op jit(solution)/shard_map/dot_general | solution.py:1060
  170.1 2.3 convert_reduce_fusion.3
  172.4 1.6 convolution_convert_fusion.5.refs_3_
  174.0 43.7 %attend_back.1 = (bf16[192,1024]{1,0:T(8,128)(2,1)}, bf16[192,1024]{1,0:T(8,128)(2,1)}, bf16[192,1024]{1,0:T(8,128)(2,1)}, bf16[384,1024]{1,0:T(8,128)(2,1)}, bf...) custom-call(s32[3,2]{1,0:T(4,128)} %copy.39.lens_ref.refs_0_, ...), custom_call_target="tpu_custom_call" | custom-call | tf_op jit(solution)/shard_map/attend_back/pallas_call | solution.py:801
  217.8 2.0 convolution_add_fusion.5
  220.7 1.6 fusion.8
  223.2 2.7 convolution_convert_fusion.3
  225.9 3.5 convolution_convert_fusion.2
  229.5 4.4 convolution_convert_fusion.1
  233.9 4.6 convolution_convert_fusion
  238.5 212.7 %reduce_grads.1 = (bf16[2,8,64,2048]{3,2,1,0:T(8,128)(2,1)}, bf16[2,8,64,2048]{3,2,1,0:T(8,128)(2,1)}, bf16[2,8,128,1024]{3,2,1,0:T(8,128)(2,1)}, f32[48,128]{1,0:T(8,128)}) custom-call(bf16[2,8,64,1536]{3,2,1,0:T(8,128)(2,1)} %bitcast.144, bf16[2,8,64,512]{3,2,1,0:T(8,128)(2,1)} %bitcast.145, bf16[2,8,64,2048]{3,2,1,0:T(8,128)(2,1)} %bitcast.137, ...), custom_call_target="tpu_custom_call" | custom-call | tf_op jit(solution)/shard_map/reduce_grads/pallas_call | solution.py:1026
  451.2 2.5 slice_bitcast_fusion.1
  461.9 4.5 maximum_convert_fusion
  466.4 4.7 %bitcast_convert_fusion = f32[2048,1024]{1,0:T(8,128)} fusion(bf16[2,8,128,1024]{3,2,1,0:T(8,128)(2,1)S(1)} %copy-done.4), kind=kLoop, calls=%fused_computation.3 | loop fusion | flops 2097152 | bytes 12582912 | tf_op jit(solution)/shard_map/convert_element_type | solution.py:1149
  (133 shorter events, 24.7 us)
Async XLA Ops:
  2.7 75.6 %copy-start.18 = (s32[1,3,16]{2,1,0:T(4,128)}, s32[1,3,16]{2,1,0:T(4,128)S(1)}, u32[]{:S(2)}) copy-start(s32[1,3,16]{2,1,0:T(4,128)S(1)} %copy.60) | copy-start | bytes 580
  12.4 66.8 %copy-start.3 = (bf16[1,3,64,1024]{3,2,1,0:T(8,128)(2,1)S(1)}, bf16[1,3,64,1024]{3,2,1,0:T(8,128)(2,1)}, u32[]{:S(2)}) copy-start(bf16[1,3,64,1024]{3,2,1,0:T(8,128)(2,1)} %param.20) | copy-start | bytes 1179652
  12.4 67.1 %copy-start.6 = (bf16[1,3,64,1024]{3,2,1,0:T(8,128)(2,1)S(1)}, bf16[1,3,64,1024]{3,2,1,0:T(8,128)(2,1)}, u32[]{:S(2)}) copy-start(bf16[1,3,64,1024]{3,2,1,0:T(8,128)(2,1)} %param.19) | copy-start | bytes 1179652
  82.4 48.3 %copy-start = (bf16[1024,1024]{1,0:T(8,128)(2,1)S(1)}, bf16[1024,1024]{1,0:T(8,128)(2,1)}, u32[]{:S(2)}) copy-start(bf16[1024,1024]{1,0:T(8,128)(2,1)} %get-tuple-element.49) | copy-start | bytes 6291460
  82.4 48.3 %copy-start.7 = (bf16[1,3,64,1024]{3,2,1,0:T(8,128)(2,1)S(1)}, bf16[1,3,64,1024]{3,2,1,0:T(8,128)(2,1)}, u32[]{:S(2)}) copy-start(bf16[1,3,64,1024]{3,2,1,0:T(8,128)(2,1)} %param.19) | copy-start | bytes 1179652
  132.9 13.2 %copy-start.15 = (bf16[192,1024]{1,0:T(8,128)(2,1)}, bf16[192,1024]{1,0:T(8,128)(2,1)S(1)}, u32[]{:S(2)}) copy-start(bf16[192,1024]{1,0:T(8,128)(2,1)S(1)} %fusion.16.refs_8_) | copy-start | bytes 1179652
  132.9 13.2 %slice-start = ((s8[8388608]{0:T(1024)(128)(4,1)}), s8[4194304]{0:T(1024)(128)(4,1)S(1)}, s32[]{:S(2)}) async-start(s8[8388608]{0:T(1024)(128)(4,1)} %bitcast.172), calls=%async_computation | async-start | bytes 8388608
  133.0 13.1 %slice-start.1 = ((s8[8388608]{0:T(1024)(128)(4,1)}), s8[4194304]{0:T(1024)(128)(4,1)S(1)}, s32[]{:S(2)}) async-start(s8[8388608]{0:T(1024)(128)(4,1)} %bitcast.172), calls=%async_computation.1 | async-start | bytes 8388608
  151.9 10.3 %copy-start.16 = (bf16[192,1024]{1,0:T(8,128)(2,1)}, bf16[192,1024]{1,0:T(8,128)(2,1)S(1)}, u32[]{:S(2)}) copy-start(bf16[192,1024]{1,0:T(8,128)(2,1)S(1)} %get-tuple-element.78.refs_12_) | copy-start | bytes 1179652
  174.0 43.7 %copy-start.9 = (f32[192,1024]{1,0:T(8,128)S(1)}, f32[192,1024]{1,0:T(8,128)}, u32[]{:S(2)}) copy-start(f32[192,1024]{1,0:T(8,128)} %get-tuple-element.84) | copy-start | bytes 2359300
  174.0 43.7 %copy-start.11 = (bf16[1024,1024]{1,0:T(8,128)(2,1)S(1)}, bf16[1024,1024]{1,0:T(8,128)(2,1)}, u32[]{:S(2)}) copy-start(bf16[1024,1024]{1,0:T(8,128)(2,1)} %get-tuple-element.44) | copy-start | bytes 6291460
  217.7 2.9 copy-start.10
  217.8 2.9 copy-start.12
  219.8 2.6 copy-start.14
  220.7 2.5 copy-start.27
  220.7 5.3 %copy-start.23 = (bf16[384,1536]{1,0:T(8,128)(2,1)S(1)}, bf16[384,1536]{1,0:T(8,128)(2,1)}, u32[]{:S(2)}) copy-start(bf16[384,1536]{1,0:T(8,128)(2,1)} %get-tuple-element.58) | copy-start | bytes 3538948
  220.7 5.3 %copy-start.26 = (bf16[384,1024]{1,0:T(8,128)(2,1)S(1)}, bf16[384,1024]{1,0:T(8,128)(2,1)}, u32[]{:S(2)}) copy-start(bf16[384,1024]{1,0:T(8,128)(2,1)} %get-tuple-element.57) | copy-start | bytes 2359300
  225.9 3.5 copy-start.22
  225.9 3.5 copy-start.25
  229.5 4.4 copy-start.21
  229.5 4.4 copy-start.24
  451.2 2.5 copy-start.19
  458.1 3.3 copy-start.5
  461.9 4.5 copy-start.4
  (6 other events, 9.2 us)

commit v3 on v2

--- a/solution.py
+++ b/solution.py
@@ -410,11 +410,13 @@
     return copy
 
 
-def gather_kernel(plan, n_weights, *refs):
-    shards, small = refs[:n_weights], refs[n_weights]
-    wholes, small_whole = refs[n_weights + 1 : 2 * n_weights + 1], refs[2 * n_weights + 1]
-    stages = refs[2 * n_weights + 2 : 3 * n_weights + 2]
-    send_sem, recv_sem, small_sems, local_sem, stage_sem = refs[3 * n_weights + 2 :]
+def gather_kernel(plan, n_weights, n_vectors, *refs):
+    shards, vectors = refs[:n_weights], refs[n_weights : n_weights + n_vectors]
+    refs = refs[n_weights + n_vectors :]
+    wholes, small_whole = refs[:n_weights], refs[n_weights]
+    stages = refs[n_weights + 1 : 2 * n_weights + 1]
+    small, small_in = refs[2 * n_weights + 1 : 2 * n_weights + 3]
+    send_sem, recv_sem, small_sems, local_sem, stage_sem = refs[2 * n_weights + 3 :]
     c, w = lax.axis_index("ctx"), lax.axis_index("wsh")
     o = 1 - w
     by_x, by_y, by_z, by_core = (c, o), (flip(c, 2), w), (flip(c, 4), w), (flip(c, 1), w)
@@ -426,11 +428,14 @@
         copy = pltpu.make_async_copy(shard, stage, stage_sem.at[index])
         copy.start()
         staged.append(copy)
-    copy = pltpu.make_async_copy(small, small_whole.at[w], local_sem.at[n_weights])
-    copy.start()
-    locals_.append(copy)
+    line, lanes = 0, small.shape[1]
+    for vector in vectors:
+        for first in range(0, vector.shape[0], lanes):
+            piece = vector[pl.ds(first, lanes)].astype(F32)
+            small[line : line + 1, :] = piece.reshape(1, lanes)
+            line += 1
     greet((by_x, by_y, by_z, by_core))
-    sent = [send(small, small_whole.at[w], small_sems.at[0], small_sems.at[1], by_x)]
+    small_sent = send(small, small_in, small_sems.at[0], small_sems.at[1], by_x)
 
     def part(chunk, side, piece, start, count):
         tensor, first, rows = plan[chunk]
@@ -493,12 +498,14 @@
         steps[chunk, 5].wait_recv()
         for kind in range(6):
             steps[chunk, kind].wait_send()
-    sent[0].wait()
+    small_sent.wait()
+    small_whole[w] = small[...]
+    small_whole[o] = small_in[...]
     for copy in locals_:
         copy.wait()
 
 
-def gather_weights(shards, small):
+def gather_weights(shards, vectors):
     plan = []
     for index, shard in enumerate(shards):
         rows = shard.shape[0]
@@ -507,26 +514,29 @@
             plan.append((index, piece * (rows // parts), rows // parts))
     count = len(shards)
     shapes = [jax.ShapeDtypeStruct((2 * s.shape[0],) + s.shape[1:], s.dtype) for s in shards]
-    shapes.append(jax.ShapeDtypeStruct((2,) + small.shape, small.dtype))
-    anywhere = pl.BlockSpec(memory_space=pl.ANY)
+    lanes = min(item.shape[0] for item in vectors)
+    lines = sum(item.shape[0] for item in vectors) // lanes
+    shapes.append(jax.ShapeDtypeStruct((2, lines, lanes), F32))
+    anywhere, vmem = pl.BlockSpec(memory_space=pl.ANY), pl.BlockSpec(memory_space=pltpu.VMEM)
     return pl.pallas_call(
-        functools.partial(gather_kernel, plan, count),
+        functools.partial(gather_kernel, plan, count, len(vectors)),
         out_shape=shapes,
-        in_specs=[anywhere] * (count + 1),
-        out_specs=[anywhere] * (count + 1),
+        in_specs=[anywhere] * count + [vmem] * len(vectors),
+        out_specs=[anywhere] * count + [vmem],
         scratch_shapes=[pltpu.VMEM(s.shape, s.dtype) for s in shards]
+        + [pltpu.VMEM((lines, lanes), F32)] * 2
         + [
             pltpu.SemaphoreType.DMA((6, len(plan))),
             pltpu.SemaphoreType.DMA((6, len(plan))),
             pltpu.SemaphoreType.DMA((2,)),
-            pltpu.SemaphoreType.DMA((count + 1,)),
+            pltpu.SemaphoreType.DMA((count,)),
             pltpu.SemaphoreType.DMA((count,)),
         ],
         compiler_params=pltpu.CompilerParams(
             collective_id=0, has_side_effects=True, vmem_limit_bytes=VMEM_BYTES
         ),
         name="gather_weights",
-    )(*shards, small)
+    )(*shards, *vectors)
 
 
 def plane_peers(c, w, count):
@@ -592,7 +602,7 @@
         keep = pltpu.make_async_copy(in_buf[m], kept_ref.at[m], keep_sem.at[m])
         keep.start()
         for b in range(blocks):
-            got = in_buf[m][slot_ref[m, b]]
+            got = in_buf[m][slot_ref[0, m, b]]
             q_s[b * BLK : (b + 1) * BLK, :] = got[:BLK, :HD]
             k_s[b * BLK : (b + 1) * BLK, :] = got[:BLK, HD:]
             v_s[b * BLK : (b + 1) * BLK, :] = unpack_fold(got[BLK:])
@@ -603,7 +613,7 @@
                 k_s[rows, :], q_s[rows, :], (((1,), (1,)), ((), ())), preferred_element_type=F32
             ) * (1.0 / math.sqrt(HD))
             place = lax.broadcasted_iota(jnp.int32, scores.shape, 0)
-            scores = jnp.where(place < lens_ref[m, s], scores, NEG_FILL)
+            scores = jnp.where(place < lens_ref[0, m, s], scores, NEG_FILL)
             top = jnp.max(scores, axis=0, keepdims=True)
             weights = jnp.exp(scores - top)
             total = jnp.sum(weights, axis=0, keepdims=True)
@@ -616,7 +626,7 @@
             a_s[s * BPS : (s + 1) * BPS] = (out_t / total).T.reshape(BPS, BLK, HD)
             lse_ref[pl.ds(m * (blocks // BPS) + s, 1), :] = top + jnp.log(total)
         for t in range(blocks):
-            back_out[m, t] = fold(a_s[block_ref[m, t]]).astype(BF16)
+            back_out[m, t] = fold(a_s[block_ref[0, m, t]]).astype(BF16)
         for peer in peers:
             send(
                 back_out.at[m, peer[0]], back_in.at[m, c], back_send.at[m], back_recv.at[m], peer
@@ -723,7 +733,7 @@
     for m in range(MB):
         all_bytes(in_buf[m], recv_sem.at[m], heads - 1).wait()
         for b in range(blocks):
-            slot = slot_ref[m, b]
+            slot = slot_ref[0, m, b]
             got = kept_ref[m, slot]
             rows = slice(b * BLK, (b + 1) * BLK)
             q_s[rows, :] = got[:BLK, :HD]
@@ -739,7 +749,7 @@
             scores = lax.dot_general(kk, qq, minor, preferred_element_type=F32) * scale
             spot = lax.broadcasted_iota(jnp.int32, scores.shape, 0)
             total = lse_ref[pl.ds(m * (blocks // BPS) + s, 1), :]
-            probs = jnp.exp(jnp.where(spot < lens_ref[m, s], scores - total, NEG_FILL))
+            probs = jnp.exp(jnp.where(spot < lens_ref[0, m, s], scores - total, NEG_FILL))
             dp = lax.dot_general(vv, dd, minor, preferred_element_type=F32)
             both = probs * dp
             delta = jnp.sum(both, axis=0, keepdims=True)
@@ -752,7 +762,7 @@
             dq_t = lax.dot_general(kk, ds, (((0,), (0,)), ((), ())), preferred_element_type=F32)
             dq_s[here] = (dq_t.T * scale).reshape(split)
         for t in range(blocks):
-            at = block_ref[m, t]
+            at = block_ref[0, m, t]
             back_out[m, t, 0:BLK, :] = jnp.concatenate([dq_s[at], dk_s[at]], axis=1).astype(BF16)
             back_out[m, t, BLK:, :] = fold(dv_s[at]).astype(BF16)
         for peer in peers:
@@ -831,14 +841,34 @@
 
 
 CHUNKS = 2
+ORDERS = {
+    (0, 0): "xyzZ",
+    (0, 1): "xzyZ",
+    (1, 0): "yxZz",
+    (1, 1): "yZxz",
+    (2, 0): "zxyZ",
+    (2, 1): "Zyxz",
+}
+
+
+def landing_shapes(order, shape):
+    shards, sides, shapes = 8, 2, []
+    for name in order:
+        if name == "x":
+            sides = 1
+        else:
+            shards //= 2
+        shapes.append((sides, shards, shape[2] // CHUNKS, shape[3]))
+    return shapes
 
 
 def reduce_kernel(ga1_ref, ga2_ref, gb_ref, gc_ref, vec_ref, *refs):
     o_a, o_b, o_c, vec_out = refs[:4]
     s_a, s_b, s_c = refs[4:7]
-    r_bufs = (refs[7:11], refs[11:15], refs[15:19])
-    v_recv, v_sum = refs[19:21]
-    load_sem, rs_send, rs_recv, ag_send, ag_recv, v_send_sem, v_recv_sem, own_sem = refs[21:]
+    r_bufs = {key: refs[7 + 4 * i : 11 + 4 * i] for i, key in enumerate(ORDERS)}
+    rest = refs[7 + 4 * len(ORDERS) :]
+    v_recv, v_sum = rest[:2]
+    load_sem, rs_send, rs_recv, ag_send, ag_recv, v_send_sem, v_recv_sem, own_sem = rest[2:]
     c, x = lax.axis_index("ctx"), lax.axis_index("wsh")
     core, y, z, zz = bit_of(c, 1), bit_of(c, 2), bit_of(c, 4), bit_of(c, 8)
     by_x, by_y, by_z = (c, 1 - x), (flip(c, 2), x), (flip(c, 4), x)
@@ -876,27 +906,24 @@
 
     for load in loads:
         load.wait()
-    yz, zy = y * 4 + z * 2, z * 4 + y * 2
-    plans = (
-        (
-            (by_x, 1 - x, x, 0, 0, 8),
-            (by_y, x, x, (1 - y) * 4, y * 4, 4),
-            (by_z, x, x, y * 4 + (1 - z) * 2, yz, 2),
-            (by_zz, x, x, yz + 1 - zz, yz + zz, 1),
-        ),
-        (
-            (by_y, None, None, (1 - y) * 4, y * 4, 4),
-            (by_z, None, None, y * 4 + (1 - z) * 2, yz, 2),
-            (by_x, 1 - x, x, yz, yz, 2),
-            (by_zz, x, x, yz + 1 - zz, yz + zz, 1),
-        ),
-        (
-            (by_z, None, None, (1 - z) * 4, z * 4, 4),
-            (by_x, 1 - x, x, z * 4, z * 4, 4),
-            (by_y, x, x, z * 4 + (1 - y) * 2, zy, 2),
-            (by_zz, x, x, zy + 1 - zz, zy + zz, 1),
-        ),
-    )
+    bits = {"y": y, "z": z, "Z": zz}
+    peers = {"x": by_x, "y": by_y, "z": by_z, "Z": by_zz}
+    plans, gathers = {}, {}
+    for key, order in ORDERS.items():
+        first, count, sided = 0, 8, False
+        plans[key], back = [], []
+        for name in order:
+            if name == "x":
+                plans[key].append((by_x, 1 - x, x, first, first, count))
+                sided = True
+                continue
+            count //= 2
+            out, keep = first + (1 - bits[name]) * count, first + bits[name] * count
+            side = x if sided else None
+            plans[key].append((peers[name], side, side, out, keep, count))
+            back.append((peers[name], keep, out, count))
+            first = keep
+        gathers[key] = back[::-1]
     sums = (s_a, s_b, s_c)
     outs = (o_a, o_b, o_c)
     flights = {}
@@ -906,30 +933,29 @@
         return pl.ds(chunk * rows, rows)
 
     def reduce_send(part, step, chunk):
-        peer, side, _, first, _, count = plans[part][step]
+        peer, side, _, first, _, count = plans[part, chunk][step]
         rows = chunk_rows(part, chunk)
+        dst = r_bufs[part, chunk][step]
         if side is None:
             src = sums[part].at[:, pl.ds(first, count), rows]
-            dst = r_bufs[part][step].at[:, :, rows]
         else:
-            src = sums[part].at[side, pl.ds(first, count), rows]
-            dst = r_bufs[part][step].at[0, :, rows]
+            src, dst = sums[part].at[side, pl.ds(first, count), rows], dst.at[0]
         flights[part, step, chunk] = send(
             src, dst, rs_send.at[part, step, chunk], rs_recv.at[part, step, chunk], peer
         )
 
     def reduce_add(part, step, chunk):
-        _, _, side, _, first, count = plans[part][step]
+        _, _, side, _, first, count = plans[part, chunk][step]
         rows = chunk_rows(part, chunk)
         flights[part, step, chunk].wait_recv()
-        total, fresh = sums[part], r_bufs[part][step]
+        total, fresh = sums[part], r_bufs[part, chunk][step]
         sides = ((0, 0), (1, 1)) if side is None else ((side, 0),)
         for here, there in sides:
 
             def body(index, carry):
                 spot = first + index
                 total[here, spot, rows] = (
-                    total[here, spot, rows].astype(F32) + fresh[there, index, rows].astype(F32)
+                    total[here, spot, rows].astype(F32) + fresh[there, index].astype(F32)
                 ).astype(BF16)
                 return carry
 
@@ -945,23 +971,13 @@
             for part in range(3):
                 reduce_add(part, step - 1, chunk)
                 reduce_send(part, step, chunk)
-    gathers = (
-        ((by_zz, yz + zz, 1), (by_z, yz, 2), (by_y, y * 4, 4)),
-        ((by_zz, yz + zz, 1), (by_z, yz, 2), (by_y, y * 4, 4)),
-        ((by_zz, zy + zz, 1), (by_y, zy, 2), (by_z, z * 4, 4)),
-    )
-    news = (
-        (yz + 1 - zz, y * 4 + (1 - z) * 2, (1 - y) * 4),
-        (yz + 1 - zz, y * 4 + (1 - z) * 2, (1 - y) * 4),
-        (zy + 1 - zz, z * 4 + (1 - y) * 2, (1 - z) * 4),
-    )
     owns, spread = [], {}
     vec_next(3, by_core)
     for chunk in range(CHUNKS):
         for part in range(3):
             reduce_add(part, 3, chunk)
             rows = chunk_rows(part, chunk)
-            peer, first, count = gathers[part][0]
+            peer, first, _, _ = gathers[part, chunk][0]
             src = sums[part].at[x, pl.ds(first, 1), rows]
             dst = outs[part].at[core, pl.ds(first, 1), rows]
             own = pltpu.make_async_copy(src, dst, own_sem.at[part, chunk])
@@ -981,12 +997,11 @@
                 spread[part, step - 1, chunk].wait_recv()
                 sem = lambda kind: (ag_send.at[part, kind, chunk], ag_recv.at[part, kind, chunk])
                 if step < 3:
-                    peer, first, count = gathers[part][step]
+                    peer, first, _, count = gathers[part, chunk][step]
                     ref = outs[part].at[core, pl.ds(first, count), rows]
                     spread[part, step, chunk] = send(ref, ref, *sem(step), peer)
-                fresh = outs[part].at[
-                    core, pl.ds(news[part][step - 1], gathers[part][step - 1][2]), rows
-                ]
+                _, _, first, count = gathers[part, chunk][step - 1]
+                fresh = outs[part].at[core, pl.ds(first, count), rows]
                 spread[part, 3 + step, chunk] = send(fresh, fresh, *sem(3 + step), by_core)
     for key, flight in spread.items():
         if key[1] >= 3:
@@ -1004,13 +1019,9 @@
     a_shape = ga1.shape[:3] + (lanes,)
     b_shape, c_shape = gb.shape, gc.shape
     scratch = [pltpu.VMEM(s, BF16) for s in (a_shape, b_shape, c_shape)]
-    halves = (
-        ((1, 8), (1, 4), (1, 2), (1, 1)),
-        ((2, 4), (2, 2), (1, 2), (1, 1)),
-        ((2, 4), (1, 4), (1, 2), (1, 1)),
-    )
-    for shape, steps in zip((a_shape, b_shape, c_shape), halves):
-        scratch += [pltpu.VMEM(lead + shape[2:], BF16) for lead in steps]
+    shapes = (a_shape, b_shape, c_shape)
+    for (part, _), order in ORDERS.items():
+        scratch += [pltpu.VMEM(shape, BF16) for shape in landing_shapes(order, shapes[part])]
     scratch += [
         pltpu.VMEM((5,) + vec.shape[1:], F32),
         pltpu.VMEM((5,) + vec.shape[1:], F32),
@@ -1041,6 +1052,39 @@
     )(ga1, ga2, gb, gc, vec)
 
 
+def widen_kernel(a_ref, b_ref, c_ref, *outs):
+    half = outs[0].shape[1] // 2
+    for index, out in enumerate(outs[:4]):
+        for core in range(2):
+            out[:, core * half : (core + 1) * half] = a_ref[
+                core, 0, :, index * half : (index + 1) * half
+            ].astype(F32)
+    up, down = outs[4:]
+    half = up.shape[1] // 2
+    for core in range(2):
+        up[:, core * half : (core + 1) * half] = b_ref[core, 0].astype(F32)
+        down[core, 0] = c_ref[core, 0].astype(F32)
+
+
+def widen(o_a, o_b, o_c):
+    shards = o_a.shape[1]
+    block = lambda item: pl.BlockSpec((2, 1) + item.shape[2:], lambda i: (0, i, 0, 0))
+    rows = o_a.shape[2]
+    square = (shards * rows, o_a.shape[3] // 2)
+    wide = (shards * rows, 2 * o_b.shape[3])
+    return pl.pallas_call(
+        widen_kernel,
+        grid=(shards,),
+        out_shape=[jax.ShapeDtypeStruct(square, F32)] * 4
+        + [jax.ShapeDtypeStruct(wide, F32), jax.ShapeDtypeStruct(o_c.shape, F32)],
+        in_specs=[block(o_a), block(o_b), block(o_c)],
+        out_specs=[pl.BlockSpec((rows, square[1]), lambda i: (i, 0))] * 4
+        + [pl.BlockSpec((rows, wide[1]), lambda i: (i, 0)), block(o_c)],
+        compiler_params=pltpu.CompilerParams(vmem_limit_bytes=VMEM_BYTES),
+        name="widen",
+    )(o_a, o_b, o_c)
+
+
 def norm_parts(summed):
     row_mean = jnp.mean(summed, axis=-1, keepdims=True)
     centred = summed - row_mean
@@ -1069,18 +1113,16 @@
     rows = MB * rows_in
     weights, vectors = params[:6], params[6:]
     sizes = [item.shape[0] for item in vectors]
-    small = jnp.concatenate(vectors).reshape(-1, 128)
-    *wholes, small_whole = gather_weights(weights, small)
+    *wholes, small_whole = gather_weights(weights, vectors)
     query_w, key_w, value_w, out_w, up_w, down_w = wholes
-    flat = small_whole.reshape(2, -1).astype(F32)
     spots = [sum(sizes[:i]) for i in range(len(sizes) + 1)]
+    lines = [spot // small_whole.shape[2] for spot in spots]
     bias_query, bias_value, bias_out, bias_up, bias_down, gain_one, shift_one, gain_two, shift_two = (
-        flat[:, spots[i] : spots[i + 1]].reshape(1, -1) for i in range(len(sizes))
+        small_whole[:, lines[i] : lines[i + 1]].reshape(1, -1) for i in range(len(sizes))
     )
     x = tokens.reshape(rows, width)
-    lens = lengths[0]
-    block_of = dealing[0]
-    slot_of = jnp.argsort(block_of, axis=1).astype(jnp.int32)
+    lens, block_of = lengths, dealing
+    slot_of = jnp.argsort(block_of, axis=2).astype(jnp.int32)
     q = (dot(x, query_w, ROW_COL) + bias_query).astype(BF16)
     k = dot(x, key_w, ROW_COL).astype(BF16)
     v = (dot(x, value_w, ROW_COL) + bias_value).astype(BF16)
@@ -1091,8 +1133,9 @@
     n_one = unit_one * gain_one + shift_one
     n_low = n_one.astype(BF16)
     u = dot(n_low, up_w, ROW_COL) + bias_up
-    act, act_back = jax.vjp(gelu_exact, u)
-    g = act.astype(BF16)
+    below = 0.5 * (1.0 + lax.erf(u * math.sqrt(0.5)))
+    slope = below + u * jnp.exp(-0.5 * u * u) * (1.0 / math.sqrt(2.0 * math.pi))
+    g, slope = lax.optimization_barrier(((u * below).astype(BF16), slope))
     h_two = n_one + (dot(g, down_w, ROW_COL) + bias_down)
     unit_two, scale_two = norm_parts(h_two)
     output = (unit_two * gain_two + shift_two).astype(BF16)
@@ -1100,9 +1143,8 @@
     cot = cotangent.reshape(rows, width).astype(F32)
     dh_two = norm_back(cot, unit_two, scale_two, gain_two)
     dm = dh_two.astype(BF16)
-    (du_full,) = act_back(dot(dm, down_w, COL_COL))
-    du = du_full.astype(BF16)
-    dn = dot(du, up_w, COL_COL) + dh_two
+    du = lax.optimization_barrier((slope * dot(dm, down_w, COL_COL)).astype(BF16))
+    dn = lax.optimization_barrier(dot(du, up_w, COL_COL)) + dh_two
     dh_one = norm_back(dn, unit_one, scale_one, gain_one)
     do = dh_one.astype(BF16)
     da = dot(do, out_w, COL_COL).astype(BF16)
@@ -1132,21 +1174,14 @@
         dh_one + dot(dq, query_w, COL_COL) + dot(dk, key_w, COL_COL) + dot(dv, value_w, COL_COL)
     )
     grad_tokens = grad_rows.astype(BF16)
-    half = width // 2
-    o_a = o_a.reshape(2, -1, o_a.shape[3])
-    square = [
-        jnp.concatenate([o_a[0, :, i * half : (i + 1) * half], o_a[1, :, i * half : (i + 1) * half]], axis=1)
-        for i in range(4)
-    ]
-    o_b = o_b.reshape(2, -1, o_b.shape[3])
-    up = jnp.concatenate([o_b[0], o_b[1]], axis=1)
-    down = o_c.reshape(-1, width)
+    *square, up, down = widen(o_a, o_b, o_c)
+    down = down.reshape(-1, width)
     vec_sum = vec_sum.reshape(-1)
     ends = [vec_sum[spots[i] : spots[i + 1]] for i in range(len(sizes))]
     shape = (1, MB, rows_in, width)
     return (
         (output.reshape(shape), grad_tokens.reshape(shape))
-        + tuple(item.astype(F32) for item in square + [up, down])
+        + (*square, up, down)
         + tuple(ends)
     )
 

time: 478 us -> 433 us (0.906)
  other arithmetic: 23.3 us -> 9.6 us
  matrix products: 65.1 us -> 52 us
  Pallas kernels: 365 us -> 352 us
  local copies, waits for them, and re-layouts: 17 us -> 11.1 us
    pallas_call x1, Pallas kernels: 213 us -> 184 us  [reduce_grads(): pl.pallas_call(reduce_kernel, out_shape=[jax.ShapeDtypeStruct(a_shape, BF...]
    convert_element_type x6 -> x0, other arithmetic: 15.5 us -> none  [per_device_heads(): item.astype(F32)]
    pallas_call x1 -> x2, Pallas kernels: 65.8 us -> 81.3 us  [the longest x1 67.4 us: gather_weights(): pl.pallas_call(functools.partial(gather_kernel, plan, count, len(vectors)...]
    dot_general x16, matrix products: 65.1 us -> 52 us  [dot(): return lax.dot_general(a, b, (dims, ((), ())), preferred_element_type=F32)]
    unnamed x90 -> x70, local copies, waits for them, and re-layouts: 9.75 us -> 6 us
where the time goes in v3:
time: 433 us; the launch traced here: 426 us
  Pallas kernels  352 us (81%)
  matrix products  52 us (12%)
  local copies, waits for them, and re-layouts  11.1 us (3%)
  other arithmetic  9.6 us (2%)
    pallas_call x1, Pallas kernels, reduce_grads(): pl.pallas_call(reduce_kernel, out_shape=[jax.ShapeDtypeStruct(a_shape, BF...  184 us
    pallas_call x1, Pallas kernels, gather_weights(): pl.pallas_call(functools.partial(gather_kernel, plan, count, len(vectors)...  67.4 us
    dot_general x16, matrix products, dot(): return lax.dot_general(a, b, (dims, ((), ())), preferred_element_type=F32)  52 us
    pallas_call x1, Pallas kernels, attend_back(): pl.pallas_call(functools.partial(attend_back_kernel, heads), out_shape=[s...  44.8 us
    pallas_call x1, Pallas kernels, attend(): pl.pallas_call(functools.partial(attend_kernel, heads), out_shape=[jax.Sh...  42.3 us
    pallas_call x1, Pallas kernels, widen(): pl.pallas_call(widen_kernel, grid=(shards,), out_shape=[jax.ShapeDtypeStr...  13.8 us

profile of v3, /device:TPU:0, one launch (start us, length us, event | category | flops | bytes accessed | tf_op | source)
XLA Modules:
  0.0 426.1 jit_solution(9148441708007314043)
XLA Ops:
  4.0 1.4 sort.17
  6.1 67.4 %gather_weights.1 = (bf16[1024,1024]{1,0:T(8,128)(2,1)}, bf16[1024,1024]{1,0:T(8,128)(2,1)}, bf16[1024,1024]{1,0:T(8,128)(2,1)}, bf16[1024,1024]{1,0:T(8,128)(2,...) custom-call(bf16[512,1024]{1,0:T(8,128)(2,1)} %refs_0_.2, ...), custom_call_target="tpu_custom_call" | custom-call | tf_op jit(solution)/shard_map/gather_weights/pallas_call | solution.py:521
  74.3 1.6 fusion.16
  76.2 3.1 fusion.11.v_ref
  82.3 42.3 %attend.1 = (bf16[192,1024]{1,0:T(8,128)(2,1)}, bf16[3,16,96,128]{3,2,1,0:T(8,128)(2,1)}, f32[8,512]{1,0:T(8,128)}) custom-call(s32[1,3,2]{2,1,0:T(4,128)} %copy.41.lens_ref.refs_0_, s32[1,3,16]{2,1,0:T(4,128)} %copy.42.slot_ref.refs_1_, s32[1,3,16]{2,1,0:T(4,128)} %copy.43.block_ref.refs_2_, bf16[192,1024]{1,0:T(8,128)(2,1)} %fusion.12.q_ref, ...), custom_call_target="tpu_custom_call" | custom-call | tf_op jit(solution)/shard_map/attend/pallas_call | solution.py:652
  124.6 1.7 fusion.17
  126.9 8.2 %fusion.4 = (f32[192,4096]{1,0:T(8,128)}, bf16[192,4096]{1,0:T(8,128)(2,1)S(1)}) fusion(f32[4096]{0:T(1024)S(1)} %bitcast.113, bf16[192,1024]{1,0:T(8,128)(2,1)S(1)} %fusion.15.refs_8_, bf16[1024,4096]{1,0:T(8,128)(2,1)} %get-tuple-element.58), kind=kOutput, calls=%fused_computation.10 | convolution fusion | flops 1619263488 | bytes 13516800 | tf_op jit(solution)/shard_map/dot_general | solution.py:1104
  135.2 2.3 fusion.18
  138.1 1.4 convert_reduce_fusion.2
  139.5 7.6 %fusion.refs_11_ = bf16[192,4096]{1,0:T(8,128)(2,1)S(1)} fusion(f32[192,4096]{1,0:T(8,128)} %get-tuple-element.61, bf16[192,1024]{1,0:T(8,128)(2,1)S(1)} %get-tuple-element.94.refs_12_, bf16[4096,1024]{1,0:T(8,128)(2,1)} %get-tuple-element.60), kind=kOutput, calls=%fused_computation.2 | convolution fusion | flops 1612185600 | bytes 13500416 | tf_op jit(solution)/shard_map/dot_general | solution.py:1104
  147.2 3.9 fusion.19
  151.1 2.6 multiply_reduce_fusion
  153.7 2.5 convert_reduce_fusion.3
  156.2 1.6 convolution_convert_fusion.5.refs_3_
  158.1 44.8 %attend_back.1 = (bf16[192,1024]{1,0:T(8,128)(2,1)}, bf16[192,1024]{1,0:T(8,128)(2,1)}, bf16[192,1024]{1,0:T(8,128)(2,1)}, bf16[384,1024]{1,0:T(8,128)(2,1)}, bf...) custom-call(s32[1,3,2]{2,1,0:T(4,128)} %copy.41.lens_ref.refs_0_, ...), custom_call_target="tpu_custom_call" | custom-call | tf_op jit(solution)/shard_map/attend_back/pallas_call | solution.py:811
  202.9 2.0 convolution_add_fusion.5
  206.6 1.6 fusion.7
  209.1 2.9 convolution_convert_fusion.3
  212.0 4.8 %convolution_convert_fusion.2 = bf16[1024,1536]{1,0:T(8,128)(2,1)} fusion(bf16[384,1024]{1,0:T(8,128)(2,1)} %get-tuple-element.67, bf16[384,1536]{1,0:T(8,128)(2,1)S(1)} %copy-done.21), kind=kOutput, calls=%fused_computation.6 | convolution fusion | flops 1209532416 | bytes 5111808 | tf_op jit(solution)/shard_map/dot_general | solution.py:1104
  216.8 4.4 %convolution_convert_fusion.1 = bf16[1024,2048]{1,0:T(8,128)(2,1)} fusion(bf16[384,1024]{1,0:T(8,128)(2,1)S(1)} %copy-done.23, bf16[384,2048]{1,0:T(8,128)(2,1)S(1)} %copy-done.20), kind=kOutput, calls=%fused_computation.5 | convolution fusion | flops 1612709888 | bytes 6553600 | tf_op jit(solution)/shard_map/dot_general | solution.py:1104
  221.3 4.4 %convolution_convert_fusion = bf16[2048,1024]{1,0:T(8,128)(2,1)} fusion(bf16[384,2048]{1,0:T(8,128)(2,1)S(1)} %copy-done.19, bf16[384,1024]{1,0:T(8,128)(2,1)S(1)} %copy-done.22), kind=kOutput, calls=%fused_computation.4 | convolution fusion | flops 1612709888 | bytes 6553600 | tf_op jit(solution)/shard_map/dot_general | solution.py:1104
  225.7 183.7 %reduce_grads.1 = (bf16[2,8,64,2048]{3,2,1,0:T(8,128)(2,1)}, bf16[2,8,64,2048]{3,2,1,0:T(8,128)(2,1)}, bf16[2,8,128,1024]{3,2,1,0:T(8,128)(2,1)}, f32[48,128]{1,0:T(8,128)}) custom-call(bf16[2,8,64,1536]{3,2,1,0:T(8,128)(2,1)} %bitcast.96, bf16[2,8,64,512]{3,2,1,0:T(8,128)(2,1)} %bitcast.97, bf16[2,8,64,2048]{3,2,1,0:T(8,128)(2,1)} %bitcast.89, ...), custom_call_target="tpu_custom_call" | custom-call | tf_op jit(solution)/shard_map/reduce_grads/pallas_call | solution.py:1037
  410.7 1.4 slice_bitcast_fusion.2
  412.0 13.8 %widen.1 = (f32[512,1024]{1,0:T(8,128)}, f32[512,1024]{1,0:T(8,128)}, f32[512,1024]{1,0:T(8,128)}, f32[512,1024]{1,0:T(8,128)}, f32[512,4096]{1,0:T(8,128)}, /*index=5*/f32[2,8,128,1024]{3,2,1,0:T(8,128)}) custom-call(bf16[2,8,64,2048]{3,2,1,0:T(8,128)(2,1)} %get-tuple-element.75.a_ref, bf16[2,8,64,2048]{3,2,1,0:T(8,128)(2,1)} %get-tuple-element.76.b_ref, ...), custom_call_target="tpu_custom_call" | custom-call | tf_op jit(solution)/shard_map/widen/pallas_call | solution.py:1075
  (105 shorter events, 13.4 us)
Async XLA Ops:
  6.1 69.8 %copy-start.5 = (bf16[1,3,64,1024]{3,2,1,0:T(8,128)(2,1)S(1)}, bf16[1,3,64,1024]{3,2,1,0:T(8,128)(2,1)}, u32[]{:S(2)}) copy-start(bf16[1,3,64,1024]{3,2,1,0:T(8,128)(2,1)} %param.20) | copy-start | bytes 1179652
  6.1 70.1 %copy-start.7 = (bf16[1,3,64,1024]{3,2,1,0:T(8,128)(2,1)S(1)}, bf16[1,3,64,1024]{3,2,1,0:T(8,128)(2,1)}, u32[]{:S(2)}) copy-start(bf16[1,3,64,1024]{3,2,1,0:T(8,128)(2,1)} %param.19) | copy-start | bytes 1179652
  76.2 3.1 copy-start.11
  81.0 43.7 %copy-start.1 = (bf16[1024,1024]{1,0:T(8,128)(2,1)S(1)}, bf16[1024,1024]{1,0:T(8,128)(2,1)}, u32[]{:S(2)}) copy-start(bf16[1024,1024]{1,0:T(8,128)(2,1)} %get-tuple-element.57) | copy-start | bytes 6291460
  126.8 8.4 %copy-start.16 = (bf16[192,1024]{1,0:T(8,128)(2,1)}, bf16[192,1024]{1,0:T(8,128)(2,1)S(1)}, u32[]{:S(2)}) copy-start(bf16[192,1024]{1,0:T(8,128)(2,1)S(1)} %fusion.15.refs_8_) | copy-start | bytes 1179652
  126.8 8.4 %slice-start = ((s8[8388608]{0:T(1024)(128)(4,1)}), s8[4194304]{0:T(1024)(128)(4,1)S(1)}, s32[]{:S(2)}) async-start(s8[8388608]{0:T(1024)(128)(4,1)} %bitcast.87), calls=%async_computation | async-start | bytes 8388608
  126.9 8.3 %slice-start.1 = ((s8[8388608]{0:T(1024)(128)(4,1)}), s8[4194304]{0:T(1024)(128)(4,1)S(1)}, s32[]{:S(2)}) async-start(s8[8388608]{0:T(1024)(128)(4,1)} %bitcast.87), calls=%async_computation.1 | async-start | bytes 8388608
  126.9 8.3 %copy-start.18 = (f32[2,1,512]{2,1,0:T(1,128)S(1)}, f32[2,1,512]{2,1,0:T(1,128)}, u32[]{:S(2)}) copy-start(f32[2,1,512]{2,1,0:T(1,128)} %get-tuple-element.105) | copy-start | bytes 12292
  135.2 2.3 copy-start.14
  138.1 9.0 %slice-start.2 = ((s8[8388608]{0:T(1024)(128)(4,1)}), s8[4194304]{0:T(1024)(128)(4,1)S(1)}, s32[]{:S(2)}) async-start(s8[8388608]{0:T(1024)(128)(4,1)} %bitcast.117), calls=%async_computation.2 | async-start | bytes 8388608
  139.5 7.6 %copy-start.6 = (bf16[192,1024]{1,0:T(8,128)(2,1)}, bf16[192,1024]{1,0:T(8,128)(2,1)S(1)}, u32[]{:S(2)}) copy-start(bf16[192,1024]{1,0:T(8,128)(2,1)S(1)} %get-tuple-element.94.refs_12_) | copy-start | bytes 1179652
  139.5 7.6 %slice-start.3 = ((s8[8388608]{0:T(1024)(128)(4,1)}), s8[4194304]{0:T(1024)(128)(4,1)S(1)}, s32[]{:S(2)}) async-start(s8[8388608]{0:T(1024)(128)(4,1)} %bitcast.117), calls=%async_computation.3 | async-start | bytes 8388608
  147.2 10.6 %copy-start = (bf16[192,4096]{1,0:T(8,128)(2,1)}, bf16[192,4096]{1,0:T(8,128)(2,1)S(1)}, u32[]{:S(2)}) copy-start(bf16[192,4096]{1,0:T(8,128)(2,1)S(1)} %fusion.refs_11_) | copy-start | bytes 4718596
  153.7 2.5 copy-start.2
  156.2 1.9 copy-start.8
  158.1 44.8 %copy-start.9 = (f32[192,1024]{1,0:T(8,128)S(1)}, f32[192,1024]{1,0:T(8,128)}, u32[]{:S(2)}) copy-start(f32[192,1024]{1,0:T(8,128)} %get-tuple-element.98) | copy-start | bytes 2359300
  158.1 44.8 %copy-start.12 = (bf16[1024,1024]{1,0:T(8,128)(2,1)S(1)}, bf16[1024,1024]{1,0:T(8,128)(2,1)}, u32[]{:S(2)}) copy-start(bf16[1024,1024]{1,0:T(8,128)(2,1)} %get-tuple-element.52) | copy-start | bytes 6291460
  202.9 2.1 copy-start.4
  202.9 2.1 copy-start.17
  208.2 3.9 copy-start.21
  212.0 4.8 %copy-start.20 = (bf16[384,2048]{1,0:T(8,128)(2,1)S(1)}, bf16[384,2048]{1,0:T(8,128)(2,1)}, u32[]{:S(2)}) copy-start(bf16[384,2048]{1,0:T(8,128)(2,1)} %get-tuple-element.72) | copy-start | bytes 4718596
  212.0 4.8 %copy-start.23 = (bf16[384,1024]{1,0:T(8,128)(2,1)S(1)}, bf16[384,1024]{1,0:T(8,128)(2,1)}, u32[]{:S(2)}) copy-start(bf16[384,1024]{1,0:T(8,128)(2,1)} %get-tuple-element.71) | copy-start | bytes 2359300
  216.8 4.4 %copy-start.19 = (bf16[384,2048]{1,0:T(8,128)(2,1)S(1)}, bf16[384,2048]{1,0:T(8,128)(2,1)}, u32[]{:S(2)}) copy-start(bf16[384,2048]{1,0:T(8,128)(2,1)} %get-tuple-element.73) | copy-start | bytes 4718596
  216.8 4.4 %copy-start.22 = (bf16[384,1024]{1,0:T(8,128)(2,1)S(1)}, bf16[384,1024]{1,0:T(8,128)(2,1)}, u32[]{:S(2)}) copy-start(bf16[384,1024]{1,0:T(8,128)(2,1)} %get-tuple-element.74) | copy-start | bytes 2359300
  (4 other events, 6.6 us)

commit v4 on v3

--- a/solution.py
+++ b/solution.py
@@ -410,135 +410,6 @@
     return copy
 
 
-def gather_kernel(plan, n_weights, n_vectors, *refs):
-    shards, vectors = refs[:n_weights], refs[n_weights : n_weights + n_vectors]
-    refs = refs[n_weights + n_vectors :]
-    wholes, small_whole = refs[:n_weights], refs[n_weights]
-    stages = refs[n_weights + 1 : 2 * n_weights + 1]
-    small, small_in = refs[2 * n_weights + 1 : 2 * n_weights + 3]
-    send_sem, recv_sem, small_sems, local_sem, stage_sem = refs[2 * n_weights + 3 :]
-    c, w = lax.axis_index("ctx"), lax.axis_index("wsh")
-    o = 1 - w
-    by_x, by_y, by_z, by_core = (c, o), (flip(c, 2), w), (flip(c, 4), w), (flip(c, 1), w)
-    core, y, z = bit_of(c, 1), bit_of(c, 2), bit_of(c, 4)
-    mine = core * 4 + z * 2 + y
-    from_y, from_z = core * 4 + z * 2 + (1 - y), core * 4 + (1 - z) * 2 + y
-    staged, locals_ = [], []
-    for index, (shard, stage) in enumerate(zip(shards, stages)):
-        copy = pltpu.make_async_copy(shard, stage, stage_sem.at[index])
-        copy.start()
-        staged.append(copy)
-    line, lanes = 0, small.shape[1]
-    for vector in vectors:
-        for first in range(0, vector.shape[0], lanes):
-            piece = vector[pl.ds(first, lanes)].astype(F32)
-            small[line : line + 1, :] = piece.reshape(1, lanes)
-            line += 1
-    greet((by_x, by_y, by_z, by_core))
-    small_sent = send(small, small_in, small_sems.at[0], small_sems.at[1], by_x)
-
-    def part(chunk, side, piece, start, count):
-        tensor, first, rows = plan[chunk]
-        size = rows // 8
-        half = shards[tensor].shape[0]
-        at = side * half + first + piece * size + start
-        return wholes[tensor].at[pl.ds(pl.multiple_of(at, 8), count)]
-
-    steps = {}
-    for chunk, (tensor, first, rows) in enumerate(plan):
-        size = rows // 8
-        src = shards[tensor].at[pl.ds(pl.multiple_of(first + mine * size, 8), size)]
-        steps[chunk, 0] = send(
-            src, part(chunk, w, mine, 0, size), send_sem.at[0, chunk], recv_sem.at[0, chunk], by_x
-        )
-
-    for index, (stage, whole) in enumerate(zip(stages, wholes)):
-        rows = stage.shape[0]
-        staged[index].wait()
-        copy = pltpu.make_async_copy(
-            stage, whole.at[pl.ds(pl.multiple_of(w * rows, rows), rows)], local_sem.at[index]
-        )
-        copy.start()
-        locals_.append(copy)
-
-    def second(chunk):
-        size = plan[chunk][2] // 8
-        steps[chunk, 0].wait_recv()
-        for kind, peer in ((1, by_y), (2, by_z)):
-            ref = part(chunk, o, mine, 0, size)
-            steps[chunk, kind] = send(
-                ref, ref, send_sem.at[kind, chunk], recv_sem.at[kind, chunk], peer
-            )
-
-    def third(chunk):
-        size = plan[chunk][2] // 8
-        steps[chunk, 1].wait_recv()
-        steps[chunk, 2].wait_recv()
-        ref = part(chunk, o, from_z, 0, size // 2)
-        steps[chunk, 3] = send(ref, ref, send_sem.at[3, chunk], recv_sem.at[3, chunk], by_y)
-        ref = part(chunk, o, from_y, size // 2, size // 2)
-        steps[chunk, 4] = send(ref, ref, send_sem.at[4, chunk], recv_sem.at[4, chunk], by_z)
-
-    def fourth(chunk):
-        size = plan[chunk][2] // 8
-        steps[chunk, 3].wait_recv()
-        steps[chunk, 4].wait_recv()
-        ref = part(chunk, o, core * 4, 0, 4 * size)
-        steps[chunk, 5] = send(ref, ref, send_sem.at[5, chunk], recv_sem.at[5, chunk], by_core)
-
-    count = len(plan)
-    for turn in range(count + 2):
-        if turn < count:
-            second(turn)
-        if 0 <= turn - 1 < count:
-            third(turn - 1)
-        if 0 <= turn - 2 < count:
-            fourth(turn - 2)
-    for chunk in range(count):
-        steps[chunk, 5].wait_recv()
-        for kind in range(6):
-            steps[chunk, kind].wait_send()
-    small_sent.wait()
-    small_whole[w] = small[...]
-    small_whole[o] = small_in[...]
-    for copy in locals_:
-        copy.wait()
-
-
-def gather_weights(shards, vectors):
-    plan = []
-    for index, shard in enumerate(shards):
-        rows = shard.shape[0]
-        parts = max(1, shard.shape[0] * shard.shape[1] // (1024 * 1024))
-        for piece in range(parts):
-            plan.append((index, piece * (rows // parts), rows // parts))
-    count = len(shards)
-    shapes = [jax.ShapeDtypeStruct((2 * s.shape[0],) + s.shape[1:], s.dtype) for s in shards]
-    lanes = min(item.shape[0] for item in vectors)
-    lines = sum(item.shape[0] for item in vectors) // lanes
-    shapes.append(jax.ShapeDtypeStruct((2, lines, lanes), F32))
-    anywhere, vmem = pl.BlockSpec(memory_space=pl.ANY), pl.BlockSpec(memory_space=pltpu.VMEM)
-    return pl.pallas_call(
-        functools.partial(gather_kernel, plan, count, len(vectors)),
-        out_shape=shapes,
-        in_specs=[anywhere] * count + [vmem] * len(vectors),
-        out_specs=[anywhere] * count + [vmem],
-        scratch_shapes=[pltpu.VMEM(s.shape, s.dtype) for s in shards]
-        + [pltpu.VMEM((lines, lanes), F32)] * 2
-        + [
-            pltpu.SemaphoreType.DMA((6, len(plan))),
-            pltpu.SemaphoreType.DMA((6, len(plan))),
-            pltpu.SemaphoreType.DMA((2,)),
-            pltpu.SemaphoreType.DMA((count,)),
-            pltpu.SemaphoreType.DMA((count,)),
-        ],
-        compiler_params=pltpu.CompilerParams(
-            collective_id=0, has_side_effects=True, vmem_limit_bytes=VMEM_BYTES
-        ),
-        name="gather_weights",
-    )(*shards, *vectors)
-
-
 def plane_peers(c, w, count):
     return [(lax.rem(c + step, count), w) for step in range(1, count)]
 
@@ -569,35 +440,200 @@
     return pltpu.make_async_copy(view, view, sem)
 
 
-def attend_kernel(
-    heads,
-    lens_ref,
-    slot_ref,
-    block_ref,
-    q_ref,
-    k_ref,
-    v_ref,
-    a_ref,
-    kept_ref,
-    lse_ref,
-    *scratch,
-):
-    in_buf = scratch[:MB]
-    out_buf, back_out, back_in, q_s, k_s, v_s, a_s = scratch[MB : MB + 7]
-    send_sem, recv_sem, back_send, back_recv, keep_sem = scratch[MB + 7 :]
+SQUARE, PAIR, ALONE = 8, 4, 2
+
+
+def weight_plan(shards):
+    plan, first_bulk = [], 3
+    for index in range(first_bulk):
+        plan.append((index, 0, shards[index].shape[0], SQUARE))
+    unit = shards[0].shape[0] * shards[0].shape[1]
+    bulk = []
+    for index in range(first_bulk, len(shards)):
+        rows, cols = shards[index].shape
+        parts = max(1, rows * cols // unit)
+        for part in range(parts):
+            bulk.append((index, part * (rows // parts), rows // parts))
+    squares, alone = BULK_WAYS
+    for number, item in enumerate(bulk):
+        if number < squares:
+            way = SQUARE
+        elif number >= len(bulk) - alone:
+            way = ALONE
+        else:
+            way = PAIR
+        plan.append(item + (way,))
+    return plan
+
+
+BULK_WAYS = (2, 2)
+
+
+def forward_kernel(heads, plan, n_weights, n_vectors, *refs):
+    lens_ref, slot_ref, block_ref, x_ref = refs[:4]
+    refs = refs[4:]
+    shards, vectors = refs[:n_weights], refs[n_weights : n_weights + n_vectors]
+    refs = refs[n_weights + n_vectors :]
+    wholes, small_whole, a_ref, kept_ref, lse_ref = refs[:n_weights], *refs[n_weights : n_weights + 4]
+    refs = refs[n_weights + 4 :]
+    near, stages, refs = refs[:3], refs[3:n_weights], refs[n_weights:]
+    small, small_in, bias, q_ref, k_ref, v_ref = refs[:6]
+    in_buf = refs[6 : 6 + MB]
+    out_buf, back_out, back_in, q_s, k_s, v_s, a_s = refs[6 + MB : 13 + MB]
+    (
+        w_send,
+        w_recv,
+        small_sems,
+        local_sem,
+        stage_sem,
+        send_sem,
+        recv_sem,
+        back_send,
+        back_recv,
+        keep_sem,
+    ) = refs[13 + MB :]
     c, w = lax.axis_index("ctx"), lax.axis_index("wsh")
+    o = 1 - w
+    by_x, by_y, by_z, by_core = (c, o), (flip(c, 2), w), (flip(c, 4), w), (flip(c, 1), w)
+    core, y, z = bit_of(c, 1), bit_of(c, 2), bit_of(c, 4)
     peers = plane_peers(c, w, heads)
-    greet(peers)
-    blocks = heads
+    targets = tuple(near) + tuple(wholes[3:])
+    staged, locals_ = [], []
+    for index, shard in enumerate(shards):
+        rows = shard.shape[0]
+        spot = pl.ds(pl.multiple_of(w * rows, rows), rows)
+        dst = near[index].at[spot] if index < 3 else stages[index - 3]
+        copy = pltpu.make_async_copy(shard, dst, stage_sem.at[index])
+        copy.start()
+        staged.append(copy)
+    line, lanes = 0, small.shape[1]
+    for vector in vectors:
+        for first in range(0, vector.shape[0], lanes):
+            piece = vector[pl.ds(first, lanes)].astype(F32)
+            small[line : line + 1, :] = piece.reshape(1, lanes)
+            line += 1
+    greet(peers + [by_x])
+    small_sent = send(small, small_in, small_sems.at[0], small_sems.at[1], by_x)
+
+    def part(chunk, side, piece, start, count):
+        tensor, first, rows, way = plan[chunk]
+        half = shards[tensor].shape[0]
+        at = side * half + first + piece * (rows // way) + start
+        return targets[tensor].at[pl.ds(pl.multiple_of(at, 8), count)]
+
+    steps = {}
+
+    def sem(kind, chunk):
+        return w_send.at[kind, chunk], w_recv.at[kind, chunk]
+
+    def own_piece(way):
+        return {SQUARE: core * 4 + z * 2 + y, PAIR: core * 2 + y, ALONE: core}[way]
+
+    for chunk, (tensor, first, rows, way) in enumerate(plan):
+        size, mine = rows // way, own_piece(way)
+        src = shards[tensor].at[pl.ds(pl.multiple_of(first + mine * size, 8), size)]
+        steps[chunk, 0] = send(src, part(chunk, w, mine, 0, size), *sem(0, chunk), by_x)
+
+    def second(chunk):
+        _, _, rows, way = plan[chunk]
+        if way == ALONE:
+            return
+        steps[chunk, 0].wait_recv()
+        ref = part(chunk, o, own_piece(way), 0, rows // way)
+        steps[chunk, 1] = send(ref, ref, *sem(1, chunk), by_y)
+        if way == SQUARE:
+            steps[chunk, 2] = send(ref, ref, *sem(2, chunk), by_z)
+
+    def third(chunk):
+        _, _, rows, way = plan[chunk]
+        if way != SQUARE:
+            return
+        size = rows // way
+        steps[chunk, 1].wait_recv()
+        steps[chunk, 2].wait_recv()
+        ref = part(chunk, o, core * 4 + (1 - z) * 2 + y, 0, size // 2)
+        steps[chunk, 3] = send(ref, ref, *sem(3, chunk), by_y)
+        ref = part(chunk, o, core * 4 + z * 2 + (1 - y), size // 2, size // 2)
+        steps[chunk, 4] = send(ref, ref, *sem(4, chunk), by_z)
+
+    def fourth(chunk):
+        _, _, rows, way = plan[chunk]
+        for kind in {SQUARE: (3, 4), PAIR: (1,), ALONE: (0,)}[way]:
+            steps[chunk, kind].wait_recv()
+        ref = part(chunk, o, core * (way // 2), 0, rows // 2)
+        steps[chunk, 5] = send(ref, ref, *sem(5, chunk), by_core)
+
+    for index in range(3):
+        staged[index].wait()
+    for turn in range(5):
+        for stage, act in enumerate((second, third, fourth)):
+            if 0 <= turn - stage < 3:
+                act(turn - stage)
+    small_sent.wait()
+    small_whole[w] = small[...]
+    small_whole[o] = small_in[...]
+    for side in range(2):
+        for row in range(2):
+            bias[row : row + 1, side * lanes : (side + 1) * lanes] = small_whole[
+                side, row : row + 1, :
+            ]
+    width = x_ref.shape[1]
+    step = 256
+    for index, (weight, out) in enumerate(zip(near, (q_ref, k_ref, v_ref))):
+        steps[index, 5].wait_recv()
+
+        def project(turn, carry):
+            cols = pl.ds(pl.multiple_of(turn * step, step), step)
+            total = jnp.dot(x_ref[...], weight[:, cols], preferred_element_type=F32)
+            if index != 1:
+                total = total + bias[index // 2 : index // 2 + 1, cols]
+            out[:, cols] = total.astype(BF16)
+            return carry
+
+        lax.fori_loop(0, width // step, project, 0)
     for m in range(MB):
         for pair in range(heads // 2):
             pack_three(q_ref, k_ref, v_ref, m * BLK, pair, out_buf.at[m])
         for peer in peers:
-            send(
-                out_buf.at[m, peer[0]], in_buf[m].at[c], send_sem.at[m], recv_sem.at[m], peer
-            )
+            send(out_buf.at[m, peer[0]], in_buf[m].at[c], send_sem.at[m], recv_sem.at[m], peer)
         in_buf[m][c] = out_buf[m, c]
+    for index in range(n_weights):
+        if index < 3:
+            copy = pltpu.make_async_copy(near[index], wholes[index], local_sem.at[index])
+        else:
+            rows = shards[index].shape[0]
+            spot = pl.ds(pl.multiple_of(w * rows, rows), rows)
+            staged[index].wait()
+            copy = pltpu.make_async_copy(
+                stages[index - 3], wholes[index].at[spot], local_sem.at[index]
+            )
+        copy.start()
+        locals_.append(copy)
+
+    bulk = range(3, len(plan))
+    kinds = {way: [i for i in bulk if plan[i][3] == way] for way in (SQUARE, PAIR, ALONE)}
+    squares, pairs, alone = kinds[SQUARE], kinds[PAIR], kinds[ALONE]
+    moves = [(second, i) for i in squares + pairs[:2]]
+    moves += [None]
+    moves += [(third, i) for i in squares] + [(second, i) for i in pairs[2:3]]
+    moves += [None]
+    moves += [(fourth, i) for i in squares] + [(second, i) for i in pairs[3:4]]
+    moves += [(fourth, i) for i in pairs[:2]]
+    moves += [None]
+    moves += [(second, i) for i in pairs[4:]] + [(fourth, i) for i in pairs[2:]]
+    moves += [(fourth, i) for i in alone]
+
+    def pump():
+        while moves:
+            move = moves.pop(0)
+            if move is None:
+                return
+            move[0](move[1])
+
+    blocks = heads
+    span = BPS * BLK
     for m in range(MB):
+        pump()
         all_bytes(in_buf[m], recv_sem.at[m], heads - 1).wait()
         keep = pltpu.make_async_copy(in_buf[m], kept_ref.at[m], keep_sem.at[m])
         keep.start()
@@ -606,9 +642,9 @@
             q_s[b * BLK : (b + 1) * BLK, :] = got[:BLK, :HD]
             k_s[b * BLK : (b + 1) * BLK, :] = got[:BLK, HD:]
             v_s[b * BLK : (b + 1) * BLK, :] = unpack_fold(got[BLK:])
-        span = BPS * BLK
-        for s in range(blocks // BPS):
-            rows = slice(s * span, (s + 1) * span)
+
+        def one_sequence(s, carry):
+            rows = pl.ds(pl.multiple_of(s * span, span), span)
             scores = lax.dot_general(
                 k_s[rows, :], q_s[rows, :], (((1,), (1,)), ((), ())), preferred_element_type=F32
             ) * (1.0 / math.sqrt(HD))
@@ -623,8 +659,11 @@
                 (((0,), (0,)), ((), ())),
                 preferred_element_type=F32,
             )
-            a_s[s * BPS : (s + 1) * BPS] = (out_t / total).T.reshape(BPS, BLK, HD)
+            a_s[pl.ds(s * BPS, BPS)] = (out_t / total).T.reshape(BPS, BLK, HD)
             lse_ref[pl.ds(m * (blocks // BPS) + s, 1), :] = top + jnp.log(total)
+            return carry
+
+        lax.fori_loop(0, blocks // BPS, one_sequence, 0)
         for t in range(blocks):
             back_out[m, t] = fold(a_s[block_ref[0, m, t]]).astype(BF16)
         for peer in peers:
@@ -632,6 +671,7 @@
                 back_out.at[m, peer[0]], back_in.at[m, c], back_send.at[m], back_recv.at[m], peer
             )
         back_in[m, c] = back_out[m, c]
+    pump()
     for m in range(MB):
         all_bytes(back_in.at[m], back_recv.at[m], heads - 1).wait()
         for pair in range(heads // 2):
@@ -642,23 +682,42 @@
         all_bytes(out_buf.at[m], send_sem.at[m], heads - 1).wait()
         all_bytes(back_out.at[m], back_send.at[m], heads - 1).wait()
         pltpu.make_async_copy(in_buf[m], kept_ref.at[m], keep_sem.at[m]).wait()
-
-
-def attend(lens, slot_of, block_of, q, k, v, heads):
-    vmem, smem = pl.BlockSpec(memory_space=pltpu.VMEM), pl.BlockSpec(memory_space=pltpu.SMEM)
-    rows, width = q.shape
+    for chunk in bulk:
+        steps[chunk, 5].wait_recv()
+    for flight in steps.values():
+        flight.wait_send()
+    for copy in locals_:
+        copy.wait()
+
+
+def forward(lens, slot_of, block_of, x, shards, vectors, heads):
+    plan = weight_plan(shards)
+    count = len(shards)
+    anywhere, vmem = pl.BlockSpec(memory_space=pl.ANY), pl.BlockSpec(memory_space=pltpu.VMEM)
+    smem = pl.BlockSpec(memory_space=pltpu.SMEM)
+    rows, width = x.shape
     pack_rows = BLK + BLK // 2
     span = BPS * BLK
+    lanes = min(item.shape[0] for item in vectors)
+    lines = sum(item.shape[0] for item in vectors) // lanes
+    whole = lambda s: (2 * s.shape[0],) + s.shape[1:]
     return pl.pallas_call(
-        functools.partial(attend_kernel, heads),
-        out_shape=[
+        functools.partial(forward_kernel, heads, plan, count, len(vectors)),
+        out_shape=[jax.ShapeDtypeStruct(whole(s), s.dtype) for s in shards]
+        + [
+            jax.ShapeDtypeStruct((2, lines, lanes), F32),
             jax.ShapeDtypeStruct((rows, width), BF16),
             jax.ShapeDtypeStruct((MB, heads, pack_rows, 128), BF16),
             jax.ShapeDtypeStruct((8, span), F32),
         ],
-        in_specs=[smem] * 3 + [vmem] * 3,
-        out_specs=[vmem, pl.BlockSpec(memory_space=pl.ANY), vmem],
-        scratch_shapes=[pltpu.VMEM((heads, pack_rows, 128), BF16)] * MB
+        in_specs=[smem] * 3 + [vmem] + [anywhere] * count + [vmem] * len(vectors),
+        out_specs=[anywhere] * count + [vmem, vmem, anywhere, vmem],
+        scratch_shapes=[pltpu.VMEM(whole(s), s.dtype) for s in shards[:3]]
+        + [pltpu.VMEM(s.shape, s.dtype) for s in shards[3:]]
+        + [pltpu.VMEM((lines, lanes), F32)] * 2
+        + [pltpu.VMEM((2, width), F32)]
+        + [pltpu.VMEM((rows, width), BF16)] * 3
+        + [pltpu.VMEM((heads, pack_rows, 128), BF16)] * MB
         + [
             pltpu.VMEM((MB, heads, pack_rows, 128), BF16),
             pltpu.VMEM((MB, heads, BLK // 2, 128), BF16),
@@ -667,17 +726,18 @@
             pltpu.VMEM((heads * BLK, HD), BF16),
             pltpu.VMEM((heads * BLK, HD), BF16),
             pltpu.VMEM((heads, BLK, HD), F32),
-            pltpu.SemaphoreType.DMA((MB,)),
-            pltpu.SemaphoreType.DMA((MB,)),
-            pltpu.SemaphoreType.DMA((MB,)),
-            pltpu.SemaphoreType.DMA((MB,)),
-            pltpu.SemaphoreType.DMA((MB,)),
-        ],
+            pltpu.SemaphoreType.DMA((6, len(plan))),
+            pltpu.SemaphoreType.DMA((6, len(plan))),
+            pltpu.SemaphoreType.DMA((2,)),
+            pltpu.SemaphoreType.DMA((count,)),
+            pltpu.SemaphoreType.DMA((count,)),
+        ]
+        + [pltpu.SemaphoreType.DMA((MB,))] * 5,
         compiler_params=pltpu.CompilerParams(
             collective_id=1, has_side_effects=True, vmem_limit_bytes=VMEM_BYTES
         ),
-        name="attend",
-    )(lens, slot_of, block_of, q, k, v)
+        name="forward",
+    )(lens, slot_of, block_of, x, *shards, *vectors)
 
 
 def attend_back_kernel(heads, *refs):
@@ -741,8 +801,9 @@
             v_s[rows, :] = unpack_fold(got[BLK:])
             a_s[rows, :] = unpack_fold(in_buf[m][slot])
         span = BPS * BLK
-        for s in range(blocks // BPS):
-            rows = slice(s * span, (s + 1) * span)
+
+        def one_sequence(s, carry):
+            rows = pl.ds(pl.multiple_of(s * span, span), span)
             qq, kk, vv, dd = q_s[rows, :], k_s[rows, :], v_s[rows, :], a_s[rows, :]
             scale = 1.0 / math.sqrt(HD)
             minor = (((1,), (1,)), ((), ()))
@@ -754,13 +815,16 @@
             both = probs * dp
             delta = jnp.sum(both, axis=0, keepdims=True)
             ds = (both - probs * delta).astype(BF16)
-            here = slice(s * BPS, (s + 1) * BPS)
+            here = pl.ds(s * BPS, BPS)
             split = (BPS, BLK, HD)
             dv = jnp.dot(probs.astype(BF16), dd, preferred_element_type=F32)
             dv_s[here] = dv.reshape(split)
             dk_s[here] = (jnp.dot(ds, qq, preferred_element_type=F32) * scale).reshape(split)
             dq_t = lax.dot_general(kk, ds, (((0,), (0,)), ((), ())), preferred_element_type=F32)
             dq_s[here] = (dq_t.T * scale).reshape(split)
+            return carry
+
+        lax.fori_loop(0, blocks // BPS, one_sequence, 0)
         for t in range(blocks):
             at = block_ref[0, m, t]
             back_out[m, t, 0:BLK, :] = jnp.concatenate([dq_s[at], dk_s[at]], axis=1).astype(BF16)
@@ -1113,21 +1177,18 @@
     rows = MB * rows_in
     weights, vectors = params[:6], params[6:]
     sizes = [item.shape[0] for item in vectors]
-    *wholes, small_whole = gather_weights(weights, vectors)
+    x = tokens.reshape(rows, width)
+    lens, block_of = lengths, dealing
+    slot_of = jnp.argsort(block_of, axis=2).astype(jnp.int32)
+    *wholes, small_whole, a, kept, lse = forward(
+        lens, slot_of, block_of, x, weights, vectors, HEADS
+    )
     query_w, key_w, value_w, out_w, up_w, down_w = wholes
     spots = [sum(sizes[:i]) for i in range(len(sizes) + 1)]
     lines = [spot // small_whole.shape[2] for spot in spots]
-    bias_query, bias_value, bias_out, bias_up, bias_down, gain_one, shift_one, gain_two, shift_two = (
+    _, _, bias_out, bias_up, bias_down, gain_one, shift_one, gain_two, shift_two = (
         small_whole[:, lines[i] : lines[i + 1]].reshape(1, -1) for i in range(len(sizes))
     )
-    x = tokens.reshape(rows, width)
-    lens, block_of = lengths, dealing
-    slot_of = jnp.argsort(block_of, axis=2).astype(jnp.int32)
-    q = (dot(x, query_w, ROW_COL) + bias_query).astype(BF16)
-    k = dot(x, key_w, ROW_COL).astype(BF16)
-    v = (dot(x, value_w, ROW_COL) + bias_value).astype(BF16)
-    a, kept, lse = attend(lens, slot_of, block_of, q, k, v, HEADS)
-
     h_one = x.astype(F32) + (dot(a, out_w, ROW_COL) + bias_out)
     unit_one, scale_one = norm_parts(h_one)
     n_one = unit_one * gain_one + shift_one

time: 433 us -> 404 us (0.933); the launches traced: 426 us -> 402 us
  Pallas kernels: 352 us -> 331 us
    pallas_call x2 -> x1, Pallas kernels: 110 us -> 92.6 us  [forward(): pl.pallas_call(functools.partial(forward_kernel, heads, plan, count, len(...]
    dot_general x16 -> x13, matrix products: 52 us -> 48.5 us  [dot(): return lax.dot_general(a, b, (dims, ((), ())), preferred_element_type=F32)]
where the time goes in v4:
time: 404 us; the launch traced here: 402 us
  Pallas kernels  331 us (82%)
  matrix products  48.5 us (12%)
  local copies, waits for them, and re-layouts  12.5 us (3%)
  other arithmetic  8.86 us (2%)
    pallas_call x1, Pallas kernels, reduce_grads(): pl.pallas_call(reduce_kernel, out_shape=[jax.ShapeDtypeStruct(a_shape, BF...  182 us
    pallas_call x1, Pallas kernels, forward(): pl.pallas_call(functools.partial(forward_kernel, heads, plan, count, len(...  92.6 us
    dot_general x13, matrix products, dot(): return lax.dot_general(a, b, (dims, ((), ())), preferred_element_type=F32)  48.5 us
    pallas_call x1, Pallas kernels, attend_back(): pl.pallas_call(functools.partial(attend_back_kernel, heads), out_shape=[s...  42.7 us
    pallas_call x1, Pallas kernels, widen(): pl.pallas_call(widen_kernel, grid=(shards,), out_shape=[jax.ShapeDtypeStr...  13.8 us

profile of v4, /device:TPU:0, one launch (start us, length us, event | category | flops | bytes accessed | tf_op | source)
XLA Modules:
  0.0 401.7 jit_solution(14237204528217930070)
XLA Ops:
  0.7 1.3 copy.41.refs_0_
  2.0 1.3 copy.43.refs_2_
  4.0 1.4 sort.17
  6.1 92.6 %forward.1 = (bf16[1024,1024]{1,0:T(8,128)(2,1)}, bf16[1024,1024]{1,0:T(8,128)(2,1)}, bf16[1024,1024]{1,0:T(8,128)(2,1)}, bf16[1024,1024]{1,0:T(8,128)(2,1)}, bf...) custom-call(s32[1,3,2]{2,1,0:T(4,128)} %copy.41.refs_0_, ...), custom_call_target="tpu_custom_call" | custom-call | tf_op jit(solution)/shard_map/forward/pallas_call | solution.py:704
  101.4 2.4 fusion.12
  104.3 8.3 %fusion.4 = (f32[192,4096]{1,0:T(8,128)}, bf16[192,4096]{1,0:T(8,128)(2,1)S(1)}) fusion(f32[4096]{0:T(1024)S(1)} %bitcast.97, bf16[192,1024]{1,0:T(8,128)(2,1)S(1)} %fusion.10.refs_8_, bf16[1024,4096]{1,0:T(8,128)(2,1)} %get-tuple-element.55), kind=kOutput, calls=%fused_computation.10 | convolution fusion | flops 1619263488 | bytes 13516800 | tf_op jit(solution)/shard_map/dot_general | solution.py:1168
  112.7 2.0 fusion.13
  115.9 1.1 convert_reduce_fusion.2
  117.0 7.6 %fusion.refs_11_ = bf16[192,4096]{1,0:T(8,128)(2,1)S(1)} fusion(f32[192,4096]{1,0:T(8,128)} %get-tuple-element.58, bf16[192,1024]{1,0:T(8,128)(2,1)S(1)} %get-tuple-element.94.refs_12_, bf16[4096,1024]{1,0:T(8,128)(2,1)} %get-tuple-element.57), kind=kOutput, calls=%fused_computation.2 | convolution fusion | flops 1612185600 | bytes 13500416 | tf_op jit(solution)/shard_map/dot_general | solution.py:1168
  124.7 3.9 fusion.14
  129.2 2.4 multiply_reduce_fusion
  132.1 2.2 convert_reduce_fusion.3
  134.4 3.3 convolution_convert_fusion.4.refs_3_
  138.7 42.7 %attend_back.1 = (bf16[192,1024]{1,0:T(8,128)(2,1)}, bf16[192,1024]{1,0:T(8,128)(2,1)}, bf16[192,1024]{1,0:T(8,128)(2,1)}, bf16[384,1024]{1,0:T(8,128)(2,1)}, bf...) custom-call(s32[1,3,2]{2,1,0:T(4,128)} %copy.41.refs_0_, ...), custom_call_target="tpu_custom_call" | custom-call | tf_op jit(solution)/shard_map/attend_back/pallas_call | solution.py:875
  181.4 2.0 convolution_add_fusion.3
  184.4 1.6 fusion.7
  187.0 2.7 convolution_convert_fusion.3
  189.7 5.0 %convolution_convert_fusion.2 = bf16[1024,1536]{1,0:T(8,128)(2,1)} fusion(bf16[384,1024]{1,0:T(8,128)(2,1)S(1)} %copy-done.21, bf16[384,1536]{1,0:T(8,128)(2,1)} %get-tuple-element.68), kind=kOutput, calls=%fused_computation.6 | convolution fusion | flops 1209532416 | bytes 5111808 | tf_op jit(solution)/shard_map/dot_general | solution.py:1168
  194.7 4.4 %convolution_convert_fusion.1 = bf16[1024,2048]{1,0:T(8,128)(2,1)} fusion(bf16[384,1024]{1,0:T(8,128)(2,1)S(1)} %copy-done.20, bf16[384,2048]{1,0:T(8,128)(2,1)S(1)} %copy-done.18), kind=kOutput, calls=%fused_computation.5 | convolution fusion | flops 1612709888 | bytes 6553600 | tf_op jit(solution)/shard_map/dot_general | solution.py:1168
  199.1 4.4 %convolution_convert_fusion = bf16[2048,1024]{1,0:T(8,128)(2,1)} fusion(bf16[384,2048]{1,0:T(8,128)(2,1)S(1)} %copy-done.17, bf16[384,1024]{1,0:T(8,128)(2,1)S(1)} %copy-done.19), kind=kOutput, calls=%fused_computation.4 | convolution fusion | flops 1612709888 | bytes 6553600 | tf_op jit(solution)/shard_map/dot_general | solution.py:1168
  203.5 181.6 %reduce_grads.1 = (bf16[2,8,64,2048]{3,2,1,0:T(8,128)(2,1)}, bf16[2,8,64,2048]{3,2,1,0:T(8,128)(2,1)}, bf16[2,8,128,1024]{3,2,1,0:T(8,128)(2,1)}, f32[48,128]{1,0:T(8,128)}) custom-call(bf16[2,8,64,1536]{3,2,1,0:T(8,128)(2,1)} %bitcast.80, bf16[2,8,64,512]{3,2,1,0:T(8,128)(2,1)} %bitcast.81, bf16[2,8,64,2048]{3,2,1,0:T(8,128)(2,1)} %bitcast.75, ...), custom_call_target="tpu_custom_call" | custom-call | tf_op jit(solution)/shard_map/reduce_grads/pallas_call | solution.py:1101
  385.1 1.3 slice_bitcast_fusion.1
  386.5 1.4 slice_bitcast_fusion.2
  387.8 13.8 %widen.1 = (f32[512,1024]{1,0:T(8,128)}, f32[512,1024]{1,0:T(8,128)}, f32[512,1024]{1,0:T(8,128)}, f32[512,1024]{1,0:T(8,128)}, f32[512,4096]{1,0:T(8,128)}, /*index=5*/f32[2,8,128,1024]{3,2,1,0:T(8,128)}) custom-call(bf16[2,8,64,2048]{3,2,1,0:T(8,128)(2,1)} %get-tuple-element.75.a_ref, bf16[2,8,64,2048]{3,2,1,0:T(8,128)(2,1)} %get-tuple-element.76.b_ref, ...), custom_call_target="tpu_custom_call" | custom-call | tf_op jit(solution)/shard_map/widen/pallas_call | solution.py:1139
  (99 shorter events, 9.8 us)
Async XLA Ops:
  6.1 94.3 %copy-start.1 = (bf16[1,3,64,1024]{3,2,1,0:T(8,128)(2,1)S(1)}, bf16[1,3,64,1024]{3,2,1,0:T(8,128)(2,1)}, u32[]{:S(2)}) copy-start(bf16[1,3,64,1024]{3,2,1,0:T(8,128)(2,1)} %param.20) | copy-start | bytes 1179652
  6.1 95.3 %copy-start.2 = (bf16[1,3,64,1024]{3,2,1,0:T(8,128)(2,1)S(1)}, bf16[1,3,64,1024]{3,2,1,0:T(8,128)(2,1)}, u32[]{:S(2)}) copy-start(bf16[1,3,64,1024]{3,2,1,0:T(8,128)(2,1)} %param.19) | copy-start | bytes 1179652
  104.1 8.6 %slice-start = ((s8[8388608]{0:T(1024)(128)(4,1)}), s8[4194304]{0:T(1024)(128)(4,1)S(1)}, s32[]{:S(2)}) async-start(s8[8388608]{0:T(1024)(128)(4,1)} %bitcast.73), calls=%async_computation | async-start | bytes 8388608
  104.3 8.3 %copy-start.11 = (bf16[192,1024]{1,0:T(8,128)(2,1)}, bf16[192,1024]{1,0:T(8,128)(2,1)S(1)}, u32[]{:S(2)}) copy-start(bf16[192,1024]{1,0:T(8,128)(2,1)S(1)} %fusion.10.refs_8_) | copy-start | bytes 1179652
  104.3 8.3 %slice-start.1 = ((s8[8388608]{0:T(1024)(128)(4,1)}), s8[4194304]{0:T(1024)(128)(4,1)S(1)}, s32[]{:S(2)}) async-start(s8[8388608]{0:T(1024)(128)(4,1)} %bitcast.73), calls=%async_computation.1 | async-start | bytes 8388608
  112.6 2.0 copy-start.9
  115.9 8.7 %slice-start.2 = ((s8[8388608]{0:T(1024)(128)(4,1)}), s8[4194304]{0:T(1024)(128)(4,1)S(1)}, s32[]{:S(2)}) async-start(s8[8388608]{0:T(1024)(128)(4,1)} %bitcast.99), calls=%async_computation.2 | async-start | bytes 8388608
  117.0 7.6 %copy-start.3 = (bf16[192,1024]{1,0:T(8,128)(2,1)}, bf16[192,1024]{1,0:T(8,128)(2,1)S(1)}, u32[]{:S(2)}) copy-start(bf16[192,1024]{1,0:T(8,128)(2,1)S(1)} %get-tuple-element.94.refs_12_) | copy-start | bytes 1179652
  117.0 7.6 %slice-start.3 = ((s8[8388608]{0:T(1024)(128)(4,1)}), s8[4194304]{0:T(1024)(128)(4,1)S(1)}, s32[]{:S(2)}) async-start(s8[8388608]{0:T(1024)(128)(4,1)} %bitcast.99), calls=%async_computation.3 | async-start | bytes 8388608
  124.7 13.7 %copy-start = (bf16[192,4096]{1,0:T(8,128)(2,1)}, bf16[192,4096]{1,0:T(8,128)(2,1)S(1)}, u32[]{:S(2)}) copy-start(bf16[192,4096]{1,0:T(8,128)(2,1)S(1)} %fusion.refs_11_) | copy-start | bytes 4718596
  134.4 4.3 %copy-start.4 = (bf16[192,1024]{1,0:T(8,128)(2,1)}, bf16[192,1024]{1,0:T(8,128)(2,1)S(1)}, u32[]{:S(2)}) copy-start(bf16[192,1024]{1,0:T(8,128)(2,1)S(1)} %get-tuple-element.97.refs_10_) | copy-start | bytes 1179652
  138.7 42.7 %copy-start.7 = (bf16[1024,1024]{1,0:T(8,128)(2,1)S(1)}, bf16[1024,1024]{1,0:T(8,128)(2,1)}, u32[]{:S(2)}) copy-start(bf16[1024,1024]{1,0:T(8,128)(2,1)} %get-tuple-element.62) | copy-start | bytes 6291460
  181.4 2.1 copy-start.6
  181.4 2.1 copy-start.12
  181.4 2.9 copy-start.5
  181.4 2.9 copy-start.8
  183.4 2.7 copy-start.10
  184.4 2.0 copy-start.13
  184.4 2.6 copy-start.22
  184.4 5.3 %copy-start.21 = (bf16[384,1024]{1,0:T(8,128)(2,1)S(1)}, bf16[384,1024]{1,0:T(8,128)(2,1)}, u32[]{:S(2)}) copy-start(bf16[384,1024]{1,0:T(8,128)(2,1)} %get-tuple-element.67) | copy-start | bytes 2359300
  189.7 5.0 %copy-start.18 = (bf16[384,2048]{1,0:T(8,128)(2,1)S(1)}, bf16[384,2048]{1,0:T(8,128)(2,1)}, u32[]{:S(2)}) copy-start(bf16[384,2048]{1,0:T(8,128)(2,1)} %get-tuple-element.72) | copy-start | bytes 4718596
  189.7 5.0 %copy-start.20 = (bf16[384,1024]{1,0:T(8,128)(2,1)S(1)}, bf16[384,1024]{1,0:T(8,128)(2,1)}, u32[]{:S(2)}) copy-start(bf16[384,1024]{1,0:T(8,128)(2,1)} %get-tuple-element.71) | copy-start | bytes 2359300
  194.7 4.4 %copy-start.17 = (bf16[384,2048]{1,0:T(8,128)(2,1)S(1)}, bf16[384,2048]{1,0:T(8,128)(2,1)}, u32[]{:S(2)}) copy-start(bf16[384,2048]{1,0:T(8,128)(2,1)} %get-tuple-element.73) | copy-start | bytes 4718596
  194.7 4.4 %copy-start.19 = (bf16[384,1024]{1,0:T(8,128)(2,1)S(1)}, bf16[384,1024]{1,0:T(8,128)(2,1)}, u32[]{:S(2)}) copy-start(bf16[384,1024]{1,0:T(8,128)(2,1)} %get-tuple-element.74) | copy-start | bytes 2359300
  (3 other events, 5.8 us)

commit v5 on v4

--- a/solution.py
+++ b/solution.py
@@ -740,42 +740,84 @@
     )(lens, slot_of, block_of, x, *shards, *vectors)
 
 
-def attend_back_kernel(heads, *refs):
+ORDERS = (
+    ("yxzZ", "zxyZ"),
+    ("xyzZ", "xzyZ"),
+    ("yxZz", "zxyZ"),
+)
+PIECES = len(ORDERS[0])
+KEYS = tuple((part, piece) for part in range(3) for piece in range(PIECES))
+
+
+def default_schedule():
+    early = [(part, piece) for piece in range(PIECES) for part in (1, 2)]
+    late = [(0, piece) for piece in range(PIECES)]
+    events = ["up", 0, "down", 1, 2] + early + ["back", "qkv", "rows"]
+    for step in range(6):
+        events += early + ["vec"] + late
+    return events + late
+
+
+def landing_shapes(order, shape):
+    shards, sides, shapes = 8, 2, []
+    for name in order:
+        if name == "x":
+            sides = 1
+        else:
+            shards //= 2
+        shapes.append((sides, shards, shape[2] // PIECES, shape[3]))
+    return shapes
+
+
+def dot_t(a, b):
+    return lax.dot_general(a, b, (((0,), (0,)), ((), ())), preferred_element_type=F32)
+
+
+def lanes_at(first, size):
+    return pl.ds(pl.multiple_of(first, 128), size)
+
+
+def backward_kernel(heads, *refs):
     lens_ref, slot_ref, block_ref, da_ref, kept_ref, lse_ref = refs[:6]
-    x_ref, a_ref, n_ref, g_ref, do_ref, du_ref, dm_ref = refs[6:13]
-    dq_ref, dk_ref, dv_ref = refs[13:16]
-    x_all, a_all, n_all, g_all, do_all, du_all, dm_all, dqkv_all = refs[16:24]
-    in_buf = refs[24 : 24 + MB]
-    out_buf, back_out, back_in = refs[24 + MB : 27 + MB]
-    q_s, k_s, v_s, a_s, dq_s, dk_s, dv_s = refs[27 + MB : 34 + MB]
-    send_sem, recv_sem, back_send, back_recv, mate_send, mate_recv, own_sem = refs[34 + MB :]
-    c, w = lax.axis_index("ctx"), lax.axis_index("wsh")
-    core = bit_of(c, 1)
-    mate = (flip(c, 1), w)
-    peers = plane_peers(c, w, heads)
-    blocks = heads
-    rows_own = da_ref.shape[0]
-    greet(peers)
-
-    place = pl.ds(pl.multiple_of(core * rows_own, rows_own), rows_own)
-    moves = []
-
-    def share(src, dst, lanes):
-        for first, size, to, per_core in lanes:
-            index = len(moves)
-            step = size if per_core else 0
-            own_from = pl.ds(pl.multiple_of(first + core * step, 128), size)
-            mate_from = pl.ds(pl.multiple_of(first + (1 - core) * step, 128), size)
-            spot = dst.at[place, pl.ds(to, size)]
-            own = pltpu.make_async_copy(src.at[:, own_from], spot, own_sem.at[index])
-            own.start()
-            gone = send(
-                src.at[:, mate_from], spot, mate_send.at[index], mate_recv.at[index], mate
-            )
-            moves.append((own, gone))
-
-    width = da_ref.shape[1]
-    hidden = g_ref.shape[1]
+    x_ref, a_ref, n_ref, g_ref, do_ref, du_ref, dm_ref, vec_ref, dh_ref = refs[6:15]
+    weights = refs[15:18]
+    rows_out, o_a, o_b, o_c, vec_out = refs[18:23]
+    refs = refs[23:]
+    in_buf = refs[:MB]
+    out_buf, back_out, back_in, q_s, k_s, v_s, a_s, dq_s, dk_s, dv_s = refs[MB : MB + 10]
+    refs = refs[MB + 10 :]
+    dq_ref, dk_ref, dv_ref, m_x, m_a, m_n, m_dm, m_do, m_du, m_g, m_dqkv = refs[:11]
+    near, (vec_s, v_recv, v_sum, s_a, s_b, s_c) = refs[11:14], refs[14:20]
+    refs = refs[20:]
+    r_bufs = {key: refs[4 * i : 4 * i + 4] for i, key in enumerate(KEYS)}
+    (
+        send_sem,
+        recv_sem,
+        back_send,
+        back_recv,
+        mate_send,
+        mate_recv,
+        near_sem,
+        rs_send,
+        rs_recv,
+        ag_send,
+        ag_recv,
+        own_sem,
+        v_send_sem,
+        v_recv_sem,
+    ) = refs[4 * len(KEYS) :]
+    c, x = lax.axis_index("ctx"), lax.axis_index("wsh")
+    core, y, z, zz = bit_of(c, 1), bit_of(c, 2), bit_of(c, 4), bit_of(c, 8)
+    by_core = (flip(c, 1), x)
+    by = {"x": (c, 1 - x), "y": (flip(c, 2), x), "z": (flip(c, 4), x), "Z": (flip(c, 8), x)}
+    bits = {"y": y, "z": z, "Z": zz}
+    peers = plane_peers(c, x, heads)
+    blocks, span = heads, BPS * BLK
+    width, hidden = da_ref.shape[1], g_ref.shape[1]
+    for index, weight in enumerate(weights):
+        pltpu.make_async_copy(weight, near[index], near_sem.at[index]).start()
+    greet(peers + [by["x"]])
+
     for m in range(MB):
         row = slice(m * BLK, (m + 1) * BLK)
         for pair in range(heads // 2):
@@ -785,12 +827,65 @@
         for peer in peers:
             send(out_buf.at[m, peer[0]], in_buf[m].at[c], send_sem.at[m], recv_sem.at[m], peer)
         in_buf[m][c] = out_buf[m, c]
-    for src, dst in ((x_ref, x_all), (a_ref, a_all), (n_ref, n_all), (dm_ref, dm_all)):
-        share(src, dst, ((0, width, 0, False),))
-    share(do_ref, do_all, ((0, width // 2, 0, True),))
-    share(du_ref, du_all, ((0, hidden // 2, 0, True),))
-    share(g_ref, g_all, ((0, hidden // 4, 0, True), (hidden // 2, hidden // 4, hidden // 4, True)))
-    for m in range(MB):
+
+    shared = {}
+
+    def share(name, src, dst):
+        index = len(shared)
+        shared[name] = send(src, dst, mate_send.at[index], mate_recv.at[index], by_core)
+
+    other = 1 - core
+    share("n", n_ref, m_n)
+    share("du", du_ref.at[:, lanes_at(other * (hidden // 2), hidden // 2)], m_du)
+    for half in range(2):
+        share(
+            "g" + str(half),
+            g_ref.at[:, lanes_at(half * (hidden // 2) + other * (hidden // 4), hidden // 4)],
+            m_g.at[:, pl.ds(half * (hidden // 4), hidden // 4)],
+        )
+    share("dm", dm_ref, m_dm)
+    share("a", a_ref, m_a)
+    share("do", do_ref.at[:, lanes_at(other * (width // 2), width // 2)], m_do)
+    share("x", x_ref, m_x)
+
+    sums, outs = (s_a, s_b, s_c), (o_a, o_b, o_c)
+    wide = 256
+
+    def tile(pairs, out, first, count):
+        def body(turn, carry):
+            at = turn * wide
+            total = sum(dot_t(lhs[...], rhs[:, lanes_at(col + at, wide)]) for lhs, rhs, col in pairs)
+            cols = lanes_at(first + at, wide)
+            out[..., cols] = total.astype(BF16).reshape(out.shape[:-1] + (wide,))
+            return carry
+
+        lax.fori_loop(0, count, body, 0)
+
+    def grads_up():
+        shared["n"].wait_recv()
+        shared["du"].wait_recv()
+        half = hidden // 2
+        tile(((n_ref, du_ref, core * half), (m_n, m_du, 0)), s_b, 0, half // wide)
+
+    def grads_down():
+        for name in ("g0", "g1", "dm"):
+            shared[name].wait_recv()
+        quarter = hidden // 4
+        for half in range(2):
+            mine = g_ref.at[:, lanes_at(half * 2 * quarter + core * quarter, quarter)]
+            others = m_g.at[:, pl.ds(half * quarter, quarter)]
+            tile(((mine, dm_ref, 0), (others, m_dm, 0)), s_c.at[half], 0, width // wide)
+
+    def grads_qkv():
+        half = width // 2
+        for name in ("a", "do", "x", "dq", "dk", "dv"):
+            shared[name].wait_recv()
+        tile(((a_ref, do_ref, core * half), (m_a, m_do, 0)), s_a, 3 * half, half // wide)
+        for index, ref in enumerate((dq_ref, dk_ref, dv_ref)):
+            pairs = ((x_ref, ref, core * half), (m_x, m_dqkv, index * half))
+            tile(pairs, s_a, index * half, half // wide)
+
+    def attention(m):
         all_bytes(in_buf[m], recv_sem.at[m], heads - 1).wait()
         for b in range(blocks):
             slot = slot_ref[0, m, b]
@@ -800,7 +895,6 @@
             k_s[rows, :] = got[:BLK, HD:]
             v_s[rows, :] = unpack_fold(got[BLK:])
             a_s[rows, :] = unpack_fold(in_buf[m][slot])
-        span = BPS * BLK
 
         def one_sequence(s, carry):
             rows = pl.ds(pl.multiple_of(s * span, span), span)
@@ -815,13 +909,11 @@
             both = probs * dp
             delta = jnp.sum(both, axis=0, keepdims=True)
             ds = (both - probs * delta).astype(BF16)
-            here = pl.ds(s * BPS, BPS)
-            split = (BPS, BLK, HD)
+            here, split = pl.ds(s * BPS, BPS), (BPS, BLK, HD)
             dv = jnp.dot(probs.astype(BF16), dd, preferred_element_type=F32)
             dv_s[here] = dv.reshape(split)
             dk_s[here] = (jnp.dot(ds, qq, preferred_element_type=F32) * scale).reshape(split)
-            dq_t = lax.dot_general(kk, ds, (((0,), (0,)), ((), ())), preferred_element_type=F32)
-            dq_s[here] = (dq_t.T * scale).reshape(split)
+            dq_s[here] = (dot_t(kk, ds).T * scale).reshape(split)
             return carry
 
         lax.fori_loop(0, blocks // BPS, one_sequence, 0)
@@ -834,185 +926,99 @@
                 back_out.at[m, peer[0]], back_in.at[m, c], back_send.at[m], back_recv.at[m], peer
             )
         back_in[m, c] = back_out[m, c]
-    for m in range(MB):
-        all_bytes(back_in.at[m], back_recv.at[m], heads - 1).wait()
-        row = slice(m * BLK, (m + 1) * BLK)
-        for pair in range(heads // 2):
-            lanes = slice(pair * 128, (pair + 1) * 128)
-            one, two = back_in[m, 2 * pair], back_in[m, 2 * pair + 1]
-            dq_ref[row, lanes] = jnp.concatenate([one[:BLK, :HD], two[:BLK, :HD]], axis=1)
-            dk_ref[row, lanes] = jnp.concatenate([one[:BLK, HD:], two[:BLK, HD:]], axis=1)
-            dv_ref[row, lanes] = jnp.concatenate(
-                [unpack_fold(one[BLK:]), unpack_fold(two[BLK:])], axis=1
-            )
-    for index, ref in enumerate((dq_ref, dk_ref, dv_ref)):
+
+    vec_peers = (by["x"], by["y"], by["z"], by["Z"], by_core)
+    vec_steps = []
+
+    def vec_send(src):
+        step = len(vec_steps)
+        vec_steps.append(
+            send(
+                src, v_recv.at[step], v_send_sem.at[step], v_recv_sem.at[step], vec_peers[step]
+            )
+        )
+
+    def vec_next():
+        step = len(vec_steps) - 1
+        vec_steps[step].wait_recv()
+        before = vec_s[x] if step == 0 else v_sum[step - 1]
+        v_sum[step] = before + v_recv[step]
+        if step + 1 < len(vec_peers):
+            vec_send(v_sum.at[step])
+
+    def come_back():
+        for m in range(MB):
+            all_bytes(back_in.at[m], back_recv.at[m], heads - 1).wait()
+            row = slice(m * BLK, (m + 1) * BLK)
+            for pair in range(heads // 2):
+                lanes = slice(pair * 128, (pair + 1) * 128)
+                one, two = back_in[m, 2 * pair], back_in[m, 2 * pair + 1]
+                dq_ref[row, lanes] = jnp.concatenate([one[:BLK, :HD], two[:BLK, :HD]], axis=1)
+                dk_ref[row, lanes] = jnp.concatenate([one[:BLK, HD:], two[:BLK, HD:]], axis=1)
+                dv_ref[row, lanes] = jnp.concatenate(
+                    [unpack_fold(one[BLK:]), unpack_fold(two[BLK:])], axis=1
+                )
         half = width // 2
-        spot = dqkv_all.at[place, pl.ds(index * half, half)]
-        number = len(moves)
-        own_from = pl.ds(pl.multiple_of(core * half, 128), half)
-        mate_from = pl.ds(pl.multiple_of((1 - core) * half, 128), half)
-        own = pltpu.make_async_copy(ref.at[:, own_from], spot, own_sem.at[number])
-        own.start()
-        gone = send(ref.at[:, mate_from], spot, mate_send.at[number], mate_recv.at[number], mate)
-        moves.append((own, gone))
-    for m in range(MB):
-        all_bytes(out_buf.at[m], send_sem.at[m], heads - 1).wait()
-        all_bytes(back_out.at[m], back_send.at[m], heads - 1).wait()
-    for own, gone in moves:
-        own.wait()
-        gone.wait()
-
-
-def attend_back(lens, slot_of, block_of, da, kept, lse, x, a, n1, g, do, du, dm, heads):
-    vmem, smem = pl.BlockSpec(memory_space=pltpu.VMEM), pl.BlockSpec(memory_space=pltpu.SMEM)
-    anywhere = pl.BlockSpec(memory_space=pl.ANY)
-    rows, width = da.shape
-    hidden = g.shape[1]
-    pack_rows = BLK + BLK // 2
-    both = 2 * rows
-    moves = 11
-    shape = lambda *dims: jax.ShapeDtypeStruct(dims, BF16)
-    return pl.pallas_call(
-        functools.partial(attend_back_kernel, heads),
-        out_shape=[shape(rows, width)] * 3
-        + [
-            shape(both, width),
-            shape(both, width),
-            shape(both, width),
-            shape(both, hidden // 2),
-            shape(both, width // 2),
-            shape(both, hidden // 2),
-            shape(both, width),
-            shape(both, 3 * width // 2),
-        ],
-        in_specs=[smem] * 3 + [vmem] * 10,
-        out_specs=[vmem] * 3 + [anywhere] * 8,
-        scratch_shapes=[pltpu.VMEM((heads, BLK // 2, 128), BF16)] * MB
-        + [
-            pltpu.VMEM((MB, heads, BLK // 2, 128), BF16),
-            pltpu.VMEM((MB, heads, pack_rows, 128), BF16),
-            pltpu.VMEM((MB, heads, pack_rows, 128), BF16),
-        ]
-        + [pltpu.VMEM((heads * BLK, HD), BF16)] * 4
-        + [pltpu.VMEM((heads, BLK, HD), F32)] * 3
-        + [pltpu.SemaphoreType.DMA((MB,))] * 4
-        + [pltpu.SemaphoreType.DMA((moves,))] * 3,
-        compiler_params=pltpu.CompilerParams(
-            collective_id=2, has_side_effects=True, vmem_limit_bytes=VMEM_BYTES
-        ),
-        name="attend_back",
-    )(lens, slot_of, block_of, da, kept, lse, x, a, n1, g, do, du, dm)
-
-
-CHUNKS = 2
-ORDERS = {
-    (0, 0): "xyzZ",
-    (0, 1): "xzyZ",
-    (1, 0): "yxZz",
-    (1, 1): "yZxz",
-    (2, 0): "zxyZ",
-    (2, 1): "Zyxz",
-}
-
-
-def landing_shapes(order, shape):
-    shards, sides, shapes = 8, 2, []
-    for name in order:
-        if name == "x":
-            sides = 1
-        else:
-            shards //= 2
-        shapes.append((sides, shards, shape[2] // CHUNKS, shape[3]))
-    return shapes
-
-
-def reduce_kernel(ga1_ref, ga2_ref, gb_ref, gc_ref, vec_ref, *refs):
-    o_a, o_b, o_c, vec_out = refs[:4]
-    s_a, s_b, s_c = refs[4:7]
-    r_bufs = {key: refs[7 + 4 * i : 11 + 4 * i] for i, key in enumerate(ORDERS)}
-    rest = refs[7 + 4 * len(ORDERS) :]
-    v_recv, v_sum = rest[:2]
-    load_sem, rs_send, rs_recv, ag_send, ag_recv, v_send_sem, v_recv_sem, own_sem = rest[2:]
-    c, x = lax.axis_index("ctx"), lax.axis_index("wsh")
-    core, y, z, zz = bit_of(c, 1), bit_of(c, 2), bit_of(c, 4), bit_of(c, 8)
-    by_x, by_y, by_z = (c, 1 - x), (flip(c, 2), x), (flip(c, 4), x)
-    by_zz, by_core = (flip(c, 8), x), (flip(c, 1), x)
-    shards = 8
-    lanes1 = ga1_ref.shape[3]
-    lanes2 = ga2_ref.shape[3]
-    loads = [
-        pltpu.make_async_copy(ga1_ref, s_a.at[:, :, :, pl.ds(0, lanes1)], load_sem.at[0]),
-        pltpu.make_async_copy(ga2_ref, s_a.at[:, :, :, pl.ds(lanes1, lanes2)], load_sem.at[1]),
-        pltpu.make_async_copy(gb_ref, s_b, load_sem.at[2]),
-        pltpu.make_async_copy(gc_ref, s_c, load_sem.at[3]),
-    ]
-    for load in loads:
-        load.start()
-    greet((by_x, by_y, by_z, by_zz, by_core))
-    vec_steps = [
-        send(vec_ref.at[1 - x], v_recv.at[0], v_send_sem.at[0], v_recv_sem.at[0], by_x)
-    ]
-
-    def vec_next(step, peer):
-        vec_steps[step].wait_recv()
-        before = vec_ref[x] if step == 0 else v_sum[step - 1]
-        v_sum[step] = before + v_recv[step]
-        if peer is not None:
-            vec_steps.append(
-                send(
-                    v_sum.at[step],
-                    v_recv.at[step + 1],
-                    v_send_sem.at[step + 1],
-                    v_recv_sem.at[step + 1],
-                    peer,
-                )
-            )
-
-    for load in loads:
-        load.wait()
-    bits = {"y": y, "z": z, "Z": zz}
-    peers = {"x": by_x, "y": by_y, "z": by_z, "Z": by_zz}
+        for index, (name, ref) in enumerate((("dq", dq_ref), ("dk", dk_ref), ("dv", dv_ref))):
+            share(
+                name,
+                ref.at[:, lanes_at(other * half, half)],
+                m_dqkv.at[:, pl.ds(index * half, half)],
+            )
+        vec_s[...] = vec_ref[...]
+        lanes = vec_s.shape[2]
+        for index, ref in enumerate((dq_ref, dv_ref)):
+            total = jnp.sum(ref[...].astype(F32), axis=0, keepdims=True)
+            for side in range(2):
+                vec_s[side, index : index + 1, :] = total[:, side * lanes : (side + 1) * lanes]
+        vec_send(vec_s.at[1 - x])
+
+    def grad_rows():
+        total = dh_ref[...]
+        for index, ref in enumerate((dq_ref, dk_ref, dv_ref)):
+            pltpu.make_async_copy(weights[index], near[index], near_sem.at[index]).wait()
+            total = total + lax.dot_general(
+                ref[...], near[index][...], (((1,), (1,)), ((), ())), preferred_element_type=F32
+            )
+        rows_out[...] = total.astype(BF16)
+
     plans, gathers = {}, {}
-    for key, order in ORDERS.items():
+    for key in KEYS:
         first, count, sided = 0, 8, False
         plans[key], back = [], []
-        for name in order:
+        for name in ORDERS[key[0]][key[1]]:
             if name == "x":
-                plans[key].append((by_x, 1 - x, x, first, first, count))
+                plans[key].append((by["x"], 1 - x, x, first, first, count))
                 sided = True
                 continue
             count //= 2
             out, keep = first + (1 - bits[name]) * count, first + bits[name] * count
             side = x if sided else None
-            plans[key].append((peers[name], side, side, out, keep, count))
-            back.append((peers[name], keep, out, count))
+            plans[key].append((by[name], side, side, out, keep, count))
+            back.append((by[name], keep, out, count))
             first = keep
         gathers[key] = back[::-1]
-    sums = (s_a, s_b, s_c)
-    outs = (o_a, o_b, o_c)
-    flights = {}
-
-    def chunk_rows(part, chunk):
-        rows = sums[part].shape[2] // CHUNKS
-        return pl.ds(chunk * rows, rows)
-
-    def reduce_send(part, step, chunk):
-        peer, side, _, first, _, count = plans[part, chunk][step]
-        rows = chunk_rows(part, chunk)
-        dst = r_bufs[part, chunk][step]
+    flights, spread, owns, state = {}, {}, {}, {}
+
+    def piece_rows(key):
+        rows = sums[key[0]].shape[2] // PIECES
+        return pl.ds(key[1] * rows, rows)
+
+    def reduce_send(key, step):
+        peer, side, _, first, _, count = plans[key][step]
+        dst = r_bufs[key][step]
         if side is None:
-            src = sums[part].at[:, pl.ds(first, count), rows]
+            src = sums[key[0]].at[:, pl.ds(first, count), piece_rows(key)]
         else:
-            src, dst = sums[part].at[side, pl.ds(first, count), rows], dst.at[0]
-        flights[part, step, chunk] = send(
-            src, dst, rs_send.at[part, step, chunk], rs_recv.at[part, step, chunk], peer
-        )
-
-    def reduce_add(part, step, chunk):
-        _, _, side, _, first, count = plans[part, chunk][step]
-        rows = chunk_rows(part, chunk)
-        flights[part, step, chunk].wait_recv()
-        total, fresh = sums[part], r_bufs[part, chunk][step]
+            src, dst = sums[key[0]].at[side, pl.ds(first, count), piece_rows(key)], dst.at[0]
+        sems = rs_send.at[key[0], key[1], step], rs_recv.at[key[0], key[1], step]
+        flights[key, step] = send(src, dst, *sems, peer)
+        state[key] = step
+
+    def reduce_add(key, step):
+        _, _, side, _, first, count = plans[key][step]
+        flights[key, step].wait_recv()
+        total, fresh, rows = sums[key[0]], r_bufs[key][step], piece_rows(key)
         sides = ((0, 0), (1, 1)) if side is None else ((side, 0),)
         for here, there in sides:
 
@@ -1025,95 +1031,125 @@
 
             lax.fori_loop(0, count, body, 0)
 
-    for chunk in range(CHUNKS):
-        for part in range(3):
-            reduce_send(part, 0, chunk)
-    vec_peers = (by_y, by_z, by_zz, by_core, None)
-    for step in range(1, 4):
-        vec_next(step - 1, vec_peers[step - 1])
-        for chunk in range(CHUNKS):
-            for part in range(3):
-                reduce_add(part, step - 1, chunk)
-                reduce_send(part, step, chunk)
-    owns, spread = [], {}
-    vec_next(3, by_core)
-    for chunk in range(CHUNKS):
-        for part in range(3):
-            reduce_add(part, 3, chunk)
-            rows = chunk_rows(part, chunk)
-            peer, first, _, _ = gathers[part, chunk][0]
-            src = sums[part].at[x, pl.ds(first, 1), rows]
-            dst = outs[part].at[core, pl.ds(first, 1), rows]
-            own = pltpu.make_async_copy(src, dst, own_sem.at[part, chunk])
-            own.start()
-            owns.append(own)
-            sem = lambda kind: (ag_send.at[part, kind, chunk], ag_recv.at[part, kind, chunk])
-            spread[part, 0, chunk] = send(src, dst, *sem(0), peer)
-            spread[part, 3, chunk] = send(src, dst, *sem(3), by_core)
-    vec_next(4, None)
-    vec_out[...] = v_sum[4]
-    for own in owns:
-        own.wait()
-    for step in range(1, 4):
-        for chunk in range(CHUNKS):
-            for part in range(3):
-                rows = chunk_rows(part, chunk)
-                spread[part, step - 1, chunk].wait_recv()
-                sem = lambda kind: (ag_send.at[part, kind, chunk], ag_recv.at[part, kind, chunk])
-                if step < 3:
-                    peer, first, _, count = gathers[part, chunk][step]
-                    ref = outs[part].at[core, pl.ds(first, count), rows]
-                    spread[part, step, chunk] = send(ref, ref, *sem(step), peer)
-                _, _, first, count = gathers[part, chunk][step - 1]
-                fresh = outs[part].at[core, pl.ds(first, count), rows]
-                spread[part, 3 + step, chunk] = send(fresh, fresh, *sem(3 + step), by_core)
-    for key, flight in spread.items():
-        if key[1] >= 3:
-            flight.wait_recv()
+    def spread_send(key, kind, src, dst, peer):
+        sems = ag_send.at[key[0], key[1], kind], ag_recv.at[key[0], key[1], kind]
+        spread[key, kind] = send(src, dst, *sems, peer)
+
+    def advance(key):
+        step = state[key]
+        out, rows = outs[key[0]], piece_rows(key)
+        if step < 4:
+            reduce_add(key, step)
+            if step < 3:
+                reduce_send(key, step + 1)
+                return
+            peer, first, _, _ = gathers[key][0]
+            src = sums[key[0]].at[x, pl.ds(first, 1), rows]
+            dst = out.at[core, pl.ds(first, 1), rows]
+            owns[key] = pltpu.make_async_copy(src, dst, own_sem.at[key[0], key[1]])
+            owns[key].start()
+            spread_send(key, 0, src, dst, peer)
+            spread_send(key, 3, src, dst, by_core)
+        else:
+            turn = step - 3
+            spread[key, turn - 1].wait_recv()
+            if turn == 1:
+                owns[key].wait()
+            if turn < 3:
+                peer, first, _, count = gathers[key][turn]
+                ref = out.at[core, pl.ds(first, count), rows]
+                spread_send(key, turn, ref, ref, peer)
+            _, _, first, count = gathers[key][turn - 1]
+            ref = out.at[core, pl.ds(first, count), rows]
+            spread_send(key, 3 + turn, ref, ref, by_core)
+        state[key] = step + 1
+
+    actions = {
+        "up": (grads_up, 1),
+        "down": (grads_down, 2),
+        "qkv": (grads_qkv, 0),
+        "back": (come_back, None),
+        "rows": (grad_rows, None),
+        "vec": (vec_next, None),
+    }
+    for event in SCHEDULE:
+        if isinstance(event, tuple):
+            advance(event)
+        elif isinstance(event, int):
+            attention(event)
+        else:
+            action, part = actions[event]
+            if event == "vec" and len(vec_steps) == len(vec_peers) and "vec" in state:
+                continue
+            if event == "vec" and len(vec_steps) == len(vec_peers):
+                state["vec"] = True
+            action()
+            if part is not None:
+                for piece in range(PIECES):
+                    reduce_send((part, piece), 0)
+    vec_out[...] = v_sum[len(vec_peers) - 1]
+    for m in range(MB):
+        all_bytes(out_buf.at[m], send_sem.at[m], heads - 1).wait()
+        all_bytes(back_out.at[m], back_send.at[m], heads - 1).wait()
+    for flight in shared.values():
+        flight.wait_send()
+    for flight in vec_steps:
         flight.wait_send()
     for flight in flights.values():
         flight.wait_send()
-    for flight in vec_steps:
+    for (_, kind), flight in spread.items():
+        if kind >= 3:
+            flight.wait_recv()
         flight.wait_send()
 
 
-def reduce_grads(ga1, ga2, gb, gc, vec):
-    vmem, anywhere = pl.BlockSpec(memory_space=pltpu.VMEM), pl.BlockSpec(memory_space=pl.ANY)
-    lanes = ga1.shape[3] + ga2.shape[3]
-    a_shape = ga1.shape[:3] + (lanes,)
-    b_shape, c_shape = gb.shape, gc.shape
-    scratch = [pltpu.VMEM(s, BF16) for s in (a_shape, b_shape, c_shape)]
-    shapes = (a_shape, b_shape, c_shape)
-    for (part, _), order in ORDERS.items():
-        scratch += [pltpu.VMEM(shape, BF16) for shape in landing_shapes(order, shapes[part])]
-    scratch += [
-        pltpu.VMEM((5,) + vec.shape[1:], F32),
-        pltpu.VMEM((5,) + vec.shape[1:], F32),
-        pltpu.SemaphoreType.DMA((4,)),
-        pltpu.SemaphoreType.DMA((3, 4, CHUNKS)),
-        pltpu.SemaphoreType.DMA((3, 4, CHUNKS)),
-        pltpu.SemaphoreType.DMA((3, 7, CHUNKS)),
-        pltpu.SemaphoreType.DMA((3, 7, CHUNKS)),
-        pltpu.SemaphoreType.DMA((5,)),
-        pltpu.SemaphoreType.DMA((5,)),
-        pltpu.SemaphoreType.DMA((3, CHUNKS)),
-    ]
+SCHEDULE = default_schedule()
+
+
+def backward(lens, slot_of, block_of, da, kept, lse, x, a, n1, g, do, du, dm, vec, dh, weights, heads):
+    vmem, smem = pl.BlockSpec(memory_space=pltpu.VMEM), pl.BlockSpec(memory_space=pltpu.SMEM)
+    anywhere = pl.BlockSpec(memory_space=pl.ANY)
+    rows, width = da.shape
+    hidden = g.shape[1]
+    pack_rows = BLK + BLK // 2
+    low = lambda *dims: pltpu.VMEM(dims, BF16)
+    a_shape, b_shape = (2, 8, width // 16, 2 * width), (2, 8, width // 16, hidden // 2)
+    c_shape = (2, 8, hidden // 32, width)
+    scratch = [low(heads, BLK // 2, 128)] * MB
+    scratch += [low(MB, heads, BLK // 2, 128)]
+    scratch += [low(MB, heads, pack_rows, 128)] * 2
+    scratch += [low(heads * BLK, HD)] * 4
+    scratch += [pltpu.VMEM((heads, BLK, HD), F32)] * 3
+    scratch += [low(rows, width)] * 7
+    scratch += [low(rows, width // 2), low(rows, hidden // 2), low(rows, hidden // 2)]
+    scratch += [low(rows, 3 * width // 2)]
+    scratch += [low(*item.shape) for item in weights]
+    scratch += [pltpu.VMEM(vec.shape, F32)] + [pltpu.VMEM((5,) + vec.shape[1:], F32)] * 2
+    scratch += [low(*shape) for shape in (a_shape, b_shape, c_shape)]
+    for key in KEYS:
+        shape = (a_shape, b_shape, c_shape)[key[0]]
+        scratch += [low(*item) for item in landing_shapes(ORDERS[key[0]][key[1]], shape)]
+    sems = lambda *dims: pltpu.SemaphoreType.DMA(dims)
+    scratch += [sems(MB)] * 4 + [sems(11)] * 2 + [sems(3)]
+    scratch += [sems(3, PIECES, 4)] * 2 + [sems(3, PIECES, 7)] * 2 + [sems(3, PIECES)]
+    scratch += [sems(5)] * 2
     return pl.pallas_call(
-        reduce_kernel,
+        functools.partial(backward_kernel, heads),
         out_shape=[
+            jax.ShapeDtypeStruct((rows, width), BF16),
             jax.ShapeDtypeStruct(a_shape, BF16),
             jax.ShapeDtypeStruct(b_shape, BF16),
             jax.ShapeDtypeStruct(c_shape, BF16),
             jax.ShapeDtypeStruct(vec.shape[1:], F32),
         ],
-        in_specs=[anywhere] * 4 + [vmem],
-        out_specs=[anywhere] * 3 + [vmem],
+        in_specs=[smem] * 3 + [vmem] * 12 + [anywhere] * 3,
+        out_specs=[vmem] + [anywhere] * 3 + [vmem],
         scratch_shapes=scratch,
         compiler_params=pltpu.CompilerParams(
-            collective_id=3, has_side_effects=True, vmem_limit_bytes=VMEM_BYTES
+            collective_id=2, has_side_effects=True, vmem_limit_bytes=VMEM_BYTES
         ),
-        name="reduce_grads",
-    )(ga1, ga2, gb, gc, vec)
+        name="backward",
+    )(lens, slot_of, block_of, da, kept, lse, x, a, n1, g, do, du, dm, vec, dh, *weights)
 
 
 def widen_kernel(a_ref, b_ref, c_ref, *outs):
@@ -1210,31 +1246,31 @@
     do = dh_one.astype(BF16)
     da = dot(do, out_w, COL_COL).astype(BF16)
 
-    dq, dk, dv, x_all, a_all, n_all, g_all, do_all, du_all, dm_all, dqkv_all = attend_back(
-        lens, slot_of, block_of, da, kept, lse, x, a, n_low, g, do, du, dm, HEADS
+    total = lambda item: jnp.sum(item.astype(F32), axis=0).reshape(2, -1, small_whole.shape[2])
+    nothing = jnp.zeros((2, 2, small_whole.shape[2]), F32)
+    vec = [nothing] + [
+        total(item)
+        for item in (do, du, dm, dn * unit_one, dn, cot * unit_two, cot)
+    ]
+    grad_tokens, o_a, o_b, o_c, vec_sum = backward(
+        lens,
+        slot_of,
+        block_of,
+        da,
+        kept,
+        lse,
+        x,
+        a,
+        n_low,
+        g,
+        do,
+        du,
+        dm,
+        jnp.concatenate(vec, axis=1),
+        dh_one,
+        (query_w, key_w, value_w),
+        HEADS,
     )
-    total = lambda item: jnp.sum(item.astype(F32), axis=0)
-    vec = [
-        total(dq),
-        total(dv),
-        total(do),
-        total(du),
-        total(dm),
-        total(dn * unit_one),
-        total(dn),
-        total(cot * unit_two),
-        total(cot),
-    ]
-    vec = jnp.concatenate([item.reshape(2, -1) for item in vec], axis=1).reshape(2, -1, 128)
-    ga1 = dot(x_all, dqkv_all, ROW_ROW).astype(BF16).reshape(2, 8, -1, dqkv_all.shape[1])
-    ga2 = dot(a_all, do_all, ROW_ROW).astype(BF16).reshape(2, 8, -1, do_all.shape[1])
-    gb = dot(n_all, du_all, ROW_ROW).astype(BF16).reshape(2, 8, -1, du_all.shape[1])
-    gc = dot(g_all, dm_all, ROW_ROW).astype(BF16).reshape(2, 8, -1, dm_all.shape[1])
-    o_a, o_b, o_c, vec_sum = reduce_grads(ga1, ga2, gb, gc, vec)
-    grad_rows = (
-        dh_one + dot(dq, query_w, COL_COL) + dot(dk, key_w, COL_COL) + dot(dv, value_w, COL_COL)
-    )
-    grad_tokens = grad_rows.astype(BF16)
     *square, up, down = widen(o_a, o_b, o_c)
     down = down.reshape(-1, width)
     vec_sum = vec_sum.reshape(-1)

time: 404 us -> 363 us (0.90)
  matrix products: 48.5 us -> 21.6 us
  Pallas kernels: 331 us -> 323 us
    dot_general x13 -> x6, matrix products: 48.5 us -> 21.6 us  [dot(): return lax.dot_general(a, b, (dims, ((), ())), preferred_element_type=F32)]
    pallas_call x2 -> x1, Pallas kernels: 224 us -> 217 us  [backward(): pl.pallas_call(functools.partial(backward_kernel, heads), out_shape=[jax....]
where the time goes in v5:
time: 363 us
  Pallas kernels  323 us (89%)
  matrix products  21.6 us (6%)
  local copies, waits for them, and re-layouts  10.7 us (3%)
  other arithmetic  5.85 us (2%)
    pallas_call x1, Pallas kernels, backward(): pl.pallas_call(functools.partial(backward_kernel, heads), out_shape=[jax....  217 us
    pallas_call x1, Pallas kernels, forward(): pl.pallas_call(functools.partial(forward_kernel, heads, plan, count, len(...  92.6 us
    dot_general x6, matrix products, dot(): return lax.dot_general(a, b, (dims, ((), ())), preferred_element_type=F32)  21.6 us
    pallas_call x1, Pallas kernels, widen(): pl.pallas_call(widen_kernel, grid=(shards,), out_shape=[jax.ShapeDtypeStr...  13.9 us

profile of v5, /device:TPU:0, one launch (start us, length us, event | category | flops | bytes accessed | tf_op | source)
XLA Modules:
  0.0 362.6 jit_solution(15762511702051799782)
XLA Ops:
  0.7 1.3 copy.41.refs_0_
  2.0 1.3 copy.43.refs_2_
  3.2 0.8 copy.40
  4.0 1.4 sort.17
  5.4 0.7 copy.42.refs_1_
  6.1 92.6 %forward.1 = (bf16[1024,1024]{1,0:T(8,128)(2,1)}, bf16[1024,1024]{1,0:T(8,128)(2,1)}, bf16[1024,1024]{1,0:T(8,128)(2,1)}, bf16[1024,1024]{1,0:T(8,128)(2,1)}, bf...) custom-call(s32[1,3,2]{2,1,0:T(4,128)} %copy.41.refs_0_, ...), custom_call_target="tpu_custom_call" | custom-call | tf_op jit(solution)/shard_map/forward/pallas_call | solution.py:704
  98.7 0.8 slice_bitcast_fusion
  99.5 1.0 fusion.10
  100.8 2.4 fusion.12
  103.7 5.8 %fusion.4 = (f32[192,4096]{1,0:T(8,128)S(1)}, bf16[192,4096]{1,0:T(8,128)(2,1)S(1)}) fusion(f32[4096]{0:T(1024)S(1)} %bitcast.74, bf16[192,1024]{1,0:T(8,128)(2,1)S(1)} %fusion.9.refs_8_, bf16[1024,4096]{1,0:T(8,128)(2,1)} %get-tuple-element.45), kind=kOutput, calls=%fused_computation.7 | convolution fusion | flops 1619263488 | bytes 13516800 | tf_op jit(solution)/shard_map/dot_general | solution.py:1204
  109.6 2.0 fusion.13
  112.3 1.1 convert_reduce_fusion.2
  113.4 2.9 fusion.refs_11_
  116.3 6.9 %fusion.14 = f32[192,1024]{1,0:T(8,128)S(1)} fusion(bf16[192,4096]{1,0:T(8,128)(2,1)S(1)} %fusion.refs_11_, bf16[1024,4096]{1,0:T(8,128)(2,1)} %get-tuple-element.45), kind=kOutput, calls=%fused_computation.51 | convolution fusion | flops 1610612736 | bytes 10747904 | tf_op jit(solution)/shard_map/dot_general | solution.py:1204
  123.2 0.5 multiply_reduce_fusion
  123.8 1.2 convert_reduce_fusion.3
  124.9 1.6 convolution_convert_fusion.refs_3_
  126.8 1.3 concatenate.3.refs_13_
  128.1 217.1 %backward.1 = (bf16[192,1024]{1,0:T(8,128)(2,1)}, bf16[2,8,64,2048]{3,2,1,0:T(8,128)(2,1)}, bf16[2,8,64,2048]{3,2,1,0:T(8,128)(2,1)}, bf16[2,8,128,1024]{3,2,1,0:T(8,128)(2,1)}, f32[12,512]{1,0:T(8,128)}) custom-call(s32[1,3,2]{2,1,0:T(4,128)} %copy.41.refs_0_, s32[1,3,16]{2,1,0:T(4,128)} %copy.42.refs_1_, s32[1,3,16]{2,1,0:T(4,128)} %copy.43.refs_2_, ...), custom_call_target="tpu_custom_call" | custom-call | tf_op jit(solution)/shard_map/backward/pallas_call | solution.py:1136
  345.2 0.7 slice_bitcast_fusion.1
  345.9 1.5 fusion.11
  347.4 0.6 copy.48
  348.0 13.9 %widen.1 = (f32[512,1024]{1,0:T(8,128)}, f32[512,1024]{1,0:T(8,128)}, f32[512,1024]{1,0:T(8,128)}, f32[512,1024]{1,0:T(8,128)}, f32[512,4096]{1,0:T(8,128)}, /*index=5*/f32[2,8,128,1024]{3,2,1,0:T(8,128)}) custom-call(bf16[2,8,64,2048]{3,2,1,0:T(8,128)(2,1)} %get-tuple-element.55.a_ref, bf16[2,8,64,2048]{3,2,1,0:T(8,128)(2,1)} %get-tuple-element.56.b_ref, ...), custom_call_target="tpu_custom_call" | custom-call | tf_op jit(solution)/shard_map/widen/pallas_call | solution.py:1175
  361.9 0.7 copy.50
  (42 shorter events, 1.8 us)
Async XLA Ops:
  6.1 94.3 %copy-start.2 = (bf16[1,3,64,1024]{3,2,1,0:T(8,128)(2,1)S(1)}, bf16[1,3,64,1024]{3,2,1,0:T(8,128)(2,1)}, u32[]{:S(2)}) copy-start(bf16[1,3,64,1024]{3,2,1,0:T(8,128)(2,1)} %param.20) | copy-start | bytes 1179652
  6.1 94.7 %copy-start.3 = (bf16[1,3,64,1024]{3,2,1,0:T(8,128)(2,1)S(1)}, bf16[1,3,64,1024]{3,2,1,0:T(8,128)(2,1)}, u32[]{:S(2)}) copy-start(bf16[1,3,64,1024]{3,2,1,0:T(8,128)(2,1)} %param.19) | copy-start | bytes 1179652
  103.5 6.1 %slice-start = ((s8[8388608]{0:T(1024)(128)(4,1)}), s8[4194304]{0:T(1024)(128)(4,1)S(1)}, s32[]{:S(2)}) async-start(s8[8388608]{0:T(1024)(128)(4,1)} %bitcast.50), calls=%async_computation | async-start | bytes 8388608
  103.7 5.8 %copy-start.6 = (bf16[192,1024]{1,0:T(8,128)(2,1)}, bf16[192,1024]{1,0:T(8,128)(2,1)S(1)}, u32[]{:S(2)}) copy-start(bf16[192,1024]{1,0:T(8,128)(2,1)S(1)} %fusion.9.refs_8_) | copy-start | bytes 1179652
  103.7 5.9 %slice-start.1 = ((s8[8388608]{0:T(1024)(128)(4,1)}), s8[4194304]{0:T(1024)(128)(4,1)S(1)}, s32[]{:S(2)}) async-start(s8[8388608]{0:T(1024)(128)(4,1)} %bitcast.50), calls=%async_computation.1 | async-start | bytes 8388608
  109.6 2.1 copy-start.7
  113.4 2.9 copy-start.4
  116.3 10.2 %copy-start = (bf16[192,4096]{1,0:T(8,128)(2,1)}, bf16[192,4096]{1,0:T(8,128)(2,1)S(1)}, u32[]{:S(2)}) copy-start(bf16[192,4096]{1,0:T(8,128)(2,1)S(1)} %fusion.refs_11_) | copy-start | bytes 4718596
  123.2 1.7 copy-start.1
  124.9 3.2 copy-start.5
  348.0 13.9 %copy-start.8 = (bf16[192,1024]{1,0:T(8,128)(2,1)S(1)}, bf16[192,1024]{1,0:T(8,128)(2,1)}, u32[]{:S(2)}) copy-start(bf16[192,1024]{1,0:T(8,128)(2,1)} %get-tuple-element.54) | copy-start | bytes 1179652

commit v6 on v5

--- a/solution.py
+++ b/solution.py
@@ -410,6 +410,9 @@
     return copy
 
 
+SEQS = HEADS // BPS
+
+
 def plane_peers(c, w, count):
     return [(lax.rem(c + step, count), w) for step in range(1, count)]
 
@@ -466,12 +469,12 @@
     return plan
 
 
-BULK_WAYS = (2, 2)
+BULK_WAYS = (4, 2)
 
 
 def forward_kernel(heads, plan, n_weights, n_vectors, *refs):
-    lens_ref, slot_ref, block_ref, x_ref = refs[:4]
-    refs = refs[4:]
+    table_ref, x_ref = refs[:2]
+    refs = refs[2:]
     shards, vectors = refs[:n_weights], refs[n_weights : n_weights + n_vectors]
     refs = refs[n_weights + n_vectors :]
     wholes, small_whole, a_ref, kept_ref, lse_ref = refs[:n_weights], *refs[n_weights : n_weights + 4]
@@ -638,7 +641,7 @@
         keep = pltpu.make_async_copy(in_buf[m], kept_ref.at[m], keep_sem.at[m])
         keep.start()
         for b in range(blocks):
-            got = in_buf[m][slot_ref[0, m, b]]
+            got = in_buf[m][table_ref[m, SEQS + blocks + b]]
             q_s[b * BLK : (b + 1) * BLK, :] = got[:BLK, :HD]
             k_s[b * BLK : (b + 1) * BLK, :] = got[:BLK, HD:]
             v_s[b * BLK : (b + 1) * BLK, :] = unpack_fold(got[BLK:])
@@ -649,7 +652,7 @@
                 k_s[rows, :], q_s[rows, :], (((1,), (1,)), ((), ())), preferred_element_type=F32
             ) * (1.0 / math.sqrt(HD))
             place = lax.broadcasted_iota(jnp.int32, scores.shape, 0)
-            scores = jnp.where(place < lens_ref[0, m, s], scores, NEG_FILL)
+            scores = jnp.where(place < table_ref[m, s], scores, NEG_FILL)
             top = jnp.max(scores, axis=0, keepdims=True)
             weights = jnp.exp(scores - top)
             total = jnp.sum(weights, axis=0, keepdims=True)
@@ -665,7 +668,7 @@
 
         lax.fori_loop(0, blocks // BPS, one_sequence, 0)
         for t in range(blocks):
-            back_out[m, t] = fold(a_s[block_ref[0, m, t]]).astype(BF16)
+            back_out[m, t] = fold(a_s[table_ref[m, SEQS + t]]).astype(BF16)
         for peer in peers:
             send(
                 back_out.at[m, peer[0]], back_in.at[m, c], back_send.at[m], back_recv.at[m], peer
@@ -690,7 +693,7 @@
         copy.wait()
 
 
-def forward(lens, slot_of, block_of, x, shards, vectors, heads):
+def forward(table, x, shards, vectors, heads):
     plan = weight_plan(shards)
     count = len(shards)
     anywhere, vmem = pl.BlockSpec(memory_space=pl.ANY), pl.BlockSpec(memory_space=pltpu.VMEM)
@@ -710,7 +713,7 @@
             jax.ShapeDtypeStruct((MB, heads, pack_rows, 128), BF16),
             jax.ShapeDtypeStruct((8, span), F32),
         ],
-        in_specs=[smem] * 3 + [vmem] + [anywhere] * count + [vmem] * len(vectors),
+        in_specs=[smem] + [vmem] + [anywhere] * count + [vmem] * len(vectors),
         out_specs=[anywhere] * count + [vmem, vmem, anywhere, vmem],
         scratch_shapes=[pltpu.VMEM(whole(s), s.dtype) for s in shards[:3]]
         + [pltpu.VMEM(s.shape, s.dtype) for s in shards[3:]]
@@ -737,13 +740,150 @@
             collective_id=1, has_side_effects=True, vmem_limit_bytes=VMEM_BYTES
         ),
         name="forward",
-    )(lens, slot_of, block_of, x, *shards, *vectors)
+    )(table, x, *shards, *vectors)
+
+
+def norm_parts(summed):
+    row_mean = jnp.mean(summed, axis=-1, keepdims=True)
+    centred = summed - row_mean
+    row_var = jnp.mean(centred * centred, axis=-1, keepdims=True)
+    scale = lax.rsqrt(row_var + EPSILON)
+    return centred * scale, scale
+
+
+def norm_back(grad, unit, scale, gain):
+    inner = grad * gain
+    mean_one = jnp.mean(inner, axis=-1, keepdims=True)
+    mean_two = jnp.mean(inner * unit, axis=-1, keepdims=True)
+    return scale * (inner - mean_one - unit * mean_two)
+
+
+def dot_minor(a, b):
+    return lax.dot_general(a, b, (((1,), (1,)), ((), ())), preferred_element_type=F32)
+
+
+ROW_OUT, ROW_UP, ROW_DOWN, ROW_GAIN_ONE, ROW_SHIFT_ONE, ROW_GAIN_TWO, ROW_SHIFT_TWO = 2, 3, 7, 8, 9, 10, 11
+
+
+def dense_kernel(a_ref, x_ref, cot_ref, small_ref, wo_hbm, wu_hbm, wd_hbm, *refs):
+    out_ref, n_ref, g_ref, do_ref, du_ref, dm_ref, dh_ref, da_ref, vec_ref = refs[:9]
+    wo, wu, wd, slope, n_full, unit, total, wo_sem, wu_sem, wd_sem = refs[9:]
+    lanes = small_ref.shape[2]
+    hidden = g_ref.shape[1]
+    per_half = hidden // 2 // lanes
+    chunks = hidden // lanes
+    loads = [pltpu.make_async_copy(wo_hbm, wo, wo_sem.at[0])]
+    for j in range(chunks):
+        cols = pl.ds(j * lanes, lanes)
+        loads.append(pltpu.make_async_copy(wu_hbm.at[:, cols], wu.at[:, cols], wu_sem.at[j]))
+        loads.append(pltpu.make_async_copy(wd_hbm.at[cols], wd.at[cols], wd_sem.at[j]))
+    for load in loads:
+        load.start()
+
+    def line(row):
+        return jnp.concatenate([small_ref[0, row : row + 1, :], small_ref[1, row : row + 1, :]], axis=1)
+
+    def keep(row, values):
+        summed = jnp.sum(values, axis=0, keepdims=True)
+        for side in range(2):
+            vec_ref[side, row : row + 1, :] = summed[:, side * lanes : (side + 1) * lanes]
+
+    loads[0].wait()
+    h_one = x_ref[...].astype(F32) + (
+        jnp.dot(a_ref[...], wo[...], preferred_element_type=F32) + line(ROW_OUT)
+    )
+    unit_one, scale_one = norm_parts(h_one)
+    unit[...] = unit_one
+    n_one = unit_one * line(ROW_GAIN_ONE) + line(ROW_SHIFT_ONE)
+    n_full[...] = n_one
+    n_ref[...] = n_one.astype(BF16)
+    total[...] = jnp.zeros_like(total)
+
+    def up_and_down(j, carry):
+        at = pl.multiple_of(j * lanes, lanes)
+        cols = pl.ds(at, lanes)
+        pltpu.make_async_copy(wu_hbm.at[:, cols], wu.at[:, cols], wu_sem.at[j]).wait()
+        pltpu.make_async_copy(wd_hbm.at[cols], wd.at[cols], wd_sem.at[j]).wait()
+        bias = small_ref[lax.div(j, per_half), pl.ds(ROW_UP + lax.rem(j, per_half), 1), :]
+        u = jnp.dot(n_ref[...], wu[:, cols], preferred_element_type=F32) + bias
+        below = 0.5 * (1.0 + lax.erf(u * math.sqrt(0.5)))
+        slope[:, cols] = below + u * jnp.exp(-0.5 * u * u) * (1.0 / math.sqrt(2.0 * math.pi))
+        g = (u * below).astype(BF16)
+        g_ref[:, cols] = g
+        total[...] += jnp.dot(g, wd[cols, :], preferred_element_type=F32)
+        return carry
+
+    lax.fori_loop(0, chunks, up_and_down, 0, unroll=True)
+    h_two = n_full[...] + (total[...] + line(ROW_DOWN))
+    unit_two, scale_two = norm_parts(h_two)
+    out_ref[...] = (unit_two * line(ROW_GAIN_TWO) + line(ROW_SHIFT_TWO)).astype(BF16)
+    cot = cot_ref[...].astype(F32)
+    keep(ROW_GAIN_TWO, cot * unit_two)
+    keep(ROW_SHIFT_TWO, cot)
+    dh_two = norm_back(cot, unit_two, scale_two, line(ROW_GAIN_TWO))
+    dm = dh_two.astype(BF16)
+    dm_ref[...] = dm
+    keep(ROW_DOWN, dm.astype(F32))
+    total[...] = dh_two
+
+    def down_and_up(j, carry):
+        cols = pl.ds(pl.multiple_of(j * lanes, lanes), lanes)
+        du = (slope[:, cols] * dot_minor(dm_ref[...], wd[cols, :])).astype(BF16)
+        du_ref[:, cols] = du
+        vec_ref[lax.div(j, per_half), pl.ds(ROW_UP + lax.rem(j, per_half), 1), :] = jnp.sum(
+            du.astype(F32), axis=0, keepdims=True
+        )
+        total[...] += dot_minor(du, wu[:, cols])
+        return carry
+
+    lax.fori_loop(0, chunks, down_and_up, 0, unroll=True)
+    dn = total[...]
+    keep(ROW_GAIN_ONE, dn * unit[...])
+    keep(ROW_SHIFT_ONE, dn)
+    dh_one = norm_back(dn, unit[...], scale_one, line(ROW_GAIN_ONE))
+    dh_ref[...] = dh_one
+    do = dh_one.astype(BF16)
+    do_ref[...] = do
+    keep(ROW_OUT, do.astype(F32))
+    da_ref[...] = dot_minor(do, wo[...]).astype(BF16)
+    for side in range(2):
+        vec_ref[side, 0:ROW_OUT, :] = jnp.zeros((ROW_OUT, lanes), F32)
+
+
+def dense(a, x, cot, small, wo, wu, wd):
+    vmem, anywhere = pl.BlockSpec(memory_space=pltpu.VMEM), pl.BlockSpec(memory_space=pl.ANY)
+    rows, width = x.shape
+    hidden = wu.shape[1]
+    chunks = hidden // small.shape[2]
+    low = lambda cols: jax.ShapeDtypeStruct((rows, cols), BF16)
+    full = lambda cols: pltpu.VMEM((rows, cols), F32)
+    return pl.pallas_call(
+        dense_kernel,
+        out_shape=[
+            low(width),
+            low(width),
+            low(hidden),
+            low(width),
+            low(hidden),
+            low(width),
+            jax.ShapeDtypeStruct((rows, width), F32),
+            low(width),
+            jax.ShapeDtypeStruct(small.shape, F32),
+        ],
+        in_specs=[vmem] * 4 + [anywhere] * 3,
+        out_specs=[vmem] * 9,
+        scratch_shapes=[pltpu.VMEM(item.shape, BF16) for item in (wo, wu, wd)]
+        + [full(hidden), full(width), full(width), full(width)]
+        + [pltpu.SemaphoreType.DMA((n,)) for n in (1, chunks, chunks)],
+        compiler_params=pltpu.CompilerParams(vmem_limit_bytes=VMEM_BYTES),
+        name="dense",
+    )(a, x, cot, small, wo, wu, wd)
 
 
 ORDERS = (
-    ("yxzZ", "zxyZ"),
-    ("xyzZ", "xzyZ"),
-    ("yxZz", "zxyZ"),
+    ("yxzZ", "xyzZ", "zxyZ", "yxzZ"),
+    ("xzyZ", "zyxZ", "xyzZ", "yzxZ"),
+    ("xyzZ", "zxyZ", "yxzZ", "xyzZ"),
 )
 PIECES = len(ORDERS[0])
 KEYS = tuple((part, piece) for part in range(3) for piece in range(PIECES))
@@ -778,11 +918,11 @@
 
 
 def backward_kernel(heads, *refs):
-    lens_ref, slot_ref, block_ref, da_ref, kept_ref, lse_ref = refs[:6]
-    x_ref, a_ref, n_ref, g_ref, do_ref, du_ref, dm_ref, vec_ref, dh_ref = refs[6:15]
-    weights = refs[15:18]
-    rows_out, o_a, o_b, o_c, vec_out = refs[18:23]
-    refs = refs[23:]
+    table_ref, da_ref, kept_ref, lse_ref = refs[:4]
+    x_ref, a_ref, n_ref, g_ref, do_ref, du_ref, dm_ref, vec_ref, dh_ref = refs[4:13]
+    weights = refs[13:16]
+    rows_out, o_a, o_b, o_c, vec_out = refs[16:21]
+    refs = refs[21:]
     in_buf = refs[:MB]
     out_buf, back_out, back_in, q_s, k_s, v_s, a_s, dq_s, dk_s, dv_s = refs[MB : MB + 10]
     refs = refs[MB + 10 :]
@@ -888,7 +1028,7 @@
     def attention(m):
         all_bytes(in_buf[m], recv_sem.at[m], heads - 1).wait()
         for b in range(blocks):
-            slot = slot_ref[0, m, b]
+            slot = table_ref[m, SEQS + blocks + b]
             got = kept_ref[m, slot]
             rows = slice(b * BLK, (b + 1) * BLK)
             q_s[rows, :] = got[:BLK, :HD]
@@ -904,7 +1044,7 @@
             scores = lax.dot_general(kk, qq, minor, preferred_element_type=F32) * scale
             spot = lax.broadcasted_iota(jnp.int32, scores.shape, 0)
             total = lse_ref[pl.ds(m * (blocks // BPS) + s, 1), :]
-            probs = jnp.exp(jnp.where(spot < lens_ref[0, m, s], scores - total, NEG_FILL))
+            probs = jnp.exp(jnp.where(spot < table_ref[m, s], scores - total, NEG_FILL))
             dp = lax.dot_general(vv, dd, minor, preferred_element_type=F32)
             both = probs * dp
             delta = jnp.sum(both, axis=0, keepdims=True)
@@ -918,7 +1058,7 @@
 
         lax.fori_loop(0, blocks // BPS, one_sequence, 0)
         for t in range(blocks):
-            at = block_ref[0, m, t]
+            at = table_ref[m, SEQS + t]
             back_out[m, t, 0:BLK, :] = jnp.concatenate([dq_s[at], dk_s[at]], axis=1).astype(BF16)
             back_out[m, t, BLK:, :] = fold(dv_s[at]).astype(BF16)
         for peer in peers:
@@ -1103,10 +1243,20 @@
         flight.wait_send()
 
 
-SCHEDULE = default_schedule()
-
-
-def backward(lens, slot_of, block_of, da, kept, lse, x, a, n1, g, do, du, dm, vec, dh, weights, heads):
+SCHEDULE = (
+    "down", 0, "up", 1, 2, (2, 0), (1, 3), (1, 1), (2, 2), (1, 0), (2, 0), (1, 3), (1, 2),
+    "back", (2, 2), (2, 0), (2, 3), (1, 2), (1, 3), "qkv", (1, 3), (2, 3), (1, 2), (1, 3),
+    (1, 1), (2, 2), (2, 0), (1, 1), "vec", (2, 1), (2, 2), (2, 0), (2, 1), (0, 1), (1, 3),
+    (2, 2), (1, 2), (2, 3), (0, 0), (2, 1), (1, 0), "vec", (2, 3), (0, 3), (0, 0), (2, 2),
+    (2, 1), (0, 3), (2, 0), (1, 3), (1, 1), (2, 1), (0, 2), "vec", (1, 2), (2, 3), (1, 0),
+    (1, 1), (0, 1), (0, 3), (0, 0), (2, 1), (1, 0), (2, 0), (2, 2), (0, 2), "vec", (0, 3),
+    (0, 1), (1, 2), (0, 3), (0, 2), (2, 3), "rows", (0, 0), (1, 0), (1, 1), (0, 2), (0, 0),
+    (0, 3), (0, 1), "vec", (0, 2), (0, 1), (1, 0), (0, 0), (1, 2), (0, 1), (0, 2), (0, 3),
+    (0, 0), (0, 1), (1, 1), (2, 3), (1, 0), (2, 1), (0, 2),
+)
+
+
+def backward(table, da, kept, lse, x, a, n1, g, do, du, dm, vec, dh, weights, heads):
     vmem, smem = pl.BlockSpec(memory_space=pltpu.VMEM), pl.BlockSpec(memory_space=pltpu.SMEM)
     anywhere = pl.BlockSpec(memory_space=pl.ANY)
     rows, width = da.shape
@@ -1142,31 +1292,39 @@
             jax.ShapeDtypeStruct(c_shape, BF16),
             jax.ShapeDtypeStruct(vec.shape[1:], F32),
         ],
-        in_specs=[smem] * 3 + [vmem] * 12 + [anywhere] * 3,
+        in_specs=[smem] + [vmem] * 12 + [anywhere] * 3,
         out_specs=[vmem] + [anywhere] * 3 + [vmem],
         scratch_shapes=scratch,
         compiler_params=pltpu.CompilerParams(
             collective_id=2, has_side_effects=True, vmem_limit_bytes=VMEM_BYTES
         ),
         name="backward",
-    )(lens, slot_of, block_of, da, kept, lse, x, a, n1, g, do, du, dm, vec, dh, *weights)
-
-
-def widen_kernel(a_ref, b_ref, c_ref, *outs):
+    )(table, da, kept, lse, x, a, n1, g, do, du, dm, vec, dh, *weights)
+
+
+def widen_kernel(a_ref, b_ref, c_ref, vec_ref, *outs):
+    @pl.when(pl.program_id(0) == 0)
+    def _():
+        line, lanes = 0, vec_ref.shape[1]
+        for out in outs[6:]:
+            for first in range(0, out.shape[0], lanes):
+                out[pl.ds(first, lanes)] = vec_ref[line, :]
+                line += 1
+
     half = outs[0].shape[1] // 2
     for index, out in enumerate(outs[:4]):
         for core in range(2):
             out[:, core * half : (core + 1) * half] = a_ref[
                 core, 0, :, index * half : (index + 1) * half
             ].astype(F32)
-    up, down = outs[4:]
+    up, down = outs[4:6]
     half = up.shape[1] // 2
     for core in range(2):
         up[:, core * half : (core + 1) * half] = b_ref[core, 0].astype(F32)
         down[core, 0] = c_ref[core, 0].astype(F32)
 
 
-def widen(o_a, o_b, o_c):
+def widen(o_a, o_b, o_c, vec, sizes):
     shards = o_a.shape[1]
     block = lambda item: pl.BlockSpec((2, 1) + item.shape[2:], lambda i: (0, i, 0, 0))
     rows = o_a.shape[2]
@@ -1176,35 +1334,15 @@
         widen_kernel,
         grid=(shards,),
         out_shape=[jax.ShapeDtypeStruct(square, F32)] * 4
-        + [jax.ShapeDtypeStruct(wide, F32), jax.ShapeDtypeStruct(o_c.shape, F32)],
-        in_specs=[block(o_a), block(o_b), block(o_c)],
+        + [jax.ShapeDtypeStruct(wide, F32), jax.ShapeDtypeStruct(o_c.shape, F32)]
+        + [jax.ShapeDtypeStruct((size,), F32) for size in sizes],
+        in_specs=[block(o_a), block(o_b), block(o_c), pl.BlockSpec(vec.shape, lambda i: (0, 0))],
         out_specs=[pl.BlockSpec((rows, square[1]), lambda i: (i, 0))] * 4
-        + [pl.BlockSpec((rows, wide[1]), lambda i: (i, 0)), block(o_c)],
+        + [pl.BlockSpec((rows, wide[1]), lambda i: (i, 0)), block(o_c)]
+        + [pl.BlockSpec((size,), lambda i: (0,)) for size in sizes],
         compiler_params=pltpu.CompilerParams(vmem_limit_bytes=VMEM_BYTES),
         name="widen",
-    )(o_a, o_b, o_c)
-
-
-def norm_parts(summed):
-    row_mean = jnp.mean(summed, axis=-1, keepdims=True)
-    centred = summed - row_mean
-    row_var = jnp.mean(centred * centred, axis=-1, keepdims=True)
-    scale = lax.rsqrt(row_var + EPSILON)
-    return centred * scale, scale
-
-
-def norm_back(grad, unit, scale, gain):
-    inner = grad * gain
-    mean_one = jnp.mean(inner, axis=-1, keepdims=True)
-    mean_two = jnp.mean(inner * unit, axis=-1, keepdims=True)
-    return scale * (inner - mean_one - unit * mean_two)
-
-
-def dot(a, b, dims):
-    return lax.dot_general(a, b, (dims, ((), ())), preferred_element_type=F32)
-
-
-ROW_COL, COL_COL, ROW_ROW = ((1,), (0,)), ((1,), (1,)), ((0,), (0,))
+    )(o_a, o_b, o_c, vec)
 
 
 def per_device_heads(tokens, cotangent, lengths, dealing, *params):
@@ -1214,48 +1352,17 @@
     weights, vectors = params[:6], params[6:]
     sizes = [item.shape[0] for item in vectors]
     x = tokens.reshape(rows, width)
-    lens, block_of = lengths, dealing
-    slot_of = jnp.argsort(block_of, axis=2).astype(jnp.int32)
-    *wholes, small_whole, a, kept, lse = forward(
-        lens, slot_of, block_of, x, weights, vectors, HEADS
+    blocks = jnp.arange(HEADS, dtype=jnp.int32)
+    at_block = dealing[0][:, :, None] == blocks[None, None, :]
+    slot_of = jnp.sum(jnp.where(at_block, blocks[None, :, None], 0), axis=1)
+    table = jnp.concatenate([lengths[0], dealing[0], slot_of], axis=1)
+    *wholes, small_whole, a, kept, lse = forward(table, x, weights, vectors, HEADS)
+    query_w, key_w, value_w, out_w, up_w, down_w = wholes
+    output, n_low, g, do, du, dm, dh_one, da, vec = dense(
+        a, x, cotangent.reshape(rows, width), small_whole, out_w, up_w, down_w
     )
-    query_w, key_w, value_w, out_w, up_w, down_w = wholes
-    spots = [sum(sizes[:i]) for i in range(len(sizes) + 1)]
-    lines = [spot // small_whole.shape[2] for spot in spots]
-    _, _, bias_out, bias_up, bias_down, gain_one, shift_one, gain_two, shift_two = (
-        small_whole[:, lines[i] : lines[i + 1]].reshape(1, -1) for i in range(len(sizes))
-    )
-    h_one = x.astype(F32) + (dot(a, out_w, ROW_COL) + bias_out)
-    unit_one, scale_one = norm_parts(h_one)
-    n_one = unit_one * gain_one + shift_one
-    n_low = n_one.astype(BF16)
-    u = dot(n_low, up_w, ROW_COL) + bias_up
-    below = 0.5 * (1.0 + lax.erf(u * math.sqrt(0.5)))
-    slope = below + u * jnp.exp(-0.5 * u * u) * (1.0 / math.sqrt(2.0 * math.pi))
-    g, slope = lax.optimization_barrier(((u * below).astype(BF16), slope))
-    h_two = n_one + (dot(g, down_w, ROW_COL) + bias_down)
-    unit_two, scale_two = norm_parts(h_two)
-    output = (unit_two * gain_two + shift_two).astype(BF16)
-
-    cot = cotangent.reshape(rows, width).astype(F32)
-    dh_two = norm_back(cot, unit_two, scale_two, gain_two)
-    dm = dh_two.astype(BF16)
-    du = lax.optimization_barrier((slope * dot(dm, down_w, COL_COL)).astype(BF16))
-    dn = lax.optimization_barrier(dot(du, up_w, COL_COL)) + dh_two
-    dh_one = norm_back(dn, unit_one, scale_one, gain_one)
-    do = dh_one.astype(BF16)
-    da = dot(do, out_w, COL_COL).astype(BF16)
-
-    total = lambda item: jnp.sum(item.astype(F32), axis=0).reshape(2, -1, small_whole.shape[2])
-    nothing = jnp.zeros((2, 2, small_whole.shape[2]), F32)
-    vec = [nothing] + [
-        total(item)
-        for item in (do, du, dm, dn * unit_one, dn, cot * unit_two, cot)
-    ]
     grad_tokens, o_a, o_b, o_c, vec_sum = backward(
-        lens,
-        slot_of,
-        block_of,
+        table,
         da,
         kept,
         lse,
@@ -1266,20 +1373,17 @@
         do,
         du,
         dm,
-        jnp.concatenate(vec, axis=1),
+        vec,
         dh_one,
         (query_w, key_w, value_w),
         HEADS,
     )
-    *square, up, down = widen(o_a, o_b, o_c)
-    down = down.reshape(-1, width)
-    vec_sum = vec_sum.reshape(-1)
-    ends = [vec_sum[spots[i] : spots[i + 1]] for i in range(len(sizes))]
+    grads = list(widen(o_a, o_b, o_c, vec_sum, sizes))
+    grads[5] = grads[5].reshape(-1, width)
     shape = (1, MB, rows_in, width)
     return (
         (output.reshape(shape), grad_tokens.reshape(shape))
-        + (*square, up, down)
-        + tuple(ends)
+        + tuple(grads)
     )
 
 

time: 363 us -> 320 us (0.88)
  matrix products: 21.6 us -> 0 us
  local copies, waits for them, and re-layouts: 10.7 us -> 2.2 us
  Pallas kernels: 323 us -> 316 us
  other arithmetic: 5.85 us -> 0.75 us
    pallas_call x1, Pallas kernels: 217 us -> 190 us  [backward(): pl.pallas_call(functools.partial(backward_kernel, heads), out_shape=[jax....]
    pallas_call x0 -> x1, Pallas kernels: none -> 22.2 us  [dense(): pl.pallas_call(dense_kernel, out_shape=[low(width), low(width), low(hidde...]
    dot_general x6 -> x0, matrix products: 21.6 us -> none  [dot(): return lax.dot_general(a, b, (dims, ((), ())), preferred_element_type=F32)]
    unnamed x30 -> x4, local copies, waits for them, and re-layouts: 6.26 us -> 1.43 us
    reduce_sum x8 -> x1, other arithmetic: 4.1 us -> 0.09 us  [per_device_heads(): slot_of = jnp.sum(jnp.where(at_block, blocks[None, :, None], 0), axis=1)]
where the time goes in v6:
time: 320 us; the launch traced here: 319 us
  Pallas kernels  316 us (99%)
    pallas_call x1, Pallas kernels, backward(): pl.pallas_call(functools.partial(backward_kernel, heads), out_shape=[jax....  190 us
    pallas_call x1, Pallas kernels, forward(): pl.pallas_call(functools.partial(forward_kernel, heads, plan, count, len(...  89.2 us
    pallas_call x1, Pallas kernels, dense(): pl.pallas_call(dense_kernel, out_shape=[low(width), low(width), low(hidde...  22.2 us
    pallas_call x1, Pallas kernels, widen(): pl.pallas_call(widen_kernel, grid=(shards,), out_shape=[jax.ShapeDtypeStr...  13.9 us

profile of v6, /device:TPU:0, one launch (start us, length us, event | category | flops | bytes accessed | tf_op | source)
XLA Modules:
  0.0 319.2 jit_solution(5592446280460282842)
XLA Ops:
  0.7 0.8 copy.37
  1.4 0.7 copy.40
  2.1 0.1 select_reduce_fusion
  2.2 0.7 pad_add_fusion.refs_0_
  2.9 89.2 %forward.1 = (bf16[1024,1024]{1,0:T(8,128)(2,1)}, bf16[1024,1024]{1,0:T(8,128)(2,1)}, bf16[1024,1024]{1,0:T(8,128)(2,1)}, bf16[1024,1024]{1,0:T(8,128)(2,1)}, bf...) custom-call(s32[3,34]{1,0:T(4,128)} %pad_add_fusion.refs_0_, ...), custom_call_target="tpu_custom_call" | custom-call | tf_op jit(solution)/shard_map/forward/pallas_call | solution.py:707
  92.0 22.2 %dense.1 = (bf16[192,1024]{1,0:T(8,128)(2,1)}, bf16[192,1024]{1,0:T(8,128)(2,1)}, bf16[192,4096]{1,0:T(8,128)(2,1)}, bf16[192,1024]{1,0:T(8,128)(2,1)}, bf16[192...) custom-call(bf16[192,1024]{1,0:T(8,128)(2,1)} %get-tuple-element.56., ...), custom_call_target="tpu_custom_call" | custom-call | tf_op jit(solution)/shard_map/dense/pallas_call | solution.py:860
  114.2 190.2 %backward.1 = (bf16[192,1024]{1,0:T(8,128)(2,1)}, bf16[2,8,64,2048]{3,2,1,0:T(8,128)(2,1)}, bf16[2,8,64,2048]{3,2,1,0:T(8,128)(2,1)}, bf16[2,8,128,1024]{3,2,1,0:T(8,128)(2,1)}, f32[12,512]{1,0:T(8,128)}) custom-call(s32[3,34]{1,0:T(4,128)} %pad_add_fusion.refs_0_, bf16[192,1024]{1,0:T(8,128)(2,1)} %get-tuple-element.62.refs_1_, ...), custom_call_target="tpu_custom_call" | custom-call | tf_op jit(solution)/shard_map/backward/pallas_call | solution.py:1286
  304.5 0.0 copy-start
  304.5 13.9 %widen.1 = (f32[512,1024]{1,0:T(8,128)}, f32[512,1024]{1,0:T(8,128)}, f32[512,1024]{1,0:T(8,128)}, f32[512,1024]{1,0:T(8,128)}, f32[512,4096]{1,0:T(8,128)}, /*i...) custom-call(bf16[2,8,64,2048]{3,2,1,0:T(8,128)(2,1)} %get-tuple-elem, ...), custom_call_target="tpu_custom_call" | custom-call | tf_op jit(solution)/shard_map/widen/pallas_call | solution.py:1333
  318.4 0.0 copy-done
  318.4 0.7 copy.42
Async XLA Ops:
  304.5 13.9 %copy-start = (bf16[192,1024]{1,0:T(8,128)(2,1)S(1)}, bf16[192,1024]{1,0:T(8,128)(2,1)}, u32[]{:S(2)}) copy-start(bf16[192,1024]{1,0:T(8,128)(2,1)} %get-tuple-element.75) | copy-start | bytes 1179652

commit v7 on v6

--- a/solution.py
+++ b/solution.py
@@ -443,46 +443,71 @@
     return pltpu.make_async_copy(view, view, sem)
 
 
+def norm_parts(summed):
+    row_mean = jnp.mean(summed, axis=-1, keepdims=True)
+    centred = summed - row_mean
+    row_var = jnp.mean(centred * centred, axis=-1, keepdims=True)
+    scale = lax.rsqrt(row_var + EPSILON)
+    return centred * scale, scale
+
+
+def norm_back(grad, unit, scale, gain):
+    inner = grad * gain
+    mean_one = jnp.mean(inner, axis=-1, keepdims=True)
+    mean_two = jnp.mean(inner * unit, axis=-1, keepdims=True)
+    return scale * (inner - mean_one - unit * mean_two)
+
+
+def dot_minor(a, b):
+    return lax.dot_general(a, b, (((1,), (1,)), ((), ())), preferred_element_type=F32)
+
+
+ROW_OUT, ROW_UP, ROW_DOWN, ROW_GAIN_ONE, ROW_SHIFT_ONE, ROW_GAIN_TWO, ROW_SHIFT_TWO = 2, 3, 7, 8, 9, 10, 11
+
+
 SQUARE, PAIR, ALONE = 8, 4, 2
+WAYS = (SQUARE,) * 3 + (SQUARE,) * 4 + (PAIR,) * 3 + (ALONE,) * 2
 
 
 def weight_plan(shards):
-    plan, first_bulk = [], 3
-    for index in range(first_bulk):
-        plan.append((index, 0, shards[index].shape[0], SQUARE))
     unit = shards[0].shape[0] * shards[0].shape[1]
-    bulk = []
-    for index in range(first_bulk, len(shards)):
-        rows, cols = shards[index].shape
+    plan = []
+    for index, (rows, cols) in enumerate(shard.shape for shard in shards):
         parts = max(1, rows * cols // unit)
         for part in range(parts):
-            bulk.append((index, part * (rows // parts), rows // parts))
-    squares, alone = BULK_WAYS
-    for number, item in enumerate(bulk):
-        if number < squares:
-            way = SQUARE
-        elif number >= len(bulk) - alone:
-            way = ALONE
-        else:
-            way = PAIR
-        plan.append(item + (way,))
+            plan.append((index, part * (rows // parts), rows // parts, WAYS[len(plan)]))
     return plan
 
 
-BULK_WAYS = (4, 2)
+def forward_schedule():
+    squares = [i for i, way in enumerate(WAYS) if way == SQUARE and i > 2]
+    pairs = [i for i, way in enumerate(WAYS) if way == PAIR]
+    alone = [i for i, way in enumerate(WAYS) if way == ALONE]
+    events = [("second", i) for i in squares + pairs[:1]] + [("att", 0)]
+    events += [("third", i) for i in squares] + [("second", i) for i in pairs[1:2]] + [("att", 1)]
+    events += [("fourth", i) for i in squares] + [("second", i) for i in pairs[2:3]] + [("att", 2)]
+    events += [("fourth", i) for i in pairs[:2]] + [("rows", 0)]
+    events += [("fourth", i) for i in pairs[2:] + alone] + [("out", 0)]
+    return events + [("hidden", t) for t in range(8)]
+
+
+FORWARD_SCHEDULE = forward_schedule()
 
 
 def forward_kernel(heads, plan, n_weights, n_vectors, *refs):
-    table_ref, x_ref = refs[:2]
-    refs = refs[2:]
+    table_ref, x_ref, cot_ref = refs[:3]
+    refs = refs[3:]
     shards, vectors = refs[:n_weights], refs[n_weights : n_weights + n_vectors]
     refs = refs[n_weights + n_vectors :]
-    wholes, small_whole, a_ref, kept_ref, lse_ref = refs[:n_weights], *refs[n_weights : n_weights + 4]
-    refs = refs[n_weights + 4 :]
-    near, stages, refs = refs[:3], refs[3:n_weights], refs[n_weights:]
-    small, small_in, bias, q_ref, k_ref, v_ref = refs[:6]
-    in_buf = refs[6 : 6 + MB]
-    out_buf, back_out, back_in, q_s, k_s, v_s, a_s = refs[6 + MB : 13 + MB]
+    wholes, kept_ref, lse_ref, a_ref = refs[:3], *refs[3:6]
+    out_ref, n_ref, g_ref, do_ref, du_ref, dm_ref, dh_ref, da_ref, vec_ref = refs[6:15]
+    refs = refs[15:]
+    near, refs = refs[:n_weights], refs[n_weights:]
+    small, small_in, small_whole, bias, q_ref, k_ref, v_ref = refs[:7]
+    slope, n_full, unit, total = refs[7:11]
+    refs = refs[11:]
+    in_buf = refs[:MB]
+    out_buf, back_out, back_in, q_s, k_s, v_s, a_s = refs[MB : 7 + MB]
     (
         w_send,
         w_recv,
@@ -494,19 +519,17 @@
         back_send,
         back_recv,
         keep_sem,
-    ) = refs[13 + MB :]
+    ) = refs[7 + MB :]
     c, w = lax.axis_index("ctx"), lax.axis_index("wsh")
     o = 1 - w
     by_x, by_y, by_z, by_core = (c, o), (flip(c, 2), w), (flip(c, 4), w), (flip(c, 1), w)
     core, y, z = bit_of(c, 1), bit_of(c, 2), bit_of(c, 4)
     peers = plane_peers(c, w, heads)
-    targets = tuple(near) + tuple(wholes[3:])
-    staged, locals_ = [], []
+    staged = []
     for index, shard in enumerate(shards):
         rows = shard.shape[0]
         spot = pl.ds(pl.multiple_of(w * rows, rows), rows)
-        dst = near[index].at[spot] if index < 3 else stages[index - 3]
-        copy = pltpu.make_async_copy(shard, dst, stage_sem.at[index])
+        copy = pltpu.make_async_copy(shard, near[index].at[spot], stage_sem.at[index])
         copy.start()
         staged.append(copy)
     line, lanes = 0, small.shape[1]
@@ -522,7 +545,7 @@
         tensor, first, rows, way = plan[chunk]
         half = shards[tensor].shape[0]
         at = side * half + first + piece * (rows // way) + start
-        return targets[tensor].at[pl.ds(pl.multiple_of(at, 8), count)]
+        return near[tensor].at[pl.ds(pl.multiple_of(at, 8), count)]
 
     steps = {}
 
@@ -539,8 +562,6 @@
 
     def second(chunk):
         _, _, rows, way = plan[chunk]
-        if way == ALONE:
-            return
         steps[chunk, 0].wait_recv()
         ref = part(chunk, o, own_piece(way), 0, rows // way)
         steps[chunk, 1] = send(ref, ref, *sem(1, chunk), by_y)
@@ -549,8 +570,6 @@
 
     def third(chunk):
         _, _, rows, way = plan[chunk]
-        if way != SQUARE:
-            return
         size = rows // way
         steps[chunk, 1].wait_recv()
         steps[chunk, 2].wait_recv()
@@ -587,10 +606,10 @@
 
         def project(turn, carry):
             cols = pl.ds(pl.multiple_of(turn * step, step), step)
-            total = jnp.dot(x_ref[...], weight[:, cols], preferred_element_type=F32)
+            product = jnp.dot(x_ref[...], weight[:, cols], preferred_element_type=F32)
             if index != 1:
-                total = total + bias[index // 2 : index // 2 + 1, cols]
-            out[:, cols] = total.astype(BF16)
+                product = product + bias[index // 2 : index // 2 + 1, cols]
+            out[:, cols] = product.astype(BF16)
             return carry
 
         lax.fori_loop(0, width // step, project, 0)
@@ -600,46 +619,14 @@
         for peer in peers:
             send(out_buf.at[m, peer[0]], in_buf[m].at[c], send_sem.at[m], recv_sem.at[m], peer)
         in_buf[m][c] = out_buf[m, c]
-    for index in range(n_weights):
-        if index < 3:
-            copy = pltpu.make_async_copy(near[index], wholes[index], local_sem.at[index])
-        else:
-            rows = shards[index].shape[0]
-            spot = pl.ds(pl.multiple_of(w * rows, rows), rows)
-            staged[index].wait()
-            copy = pltpu.make_async_copy(
-                stages[index - 3], wholes[index].at[spot], local_sem.at[index]
-            )
-        copy.start()
-        locals_.append(copy)
-
-    bulk = range(3, len(plan))
-    kinds = {way: [i for i in bulk if plan[i][3] == way] for way in (SQUARE, PAIR, ALONE)}
-    squares, pairs, alone = kinds[SQUARE], kinds[PAIR], kinds[ALONE]
-    moves = [(second, i) for i in squares + pairs[:2]]
-    moves += [None]
-    moves += [(third, i) for i in squares] + [(second, i) for i in pairs[2:3]]
-    moves += [None]
-    moves += [(fourth, i) for i in squares] + [(second, i) for i in pairs[3:4]]
-    moves += [(fourth, i) for i in pairs[:2]]
-    moves += [None]
-    moves += [(second, i) for i in pairs[4:]] + [(fourth, i) for i in pairs[2:]]
-    moves += [(fourth, i) for i in alone]
-
-    def pump():
-        while moves:
-            move = moves.pop(0)
-            if move is None:
-                return
-            move[0](move[1])
-
+    for index in range(3):
+        pltpu.make_async_copy(near[index], wholes[index], local_sem.at[index]).start()
     blocks = heads
     span = BPS * BLK
-    for m in range(MB):
-        pump()
+
+    def attention(m):
         all_bytes(in_buf[m], recv_sem.at[m], heads - 1).wait()
-        keep = pltpu.make_async_copy(in_buf[m], kept_ref.at[m], keep_sem.at[m])
-        keep.start()
+        pltpu.make_async_copy(in_buf[m], kept_ref.at[m], keep_sem.at[m]).start()
         for b in range(blocks):
             got = in_buf[m][table_ref[m, SEQS + blocks + b]]
             q_s[b * BLK : (b + 1) * BLK, :] = got[:BLK, :HD]
@@ -655,15 +642,15 @@
             scores = jnp.where(place < table_ref[m, s], scores, NEG_FILL)
             top = jnp.max(scores, axis=0, keepdims=True)
             weights = jnp.exp(scores - top)
-            total = jnp.sum(weights, axis=0, keepdims=True)
+            summed = jnp.sum(weights, axis=0, keepdims=True)
             out_t = lax.dot_general(
                 v_s[rows, :],
                 weights.astype(BF16),
                 (((0,), (0,)), ((), ())),
                 preferred_element_type=F32,
             )
-            a_s[pl.ds(s * BPS, BPS)] = (out_t / total).T.reshape(BPS, BLK, HD)
-            lse_ref[pl.ds(m * (blocks // BPS) + s, 1), :] = top + jnp.log(total)
+            a_s[pl.ds(s * BPS, BPS)] = (out_t / summed).T.reshape(BPS, BLK, HD)
+            lse_ref[pl.ds(m * (blocks // BPS) + s, 1), :] = top + jnp.log(summed)
             return carry
 
         lax.fori_loop(0, blocks // BPS, one_sequence, 0)
@@ -674,52 +661,164 @@
                 back_out.at[m, peer[0]], back_in.at[m, c], back_send.at[m], back_recv.at[m], peer
             )
         back_in[m, c] = back_out[m, c]
-    pump()
-    for m in range(MB):
-        all_bytes(back_in.at[m], back_recv.at[m], heads - 1).wait()
-        for pair in range(heads // 2):
-            a_ref[m * BLK : (m + 1) * BLK, pair * 128 : (pair + 1) * 128] = jnp.concatenate(
-                [unpack_fold(back_in[m, 2 * pair]), unpack_fold(back_in[m, 2 * pair + 1])], axis=1
-            )
+
+    def come_back(_):
+        for m in range(MB):
+            all_bytes(back_in.at[m], back_recv.at[m], heads - 1).wait()
+            for pair in range(heads // 2):
+                a_ref[m * BLK : (m + 1) * BLK, pair * 128 : (pair + 1) * 128] = jnp.concatenate(
+                    [unpack_fold(back_in[m, 2 * pair]), unpack_fold(back_in[m, 2 * pair + 1])],
+                    axis=1,
+                )
+
+    def line_of(row):
+        return jnp.concatenate(
+            [small_whole[0, row : row + 1, :], small_whole[1, row : row + 1, :]], axis=1
+        )
+
+    def keep(row, values):
+        summed = jnp.sum(values, axis=0, keepdims=True)
+        for side in range(2):
+            vec_ref[side, row : row + 1, :] = summed[:, side * lanes : (side + 1) * lanes]
+
+    out_w, up_w, down_w = near[3:]
+    chunks_of = {t: [i for i, item in enumerate(plan) if item[0] == t] for t in range(n_weights)}
+
+    def arrived(tensor, chunks):
+        for chunk in chunks:
+            steps[chunk, 5].wait_recv()
+
+    def out_project(_):
+        staged[3].wait()
+        arrived(3, chunks_of[3])
+        h_one = x_ref[...].astype(F32) + (
+            jnp.dot(a_ref[...], out_w[...], preferred_element_type=F32) + line_of(ROW_OUT)
+        )
+        unit_one, scale_one = norm_parts(h_one)
+        unit[...] = unit_one
+        n_one = unit_one * line_of(ROW_GAIN_ONE) + line_of(ROW_SHIFT_ONE)
+        n_full[...] = n_one
+        n_ref[...] = n_one.astype(BF16)
+        total[...] = jnp.zeros_like(total)
+        kept_scale.append(scale_one)
+
+    kept_scale = []
+    hidden = g_ref.shape[1]
+    hidden_steps = hidden // lanes
+    per_half = hidden_steps // 2
+
+    def hidden_at(turn):
+        j = lax.rem(w * per_half + turn, hidden_steps)
+        cols = pl.ds(pl.multiple_of(j * lanes, lanes), lanes)
+        return cols, lax.div(j, per_half), pl.ds(ROW_UP + lax.rem(j, per_half), 1)
+
+    def hidden_up(turn):
+        if turn == 0:
+            staged[4].wait()
+            arrived(4, chunks_of[4])
+            staged[5].wait()
+        elif turn >= per_half:
+            share = len(chunks_of[5]) // per_half
+            first = (turn - per_half) * share
+            arrived(5, chunks_of[5][first : first + share])
+        cols, side, row = hidden_at(turn)
+        u = jnp.dot(n_ref[...], up_w[:, cols], preferred_element_type=F32) + small_whole[side, row, :]
+        below = 0.5 * (1.0 + lax.erf(u * math.sqrt(0.5)))
+        slope[:, cols] = below + u * jnp.exp(-0.5 * u * u) * (1.0 / math.sqrt(2.0 * math.pi))
+        g = (u * below).astype(BF16)
+        g_ref[:, cols] = g
+        total[...] += jnp.dot(g, down_w[cols, :], preferred_element_type=F32)
+
+    acts = {
+        "second": second,
+        "third": third,
+        "fourth": fourth,
+        "att": attention,
+        "rows": come_back,
+        "out": out_project,
+        "hidden": hidden_up,
+    }
+    for name, value in FORWARD_SCHEDULE:
+        acts[name](value)
+
+    h_two = n_full[...] + (total[...] + line_of(ROW_DOWN))
+    unit_two, scale_two = norm_parts(h_two)
+    out_ref[...] = (unit_two * line_of(ROW_GAIN_TWO) + line_of(ROW_SHIFT_TWO)).astype(BF16)
+    cot = cot_ref[...].astype(F32)
+    keep(ROW_GAIN_TWO, cot * unit_two)
+    keep(ROW_SHIFT_TWO, cot)
+    dh_two = norm_back(cot, unit_two, scale_two, line_of(ROW_GAIN_TWO))
+    dm = dh_two.astype(BF16)
+    dm_ref[...] = dm
+    keep(ROW_DOWN, dm.astype(F32))
+    total[...] = dh_two
+    for turn in range(hidden_steps):
+        cols, side, row = hidden_at(turn)
+        du = (slope[:, cols] * dot_minor(dm_ref[...], down_w[cols, :])).astype(BF16)
+        du_ref[:, cols] = du
+        vec_ref[side, row, :] = jnp.sum(du.astype(F32), axis=0, keepdims=True)
+        total[...] += dot_minor(du, up_w[:, cols])
+    dn = total[...]
+    keep(ROW_GAIN_ONE, dn * unit[...])
+    keep(ROW_SHIFT_ONE, dn)
+    dh_one = norm_back(dn, unit[...], kept_scale[0], line_of(ROW_GAIN_ONE))
+    dh_ref[...] = dh_one
+    do = dh_one.astype(BF16)
+    do_ref[...] = do
+    keep(ROW_OUT, do.astype(F32))
+    da_ref[...] = dot_minor(do, out_w[...]).astype(BF16)
+    for side in range(2):
+        vec_ref[side, 0:ROW_OUT, :] = jnp.zeros((ROW_OUT, lanes), F32)
+
     for m in range(MB):
         all_bytes(out_buf.at[m], send_sem.at[m], heads - 1).wait()
         all_bytes(back_out.at[m], back_send.at[m], heads - 1).wait()
         pltpu.make_async_copy(in_buf[m], kept_ref.at[m], keep_sem.at[m]).wait()
-    for chunk in bulk:
-        steps[chunk, 5].wait_recv()
     for flight in steps.values():
         flight.wait_send()
-    for copy in locals_:
-        copy.wait()
-
-
-def forward(table, x, shards, vectors, heads):
+    for index in range(3):
+        pltpu.make_async_copy(near[index], wholes[index], local_sem.at[index]).wait()
+
+
+def forward(table, x, cot, shards, vectors, heads):
     plan = weight_plan(shards)
     count = len(shards)
     anywhere, vmem = pl.BlockSpec(memory_space=pl.ANY), pl.BlockSpec(memory_space=pltpu.VMEM)
     smem = pl.BlockSpec(memory_space=pltpu.SMEM)
     rows, width = x.shape
+    hidden = shards[4].shape[1]
     pack_rows = BLK + BLK // 2
     span = BPS * BLK
     lanes = min(item.shape[0] for item in vectors)
     lines = sum(item.shape[0] for item in vectors) // lanes
     whole = lambda s: (2 * s.shape[0],) + s.shape[1:]
+    low = lambda cols: jax.ShapeDtypeStruct((rows, cols), BF16)
+    full = lambda cols: pltpu.VMEM((rows, cols), F32)
+    sems = lambda *dims: pltpu.SemaphoreType.DMA(dims)
     return pl.pallas_call(
         functools.partial(forward_kernel, heads, plan, count, len(vectors)),
-        out_shape=[jax.ShapeDtypeStruct(whole(s), s.dtype) for s in shards]
+        out_shape=[jax.ShapeDtypeStruct(whole(s), s.dtype) for s in shards[:3]]
         + [
-            jax.ShapeDtypeStruct((2, lines, lanes), F32),
-            jax.ShapeDtypeStruct((rows, width), BF16),
             jax.ShapeDtypeStruct((MB, heads, pack_rows, 128), BF16),
             jax.ShapeDtypeStruct((8, span), F32),
+            low(width),
+            low(width),
+            low(width),
+            low(hidden),
+            low(width),
+            low(hidden),
+            low(width),
+            jax.ShapeDtypeStruct((rows, width), F32),
+            low(width),
+            jax.ShapeDtypeStruct((2, lines, lanes), F32),
         ],
-        in_specs=[smem] + [vmem] + [anywhere] * count + [vmem] * len(vectors),
-        out_specs=[anywhere] * count + [vmem, vmem, anywhere, vmem],
-        scratch_shapes=[pltpu.VMEM(whole(s), s.dtype) for s in shards[:3]]
-        + [pltpu.VMEM(s.shape, s.dtype) for s in shards[3:]]
+        in_specs=[smem, vmem, vmem] + [anywhere] * count + [vmem] * len(vectors),
+        out_specs=[anywhere] * 4 + [vmem] * 11,
+        scratch_shapes=[pltpu.VMEM(whole(s), s.dtype) for s in shards]
         + [pltpu.VMEM((lines, lanes), F32)] * 2
-        + [pltpu.VMEM((2, width), F32)]
+        + [pltpu.VMEM((2, lines, lanes), F32), pltpu.VMEM((2, width), F32)]
         + [pltpu.VMEM((rows, width), BF16)] * 3
+        + [full(hidden), full(width), full(width), full(width)]
         + [pltpu.VMEM((heads, pack_rows, 128), BF16)] * MB
         + [
             pltpu.VMEM((MB, heads, pack_rows, 128), BF16),
@@ -729,155 +828,14 @@
             pltpu.VMEM((heads * BLK, HD), BF16),
             pltpu.VMEM((heads * BLK, HD), BF16),
             pltpu.VMEM((heads, BLK, HD), F32),
-            pltpu.SemaphoreType.DMA((6, len(plan))),
-            pltpu.SemaphoreType.DMA((6, len(plan))),
-            pltpu.SemaphoreType.DMA((2,)),
-            pltpu.SemaphoreType.DMA((count,)),
-            pltpu.SemaphoreType.DMA((count,)),
         ]
-        + [pltpu.SemaphoreType.DMA((MB,))] * 5,
+        + [sems(6, len(plan)), sems(6, len(plan)), sems(2), sems(3), sems(count)]
+        + [sems(MB)] * 5,
         compiler_params=pltpu.CompilerParams(
             collective_id=1, has_side_effects=True, vmem_limit_bytes=VMEM_BYTES
         ),
         name="forward",
-    )(table, x, *shards, *vectors)
-
-
-def norm_parts(summed):
-    row_mean = jnp.mean(summed, axis=-1, keepdims=True)
-    centred = summed - row_mean
-    row_var = jnp.mean(centred * centred, axis=-1, keepdims=True)
-    scale = lax.rsqrt(row_var + EPSILON)
-    return centred * scale, scale
-
-
-def norm_back(grad, unit, scale, gain):
-    inner = grad * gain
-    mean_one = jnp.mean(inner, axis=-1, keepdims=True)
-    mean_two = jnp.mean(inner * unit, axis=-1, keepdims=True)
-    return scale * (inner - mean_one - unit * mean_two)
-
-
-def dot_minor(a, b):
-    return lax.dot_general(a, b, (((1,), (1,)), ((), ())), preferred_element_type=F32)
-
-
-ROW_OUT, ROW_UP, ROW_DOWN, ROW_GAIN_ONE, ROW_SHIFT_ONE, ROW_GAIN_TWO, ROW_SHIFT_TWO = 2, 3, 7, 8, 9, 10, 11
-
-
-def dense_kernel(a_ref, x_ref, cot_ref, small_ref, wo_hbm, wu_hbm, wd_hbm, *refs):
-    out_ref, n_ref, g_ref, do_ref, du_ref, dm_ref, dh_ref, da_ref, vec_ref = refs[:9]
-    wo, wu, wd, slope, n_full, unit, total, wo_sem, wu_sem, wd_sem = refs[9:]
-    lanes = small_ref.shape[2]
-    hidden = g_ref.shape[1]
-    per_half = hidden // 2 // lanes
-    chunks = hidden // lanes
-    loads = [pltpu.make_async_copy(wo_hbm, wo, wo_sem.at[0])]
-    for j in range(chunks):
-        cols = pl.ds(j * lanes, lanes)
-        loads.append(pltpu.make_async_copy(wu_hbm.at[:, cols], wu.at[:, cols], wu_sem.at[j]))
-        loads.append(pltpu.make_async_copy(wd_hbm.at[cols], wd.at[cols], wd_sem.at[j]))
-    for load in loads:
-        load.start()
-
-    def line(row):
-        return jnp.concatenate([small_ref[0, row : row + 1, :], small_ref[1, row : row + 1, :]], axis=1)
-
-    def keep(row, values):
-        summed = jnp.sum(values, axis=0, keepdims=True)
-        for side in range(2):
-            vec_ref[side, row : row + 1, :] = summed[:, side * lanes : (side + 1) * lanes]
-
-    loads[0].wait()
-    h_one = x_ref[...].astype(F32) + (
-        jnp.dot(a_ref[...], wo[...], preferred_element_type=F32) + line(ROW_OUT)
-    )
-    unit_one, scale_one = norm_parts(h_one)
-    unit[...] = unit_one
-    n_one = unit_one * line(ROW_GAIN_ONE) + line(ROW_SHIFT_ONE)
-    n_full[...] = n_one
-    n_ref[...] = n_one.astype(BF16)
-    total[...] = jnp.zeros_like(total)
-
-    def up_and_down(j, carry):
-        at = pl.multiple_of(j * lanes, lanes)
-        cols = pl.ds(at, lanes)
-        pltpu.make_async_copy(wu_hbm.at[:, cols], wu.at[:, cols], wu_sem.at[j]).wait()
-        pltpu.make_async_copy(wd_hbm.at[cols], wd.at[cols], wd_sem.at[j]).wait()
-        bias = small_ref[lax.div(j, per_half), pl.ds(ROW_UP + lax.rem(j, per_half), 1), :]
-        u = jnp.dot(n_ref[...], wu[:, cols], preferred_element_type=F32) + bias
-        below = 0.5 * (1.0 + lax.erf(u * math.sqrt(0.5)))
-        slope[:, cols] = below + u * jnp.exp(-0.5 * u * u) * (1.0 / math.sqrt(2.0 * math.pi))
-        g = (u * below).astype(BF16)
-        g_ref[:, cols] = g
-        total[...] += jnp.dot(g, wd[cols, :], preferred_element_type=F32)
-        return carry
-
-    lax.fori_loop(0, chunks, up_and_down, 0, unroll=True)
-    h_two = n_full[...] + (total[...] + line(ROW_DOWN))
-    unit_two, scale_two = norm_parts(h_two)
-    out_ref[...] = (unit_two * line(ROW_GAIN_TWO) + line(ROW_SHIFT_TWO)).astype(BF16)
-    cot = cot_ref[...].astype(F32)
-    keep(ROW_GAIN_TWO, cot * unit_two)
-    keep(ROW_SHIFT_TWO, cot)
-    dh_two = norm_back(cot, unit_two, scale_two, line(ROW_GAIN_TWO))
-    dm = dh_two.astype(BF16)
-    dm_ref[...] = dm
-    keep(ROW_DOWN, dm.astype(F32))
-    total[...] = dh_two
-
-    def down_and_up(j, carry):
-        cols = pl.ds(pl.multiple_of(j * lanes, lanes), lanes)
-        du = (slope[:, cols] * dot_minor(dm_ref[...], wd[cols, :])).astype(BF16)
-        du_ref[:, cols] = du
-        vec_ref[lax.div(j, per_half), pl.ds(ROW_UP + lax.rem(j, per_half), 1), :] = jnp.sum(
-            du.astype(F32), axis=0, keepdims=True
-        )
-        total[...] += dot_minor(du, wu[:, cols])
-        return carry
-
-    lax.fori_loop(0, chunks, down_and_up, 0, unroll=True)
-    dn = total[...]
-    keep(ROW_GAIN_ONE, dn * unit[...])
-    keep(ROW_SHIFT_ONE, dn)
-    dh_one = norm_back(dn, unit[...], scale_one, line(ROW_GAIN_ONE))
-    dh_ref[...] = dh_one
-    do = dh_one.astype(BF16)
-    do_ref[...] = do
-    keep(ROW_OUT, do.astype(F32))
-    da_ref[...] = dot_minor(do, wo[...]).astype(BF16)
-    for side in range(2):
-        vec_ref[side, 0:ROW_OUT, :] = jnp.zeros((ROW_OUT, lanes), F32)
-
-
-def dense(a, x, cot, small, wo, wu, wd):
-    vmem, anywhere = pl.BlockSpec(memory_space=pltpu.VMEM), pl.BlockSpec(memory_space=pl.ANY)
-    rows, width = x.shape
-    hidden = wu.shape[1]
-    chunks = hidden // small.shape[2]
-    low = lambda cols: jax.ShapeDtypeStruct((rows, cols), BF16)
-    full = lambda cols: pltpu.VMEM((rows, cols), F32)
-    return pl.pallas_call(
-        dense_kernel,
-        out_shape=[
-            low(width),
-            low(width),
-            low(hidden),
-            low(width),
-            low(hidden),
-            low(width),
-            jax.ShapeDtypeStruct((rows, width), F32),
-            low(width),
-            jax.ShapeDtypeStruct(small.shape, F32),
-        ],
-        in_specs=[vmem] * 4 + [anywhere] * 3,
-        out_specs=[vmem] * 9,
-        scratch_shapes=[pltpu.VMEM(item.shape, BF16) for item in (wo, wu, wd)]
-        + [full(hidden), full(width), full(width), full(width)]
-        + [pltpu.SemaphoreType.DMA((n,)) for n in (1, chunks, chunks)],
-        compiler_params=pltpu.CompilerParams(vmem_limit_bytes=VMEM_BYTES),
-        name="dense",
-    )(a, x, cot, small, wo, wu, wd)
+    )(table, x, cot, *shards, *vectors)
 
 
 ORDERS = (
@@ -1356,10 +1314,8 @@
     at_block = dealing[0][:, :, None] == blocks[None, None, :]
     slot_of = jnp.sum(jnp.where(at_block, blocks[None, :, None], 0), axis=1)
     table = jnp.concatenate([lengths[0], dealing[0], slot_of], axis=1)
-    *wholes, small_whole, a, kept, lse = forward(table, x, weights, vectors, HEADS)
-    query_w, key_w, value_w, out_w, up_w, down_w = wholes
-    output, n_low, g, do, du, dm, dh_one, da, vec = dense(
-        a, x, cotangent.reshape(rows, width), small_whole, out_w, up_w, down_w
+    query_w, key_w, value_w, kept, lse, a, output, n_low, g, do, du, dm, dh_one, da, vec = forward(
+        table, x, cotangent.reshape(rows, width), weights, vectors, HEADS
     )
     grad_tokens, o_a, o_b, o_c, vec_sum = backward(
         table,

time: 320 us -> 311 us (0.972)
  Pallas kernels: 316 us -> 307 us
    pallas_call x1 -> x0, Pallas kernels: 22.2 us -> none  [dense(): pl.pallas_call(dense_kernel, out_shape=[low(width), low(width), low(hidde...]
    pallas_call x1, Pallas kernels: 89.2 us -> 102 us  [forward(): pl.pallas_call(functools.partial(forward_kernel, heads, plan, count, len(...]
where the time goes in v7:
time: 311 us
  Pallas kernels  307 us (99%)
    pallas_call x1, Pallas kernels, backward(): pl.pallas_call(functools.partial(backward_kernel, heads), out_shape=[jax....  190 us
    pallas_call x1, Pallas kernels, forward(): pl.pallas_call(functools.partial(forward_kernel, heads, plan, count, len(...  102 us
    pallas_call x1, Pallas kernels, widen(): pl.pallas_call(widen_kernel, grid=(shards,), out_shape=[jax.ShapeDtypeStr...  14 us

profile of v7, /device:TPU:0, one launch (start us, length us, event | category | flops | bytes accessed | tf_op | source)
XLA Modules:
  0.0 311.0 jit_solution(6405245181894544043)
XLA Ops:
  0.7 0.8 copy.37
  1.4 0.7 copy.40
  2.1 0.1 select_reduce_fusion
  2.2 0.7 pad_add_fusion.refs_0_
  2.9 102.1 %forward.1 = (bf16[1024,1024]{1,0:T(8,128)(2,1)}, bf16[1024,1024]{1,0:T(8,128)(2,1)}, bf16[1024,1024]{1,0:T(8,128)(2,1)}, bf16[3,16,96,128]{3,2,1,0:T(8,128)(2,1...) custom-call(s32[3,34]{1,0:T(4,128)} %pad_add_fusion.refs_0_, ...), custom_call_target="tpu_custom_call" | custom-call | tf_op jit(solution)/shard_map/forward/pallas_call | solution.py:798
  105.0 190.5 %backward.1 = (bf16[192,1024]{1,0:T(8,128)(2,1)}, bf16[2,8,64,2048]{3,2,1,0:T(8,128)(2,1)}, bf16[2,8,64,2048]{3,2,1,0:T(8,128)(2,1)}, bf16[2,8,128,1024]{3,2,1,0:T(8,128)(2,1)}, f32[12,512]{1,0:T(8,128)}) custom-call(s32[3,34]{1,0:T(4,128)} %pad_add_fusion.refs_0_, bf16[192,1024]{1,0:T(8,128)(2,1)} %get-tuple-element.53.refs_1_, ...), custom_call_target="tpu_custom_call" | custom-call | tf_op jit(solution)/shard_map/backward/pallas_call | solution.py:1244
  295.5 0.0 copy-start
  295.5 0.0 copy-start.1
  295.5 14.0 %widen.1 = (f32[512,1024]{1,0:T(8,128)}, f32[512,1024]{1,0:T(8,128)}, f32[512,1024]{1,0:T(8,128)}, f32[512,1024]{1,0:T(8,128)}, f32[512,4096]{1,0:T(8,128)}, /*i...) custom-call(bf16[2,8,64,2048]{3,2,1,0:T(8,128)(2,1)} %get-tuple-elem, ...), custom_call_target="tpu_custom_call" | custom-call | tf_op jit(solution)/shard_map/widen/pallas_call | solution.py:1291
  309.5 0.0 copy-done
  309.5 0.7 copy.43
  310.2 0.0 copy-done.1
  310.3 0.7 copy.44
Async XLA Ops:
  295.5 14.0 %copy-start = (bf16[192,1024]{1,0:T(8,128)(2,1)S(1)}, bf16[192,1024]{1,0:T(8,128)(2,1)}, u32[]{:S(2)}) copy-start(bf16[192,1024]{1,0:T(8,128)(2,1)} %get-tuple-element.52) | copy-start | bytes 1179652
  295.5 14.8 %copy-start.1 = (bf16[192,1024]{1,0:T(8,128)(2,1)S(1)}, bf16[192,1024]{1,0:T(8,128)(2,1)}, u32[]{:S(2)}) copy-start(bf16[192,1024]{1,0:T(8,128)(2,1)} %get-tuple-element.67) | copy-start | bytes 1179652

commit v8 on v7

--- a/solution.py
+++ b/solution.py
@@ -465,8 +465,21 @@
 ROW_OUT, ROW_UP, ROW_DOWN, ROW_GAIN_ONE, ROW_SHIFT_ONE, ROW_GAIN_TWO, ROW_SHIFT_TWO = 2, 3, 7, 8, 9, 10, 11
 
 
-SQUARE, PAIR, ALONE = 8, 4, 2
-WAYS = (SQUARE,) * 3 + (SQUARE,) * 4 + (PAIR,) * 3 + (ALONE,) * 2
+SQUARE, PAIR_Y, PAIR_Z, ALONE = (8, "yz"), (4, "y"), (4, "z"), (2, "")
+WAYS = (
+    SQUARE, SQUARE, SQUARE, SQUARE, PAIR_Y, SQUARE, PAIR_Z, PAIR_Y, ALONE, PAIR_Z, PAIR_Y, ALONE,
+)
+SEND_ORDER = (2, 0, 1, 3, 5, 7, 4, 6, 9, 10, 8, 11)
+FORWARD_SCHEDULE = (
+    ("second", 2), ("second", 0), ("third", 2), ("second", 1), ("third", 0), ("fourth", 2),
+    ("third", 1), ("second", 3), ("second", 5), ("fourth", 0), ("project", 2), ("fourth", 1),
+    ("project", 0), ("project", 1), ("pack", 0), ("second", 7), ("third", 3), ("second", 4),
+    ("second", 6), ("att", 0), ("fourth", 7), ("third", 5), ("fourth", 3), ("att", 1), ("att",
+    2), ("fourth", 5), ("fourth", 8), ("second", 10), ("second", 9), ("fourth", 6), ("fourth",
+    4), ("rows", 0), ("out", 0), ("hidden", 0), ("fourth", 10), ("hidden", 1), ("hidden", 2),
+    ("fourth", 9), ("hidden", 3), ("hidden", 4), ("fourth", 11), ("hidden", 5), ("hidden", 6),
+    ("hidden", 7),
+)
 
 
 def weight_plan(shards):
@@ -477,21 +490,6 @@
         for part in range(parts):
             plan.append((index, part * (rows // parts), rows // parts, WAYS[len(plan)]))
     return plan
-
-
-def forward_schedule():
-    squares = [i for i, way in enumerate(WAYS) if way == SQUARE and i > 2]
-    pairs = [i for i, way in enumerate(WAYS) if way == PAIR]
-    alone = [i for i, way in enumerate(WAYS) if way == ALONE]
-    events = [("second", i) for i in squares + pairs[:1]] + [("att", 0)]
-    events += [("third", i) for i in squares] + [("second", i) for i in pairs[1:2]] + [("att", 1)]
-    events += [("fourth", i) for i in squares] + [("second", i) for i in pairs[2:3]] + [("att", 2)]
-    events += [("fourth", i) for i in pairs[:2]] + [("rows", 0)]
-    events += [("fourth", i) for i in pairs[2:] + alone] + [("out", 0)]
-    return events + [("hidden", t) for t in range(8)]
-
-
-FORWARD_SCHEDULE = forward_schedule()
 
 
 def forward_kernel(heads, plan, n_weights, n_vectors, *refs):
@@ -544,7 +542,7 @@
     def part(chunk, side, piece, start, count):
         tensor, first, rows, way = plan[chunk]
         half = shards[tensor].shape[0]
-        at = side * half + first + piece * (rows // way) + start
+        at = side * half + first + piece * (rows // way[0]) + start
         return near[tensor].at[pl.ds(pl.multiple_of(at, 8), count)]
 
     steps = {}
@@ -553,24 +551,30 @@
         return w_send.at[kind, chunk], w_recv.at[kind, chunk]
 
     def own_piece(way):
-        return {SQUARE: core * 4 + z * 2 + y, PAIR: core * 2 + y, ALONE: core}[way]
-
-    for chunk, (tensor, first, rows, way) in enumerate(plan):
-        size, mine = rows // way, own_piece(way)
+        return {
+            SQUARE: core * 4 + z * 2 + y,
+            PAIR_Y: core * 2 + y,
+            PAIR_Z: core * 2 + z,
+            ALONE: core,
+        }[way]
+
+    for chunk in SEND_ORDER:
+        tensor, first, rows, way = plan[chunk]
+        size, mine = rows // way[0], own_piece(way)
         src = shards[tensor].at[pl.ds(pl.multiple_of(first + mine * size, 8), size)]
         steps[chunk, 0] = send(src, part(chunk, w, mine, 0, size), *sem(0, chunk), by_x)
 
     def second(chunk):
         _, _, rows, way = plan[chunk]
         steps[chunk, 0].wait_recv()
-        ref = part(chunk, o, own_piece(way), 0, rows // way)
-        steps[chunk, 1] = send(ref, ref, *sem(1, chunk), by_y)
-        if way == SQUARE:
-            steps[chunk, 2] = send(ref, ref, *sem(2, chunk), by_z)
+        ref = part(chunk, o, own_piece(way), 0, rows // way[0])
+        for name in way[1]:
+            kind, peer = {"y": (1, by_y), "z": (2, by_z)}[name]
+            steps[chunk, kind] = send(ref, ref, *sem(kind, chunk), peer)
 
     def third(chunk):
         _, _, rows, way = plan[chunk]
-        size = rows // way
+        size = rows // way[0]
         steps[chunk, 1].wait_recv()
         steps[chunk, 2].wait_recv()
         ref = part(chunk, o, core * 4 + (1 - z) * 2 + y, 0, size // 2)
@@ -580,31 +584,31 @@
 
     def fourth(chunk):
         _, _, rows, way = plan[chunk]
-        for kind in {SQUARE: (3, 4), PAIR: (1,), ALONE: (0,)}[way]:
+        for kind in {SQUARE: (3, 4), PAIR_Y: (1,), PAIR_Z: (2,), ALONE: (0,)}[way]:
             steps[chunk, kind].wait_recv()
-        ref = part(chunk, o, core * (way // 2), 0, rows // 2)
+        ref = part(chunk, o, core * (way[0] // 2), 0, rows // 2)
         steps[chunk, 5] = send(ref, ref, *sem(5, chunk), by_core)
 
-    for index in range(3):
-        staged[index].wait()
-    for turn in range(5):
-        for stage, act in enumerate((second, third, fourth)):
-            if 0 <= turn - stage < 3:
-                act(turn - stage)
-    small_sent.wait()
-    small_whole[w] = small[...]
-    small_whole[o] = small_in[...]
-    for side in range(2):
-        for row in range(2):
-            bias[row : row + 1, side * lanes : (side + 1) * lanes] = small_whole[
-                side, row : row + 1, :
-            ]
     width = x_ref.shape[1]
     step = 256
-    for index, (weight, out) in enumerate(zip(near, (q_ref, k_ref, v_ref))):
+    projected = []
+
+    def project(index):
+        if not projected:
+            small_sent.wait()
+            small_whole[w] = small[...]
+            small_whole[o] = small_in[...]
+            for side in range(2):
+                for row in range(2):
+                    bias[row : row + 1, side * lanes : (side + 1) * lanes] = small_whole[
+                        side, row : row + 1, :
+                    ]
+        projected.append(index)
+        staged[index].wait()
         steps[index, 5].wait_recv()
-
-        def project(turn, carry):
+        weight, out = near[index], (q_ref, k_ref, v_ref)[index]
+
+        def some_columns(turn, carry):
             cols = pl.ds(pl.multiple_of(turn * step, step), step)
             product = jnp.dot(x_ref[...], weight[:, cols], preferred_element_type=F32)
             if index != 1:
@@ -612,15 +616,19 @@
             out[:, cols] = product.astype(BF16)
             return carry
 
-        lax.fori_loop(0, width // step, project, 0)
-    for m in range(MB):
-        for pair in range(heads // 2):
-            pack_three(q_ref, k_ref, v_ref, m * BLK, pair, out_buf.at[m])
-        for peer in peers:
-            send(out_buf.at[m, peer[0]], in_buf[m].at[c], send_sem.at[m], recv_sem.at[m], peer)
-        in_buf[m][c] = out_buf[m, c]
-    for index in range(3):
+        lax.fori_loop(0, width // step, some_columns, 0)
         pltpu.make_async_copy(near[index], wholes[index], local_sem.at[index]).start()
+
+    def pack(_):
+        for m in range(MB):
+            for pair in range(heads // 2):
+                pack_three(q_ref, k_ref, v_ref, m * BLK, pair, out_buf.at[m])
+            for peer in peers:
+                send(
+                    out_buf.at[m, peer[0]], in_buf[m].at[c], send_sem.at[m], recv_sem.at[m], peer
+                )
+            in_buf[m][c] = out_buf[m, c]
+
     blocks = heads
     span = BPS * BLK
 
@@ -733,6 +741,8 @@
         "second": second,
         "third": third,
         "fourth": fourth,
+        "project": project,
+        "pack": pack,
         "att": attention,
         "rows": come_back,
         "out": out_project,
@@ -839,21 +849,23 @@
 
 
 ORDERS = (
-    ("yxzZ", "xyzZ", "zxyZ", "yxzZ"),
-    ("xzyZ", "zyxZ", "xyzZ", "yzxZ"),
-    ("xyzZ", "zxyZ", "yxzZ", "xyzZ"),
+    ("xyzZ", "xyzZ", "yxzZ", "xyzZ"),
+    ("yzxZ", "xZyz", "zxyZ", "xyzZ"),
+    ("yxzZ", "xyZz", "zyxZ", "xyzZ"),
 )
 PIECES = len(ORDERS[0])
+SCHEDULE = (
+    "up", 0, 1, 2, "down", (1, 3), "back", (1, 1), (2, 0), (2, 1), "qkv", (1, 3), (2, 1),
+    (1, 1), (1, 3), (2, 0), (2, 3), (1, 0), (2, 1), (1, 3), "vec", (2, 0), (2, 1), (0, 0),
+    (1, 1), (2, 3), (2, 2), (2, 1), (2, 3), (1, 0), (2, 0), (1, 1), (1, 3), (2, 1), "vec",
+    (2, 2), (0, 0), (0, 1), (1, 2), (2, 0), (0, 2), (0, 3), (0, 0), (2, 3), (2, 0), (1, 0),
+    (0, 1), (2, 3), "vec", (2, 2), (1, 0), (1, 2), (2, 3), (0, 1), (0, 3), (0, 0), (1, 2),
+    (1, 0), (2, 1), (0, 3), (0, 2), (0, 1), "vec", (1, 3), (2, 3), (1, 2), (1, 0), (1, 1),
+    (0, 0), (0, 2), (0, 3), "rows", (0, 1), (2, 0), (1, 2), (0, 0), (2, 2), (1, 0), (0, 2),
+    "vec", (0, 3), (2, 2), (0, 2), (0, 1), (1, 3), (1, 1), (0, 3), (0, 2), (0, 0), (2, 2),
+    (0, 1), (1, 2), (1, 1), (2, 2), (0, 3), (1, 2), (0, 2),
+)
 KEYS = tuple((part, piece) for part in range(3) for piece in range(PIECES))
-
-
-def default_schedule():
-    early = [(part, piece) for piece in range(PIECES) for part in (1, 2)]
-    late = [(0, piece) for piece in range(PIECES)]
-    events = ["up", 0, "down", 1, 2] + early + ["back", "qkv", "rows"]
-    for step in range(6):
-        events += early + ["vec"] + late
-    return events + late
 
 
 def landing_shapes(order, shape):
@@ -947,7 +959,7 @@
     share("x", x_ref, m_x)
 
     sums, outs = (s_a, s_b, s_c), (o_a, o_b, o_c)
-    wide = 256
+    wide = 512
 
     def tile(pairs, out, first, count):
         def body(turn, carry):
@@ -1199,19 +1211,6 @@
         if kind >= 3:
             flight.wait_recv()
         flight.wait_send()
-
-
-SCHEDULE = (
-    "down", 0, "up", 1, 2, (2, 0), (1, 3), (1, 1), (2, 2), (1, 0), (2, 0), (1, 3), (1, 2),
-    "back", (2, 2), (2, 0), (2, 3), (1, 2), (1, 3), "qkv", (1, 3), (2, 3), (1, 2), (1, 3),
-    (1, 1), (2, 2), (2, 0), (1, 1), "vec", (2, 1), (2, 2), (2, 0), (2, 1), (0, 1), (1, 3),
-    (2, 2), (1, 2), (2, 3), (0, 0), (2, 1), (1, 0), "vec", (2, 3), (0, 3), (0, 0), (2, 2),
-    (2, 1), (0, 3), (2, 0), (1, 3), (1, 1), (2, 1), (0, 2), "vec", (1, 2), (2, 3), (1, 0),
-    (1, 1), (0, 1), (0, 3), (0, 0), (2, 1), (1, 0), (2, 0), (2, 2), (0, 2), "vec", (0, 3),
-    (0, 1), (1, 2), (0, 3), (0, 2), (2, 3), "rows", (0, 0), (1, 0), (1, 1), (0, 2), (0, 0),
-    (0, 3), (0, 1), "vec", (0, 2), (0, 1), (1, 0), (0, 0), (1, 2), (0, 1), (0, 2), (0, 3),
-    (0, 0), (0, 1), (1, 1), (2, 3), (1, 0), (2, 1), (0, 2),
-)
 
 
 def backward(table, da, kept, lse, x, a, n1, g, do, du, dm, vec, dh, weights, heads):

time: 311 us -> 285 us (0.916)
  Pallas kernels: 307 us -> 280 us
    pallas_call x1, Pallas kernels: 190 us -> 177 us  [backward(): pl.pallas_call(functools.partial(backward_kernel, heads), out_shape=[jax....]
    pallas_call x1, Pallas kernels: 102 us -> 89.5 us  [forward(): pl.pallas_call(functools.partial(forward_kernel, heads, plan, count, len(...]
where the time goes in v8:
time: 285 us; the launch traced here: 284 us
  Pallas kernels  280 us (98%)
  local copies, waits for them, and re-layouts  2.95 us (1%)
    pallas_call x1, Pallas kernels, backward(): pl.pallas_call(functools.partial(backward_kernel, heads), out_shape=[jax....  177 us
    pallas_call x1, Pallas kernels, forward(): pl.pallas_call(functools.partial(forward_kernel, heads, plan, count, len(...  89.5 us
    pallas_call x1, Pallas kernels, widen(): pl.pallas_call(widen_kernel, grid=(shards,), out_shape=[jax.ShapeDtypeStr...  14 us

profile of v8, /device:TPU:0, one launch (start us, length us, event | category | flops | bytes accessed | tf_op | source)
XLA Modules:
  0.0 284.4 jit_solution(12432303401965495119)
XLA Ops:
  0.7 0.8 copy.37
  1.4 0.7 copy.40
  2.1 0.1 select_reduce_fusion
  2.2 0.7 pad_add_fusion.refs_0_
  2.9 89.5 %forward.1 = (bf16[1024,1024]{1,0:T(8,128)(2,1)}, bf16[1024,1024]{1,0:T(8,128)(2,1)}, bf16[1024,1024]{1,0:T(8,128)(2,1)}, bf16[3,16,96,128]{3,2,1,0:T(8,128)(2,1...) custom-call(s32[3,34]{1,0:T(4,128)} %pad_add_fusion.refs_0_, ...), custom_call_target="tpu_custom_call" | custom-call | tf_op jit(solution)/shard_map/forward/pallas_call | solution.py:808
  92.4 176.5 %backward.1 = (bf16[192,1024]{1,0:T(8,128)(2,1)}, bf16[2,8,64,2048]{3,2,1,0:T(8,128)(2,1)}, bf16[2,8,64,2048]{3,2,1,0:T(8,128)(2,1)}, bf16[2,8,128,1024]{3,2,1,0:T(8,128)(2,1)}, f32[12,512]{1,0:T(8,128)}) custom-call(s32[3,34]{1,0:T(4,128)} %pad_add_fusion.refs_0_, bf16[192,1024]{1,0:T(8,128)(2,1)} %get-tuple-element.53.refs_1_, ...), custom_call_target="tpu_custom_call" | custom-call | tf_op jit(solution)/shard_map/backward/pallas_call | solution.py:1243
  268.9 0.0 copy-start
  268.9 0.0 copy-start.1
  268.9 14.0 %widen.1 = (f32[512,1024]{1,0:T(8,128)}, f32[512,1024]{1,0:T(8,128)}, f32[512,1024]{1,0:T(8,128)}, f32[512,1024]{1,0:T(8,128)}, f32[512,4096]{1,0:T(8,128)}, /*i...) custom-call(bf16[2,8,64,2048]{3,2,1,0:T(8,128)(2,1)} %get-tuple-elem, ...), custom_call_target="tpu_custom_call" | custom-call | tf_op jit(solution)/shard_map/widen/pallas_call | solution.py:1290
  282.9 0.0 copy-done
  282.9 0.7 copy.43
  283.7 0.0 copy-done.1
  283.7 0.7 copy.44
Async XLA Ops:
  268.9 14.0 %copy-start = (bf16[192,1024]{1,0:T(8,128)(2,1)S(1)}, bf16[192,1024]{1,0:T(8,128)(2,1)}, u32[]{:S(2)}) copy-start(bf16[192,1024]{1,0:T(8,128)(2,1)} %get-tuple-element.52) | copy-start | bytes 1179652
  268.9 14.8 %copy-start.1 = (bf16[192,1024]{1,0:T(8,128)(2,1)S(1)}, bf16[192,1024]{1,0:T(8,128)(2,1)}, u32[]{:S(2)}) copy-start(bf16[192,1024]{1,0:T(8,128)(2,1)} %get-tuple-element.67) | copy-start | bytes 1179652

commit v9 on v8

--- a/solution.py
+++ b/solution.py
@@ -849,27 +849,27 @@
 
 
 ORDERS = (
-    ("xyzZ", "xyzZ", "yxzZ", "xyzZ"),
-    ("yzxZ", "xZyz", "zxyZ", "xyzZ"),
-    ("yxzZ", "xyZz", "zyxZ", "xyzZ"),
+    ("yxzZ", "xyzZ", "xyzZ", "xyzZ"),
+    ("xzyZ", "xyzZ", "yxzZ", "zxyZ"),
+    ("yZz", "yzZ", "yZz", "zyZ"),
 )
 PIECES = len(ORDERS[0])
 SCHEDULE = (
-    "up", 0, 1, 2, "down", (1, 3), "back", (1, 1), (2, 0), (2, 1), "qkv", (1, 3), (2, 1),
-    (1, 1), (1, 3), (2, 0), (2, 3), (1, 0), (2, 1), (1, 3), "vec", (2, 0), (2, 1), (0, 0),
-    (1, 1), (2, 3), (2, 2), (2, 1), (2, 3), (1, 0), (2, 0), (1, 1), (1, 3), (2, 1), "vec",
-    (2, 2), (0, 0), (0, 1), (1, 2), (2, 0), (0, 2), (0, 3), (0, 0), (2, 3), (2, 0), (1, 0),
-    (0, 1), (2, 3), "vec", (2, 2), (1, 0), (1, 2), (2, 3), (0, 1), (0, 3), (0, 0), (1, 2),
-    (1, 0), (2, 1), (0, 3), (0, 2), (0, 1), "vec", (1, 3), (2, 3), (1, 2), (1, 0), (1, 1),
-    (0, 0), (0, 2), (0, 3), "rows", (0, 1), (2, 0), (1, 2), (0, 0), (2, 2), (1, 0), (0, 2),
-    "vec", (0, 3), (2, 2), (0, 2), (0, 1), (1, 3), (1, 1), (0, 3), (0, 2), (0, 0), (2, 2),
-    (0, 1), (1, 2), (1, 1), (2, 2), (0, 3), (1, 2), (0, 2),
+    "up", 0, 1, (1, 2), 2, "down", "back", (2, 0), (1, 0), (2, 3), "qkv", (2, 1), (1, 3),
+    (2, 2), (1, 1), (1, 2), (2, 0), (2, 1), (1, 0), (2, 3), "vec", (2, 2), (2, 0), (2, 1),
+    (2, 2), (1, 2), (0, 1), (2, 1), (2, 3), (1, 2), (2, 2), (2, 1), (0, 0), "vec", (0, 2),
+    (1, 0), (2, 0), (1, 2), (2, 3), (0, 1), (1, 1), (0, 3), (2, 1), (0, 2), (0, 1), (1, 1),
+    "vec", (1, 3), (0, 2), (0, 3), (2, 0), (1, 1), (0, 2), (0, 0), (1, 2), (2, 2), (0, 3),
+    (1, 1), (1, 3), (0, 0), "vec", (0, 1), (1, 2), (0, 2), (0, 3), (1, 1), (1, 0), (0, 1),
+    (0, 0), (2, 0), (0, 2), (0, 3), (1, 3), (2, 3), (0, 1), (1, 3), "vec", (1, 1), (0, 0),
+    (0, 2), (1, 0), (0, 3), (1, 3), (1, 0), (2, 3), (0, 0), (0, 3), "rows", (1, 3), (0, 1),
+    (2, 2), (1, 0), (0, 0),
 )
 KEYS = tuple((part, piece) for part in range(3) for piece in range(PIECES))
 
 
 def landing_shapes(order, shape):
-    shards, sides, shapes = 8, 2, []
+    shards, sides, shapes = 8, shape[0], []
     for name in order:
         if name == "x":
             sides = 1
@@ -896,10 +896,14 @@
     in_buf = refs[:MB]
     out_buf, back_out, back_in, q_s, k_s, v_s, a_s, dq_s, dk_s, dv_s = refs[MB : MB + 10]
     refs = refs[MB + 10 :]
-    dq_ref, dk_ref, dv_ref, m_x, m_a, m_n, m_dm, m_do, m_du, m_g, m_dqkv = refs[:11]
-    near, (vec_s, v_recv, v_sum, s_a, s_b, s_c) = refs[11:14], refs[14:20]
-    refs = refs[20:]
-    r_bufs = {key: refs[4 * i : 4 * i + 4] for i, key in enumerate(KEYS)}
+    dq_ref, dk_ref, dv_ref, m_x, m_a, m_n, m_do, m_du, m_dqkv, m_g, m_dm = refs[:11]
+    far_g, far_dm, cross_g, cross_dm = refs[11:15]
+    near, (vec_s, v_recv, v_sum, s_a, s_b, s_c) = refs[15:18], refs[18:24]
+    refs = refs[24:]
+    r_bufs = {}
+    for part, piece in KEYS:
+        size = len(ORDERS[part][piece])
+        r_bufs[part, piece], refs = refs[:size], refs[size:]
     (
         send_sem,
         recv_sem,
@@ -915,7 +919,7 @@
         own_sem,
         v_send_sem,
         v_recv_sem,
-    ) = refs[4 * len(KEYS) :]
+    ) = refs
     c, x = lax.axis_index("ctx"), lax.axis_index("wsh")
     core, y, z, zz = bit_of(c, 1), bit_of(c, 2), bit_of(c, 4), bit_of(c, 8)
     by_core = (flip(c, 1), x)
@@ -926,7 +930,8 @@
     width, hidden = da_ref.shape[1], g_ref.shape[1]
     for index, weight in enumerate(weights):
         pltpu.make_async_copy(weight, near[index], near_sem.at[index]).start()
-    greet(peers + [by["x"]])
+    by_cross = (flip(c, 1), 1 - x)
+    greet(peers + [by["x"], by_cross])
 
     for m in range(MB):
         row = slice(m * BLK, (m + 1) * BLK)
@@ -940,19 +945,22 @@
 
     shared = {}
 
-    def share(name, src, dst):
+    def share(name, src, dst, peer=by_core):
         index = len(shared)
-        shared[name] = send(src, dst, mate_send.at[index], mate_recv.at[index], by_core)
+        shared[name] = send(src, dst, mate_send.at[index], mate_recv.at[index], peer)
 
     other = 1 - core
+    quarter = hidden // 4
+
+    def hidden_rows(side, which):
+        return g_ref.at[:, lanes_at(side * 2 * quarter + which * quarter, quarter)]
+
+    share("far_g", hidden_rows(1 - x, core), far_g, by["x"])
+    share("far_dm", dm_ref, far_dm, by["x"])
+    share("cross_g", hidden_rows(1 - x, other), cross_g, by_cross)
     share("n", n_ref, m_n)
     share("du", du_ref.at[:, lanes_at(other * (hidden // 2), hidden // 2)], m_du)
-    for half in range(2):
-        share(
-            "g" + str(half),
-            g_ref.at[:, lanes_at(half * (hidden // 2) + other * (hidden // 4), hidden // 4)],
-            m_g.at[:, pl.ds(half * (hidden // 4), hidden // 4)],
-        )
+    share("g", hidden_rows(x, other), m_g)
     share("dm", dm_ref, m_dm)
     share("a", a_ref, m_a)
     share("do", do_ref.at[:, lanes_at(other * (width // 2), width // 2)], m_do)
@@ -978,13 +986,13 @@
         tile(((n_ref, du_ref, core * half), (m_n, m_du, 0)), s_b, 0, half // wide)
 
     def grads_down():
-        for name in ("g0", "g1", "dm"):
+        shared["far_dm"].wait_recv()
+        share("cross_dm", far_dm, cross_dm)
+        for name in ("g", "dm", "far_g", "cross_g", "cross_dm"):
             shared[name].wait_recv()
-        quarter = hidden // 4
-        for half in range(2):
-            mine = g_ref.at[:, lanes_at(half * 2 * quarter + core * quarter, quarter)]
-            others = m_g.at[:, pl.ds(half * quarter, quarter)]
-            tile(((mine, dm_ref, 0), (others, m_dm, 0)), s_c.at[half], 0, width // wide)
+        pairs = ((hidden_rows(x, core), dm_ref, 0), (m_g, m_dm, 0))
+        pairs += ((far_g, far_dm, 0), (cross_g, cross_dm, 0))
+        tile(pairs, s_c.at[0], 0, width // wide)
 
     def grads_qkv():
         half = width // 2
@@ -1094,7 +1102,8 @@
 
     plans, gathers = {}, {}
     for key in KEYS:
-        first, count, sided = 0, 8, False
+        alone = sums[key[0]].shape[0] == 1
+        first, count, sided = 0, 8, alone
         plans[key], back = [], []
         for name in ORDERS[key[0]][key[1]]:
             if name == "x":
@@ -1103,7 +1112,7 @@
                 continue
             count //= 2
             out, keep = first + (1 - bits[name]) * count, first + bits[name] * count
-            side = x if sided else None
+            side = (0 if alone else x) if sided else None
             plans[key].append((by[name], side, side, out, keep, count))
             back.append((by[name], keep, out, count))
             first = keep
@@ -1146,22 +1155,23 @@
         spread[key, kind] = send(src, dst, *sems, peer)
 
     def advance(key):
-        step = state[key]
+        step, steps = state[key], len(plans[key])
         out, rows = outs[key[0]], piece_rows(key)
-        if step < 4:
+        if step < steps:
             reduce_add(key, step)
-            if step < 3:
+            if step < steps - 1:
                 reduce_send(key, step + 1)
                 return
             peer, first, _, _ = gathers[key][0]
-            src = sums[key[0]].at[x, pl.ds(first, 1), rows]
+            side = x if sums[key[0]].shape[0] == 2 else 0
+            src = sums[key[0]].at[side, pl.ds(first, 1), rows]
             dst = out.at[core, pl.ds(first, 1), rows]
             owns[key] = pltpu.make_async_copy(src, dst, own_sem.at[key[0], key[1]])
             owns[key].start()
             spread_send(key, 0, src, dst, peer)
             spread_send(key, 3, src, dst, by_core)
         else:
-            turn = step - 3
+            turn = step - steps + 1
             spread[key, turn - 1].wait_recv()
             if turn == 1:
                 owns[key].wait()
@@ -1221,15 +1231,15 @@
     pack_rows = BLK + BLK // 2
     low = lambda *dims: pltpu.VMEM(dims, BF16)
     a_shape, b_shape = (2, 8, width // 16, 2 * width), (2, 8, width // 16, hidden // 2)
-    c_shape = (2, 8, hidden // 32, width)
+    c_shape = (1, 8, hidden // 32, width)
     scratch = [low(heads, BLK // 2, 128)] * MB
     scratch += [low(MB, heads, BLK // 2, 128)]
     scratch += [low(MB, heads, pack_rows, 128)] * 2
     scratch += [low(heads * BLK, HD)] * 4
     scratch += [pltpu.VMEM((heads, BLK, HD), F32)] * 3
-    scratch += [low(rows, width)] * 7
-    scratch += [low(rows, width // 2), low(rows, hidden // 2), low(rows, hidden // 2)]
-    scratch += [low(rows, 3 * width // 2)]
+    scratch += [low(rows, width)] * 6
+    scratch += [low(rows, width // 2), low(rows, hidden // 2), low(rows, 3 * width // 2)]
+    scratch += [low(rows, hidden // 4), low(rows, width)] * 3
     scratch += [low(*item.shape) for item in weights]
     scratch += [pltpu.VMEM(vec.shape, F32)] + [pltpu.VMEM((5,) + vec.shape[1:], F32)] * 2
     scratch += [low(*shape) for shape in (a_shape, b_shape, c_shape)]
@@ -1237,7 +1247,7 @@
         shape = (a_shape, b_shape, c_shape)[key[0]]
         scratch += [low(*item) for item in landing_shapes(ORDERS[key[0]][key[1]], shape)]
     sems = lambda *dims: pltpu.SemaphoreType.DMA(dims)
-    scratch += [sems(MB)] * 4 + [sems(11)] * 2 + [sems(3)]
+    scratch += [sems(MB)] * 4 + [sems(14)] * 2 + [sems(3)]
     scratch += [sems(3, PIECES, 4)] * 2 + [sems(3, PIECES, 7)] * 2 + [sems(3, PIECES)]
     scratch += [sems(5)] * 2
     return pl.pallas_call(
@@ -1246,7 +1256,7 @@
             jax.ShapeDtypeStruct((rows, width), BF16),
             jax.ShapeDtypeStruct(a_shape, BF16),
             jax.ShapeDtypeStruct(b_shape, BF16),
-            jax.ShapeDtypeStruct(c_shape, BF16),
+            jax.ShapeDtypeStruct((2,) + c_shape[1:], BF16),
             jax.ShapeDtypeStruct(vec.shape[1:], F32),
         ],
         in_specs=[smem] + [vmem] * 12 + [anywhere] * 3,

time: 285 us -> 277 us (0.972)
  Pallas kernels: 280 us -> 272 us
    pallas_call x1, Pallas kernels: 177 us -> 168 us  [backward(): pl.pallas_call(functools.partial(backward_kernel, heads), out_shape=[jax....]
where the time goes in v9:
time: 277 us; the launch traced here: 276 us
  Pallas kernels  272 us (98%)
  local copies, waits for them, and re-layouts  2.95 us (1%)
    pallas_call x1, Pallas kernels, backward(): pl.pallas_call(functools.partial(backward_kernel, heads), out_shape=[jax....  168 us
    pallas_call x1, Pallas kernels, forward(): pl.pallas_call(functools.partial(forward_kernel, heads, plan, count, len(...  89.5 us
    pallas_call x1, Pallas kernels, widen(): pl.pallas_call(widen_kernel, grid=(shards,), out_shape=[jax.ShapeDtypeStr...  14 us

profile of v9, /device:TPU:0, one launch (start us, length us, event | category | flops | bytes accessed | tf_op | source)
XLA Modules:
  0.0 276.1 jit_solution(17983051241080431866)
XLA Ops:
  0.7 0.8 copy.37
  1.4 0.7 copy.40
  2.1 0.1 select_reduce_fusion
  2.2 0.7 pad_add_fusion.refs_0_
  2.9 89.5 %forward.1 = (bf16[1024,1024]{1,0:T(8,128)(2,1)}, bf16[1024,1024]{1,0:T(8,128)(2,1)}, bf16[1024,1024]{1,0:T(8,128)(2,1)}, bf16[3,16,96,128]{3,2,1,0:T(8,128)(2,1...) custom-call(s32[3,34]{1,0:T(4,128)} %pad_add_fusion.refs_0_, ...), custom_call_target="tpu_custom_call" | custom-call | tf_op jit(solution)/shard_map/forward/pallas_call | solution.py:808
  92.4 168.2 %backward.1 = (bf16[192,1024]{1,0:T(8,128)(2,1)}, bf16[2,8,64,2048]{3,2,1,0:T(8,128)(2,1)}, bf16[2,8,64,2048]{3,2,1,0:T(8,128)(2,1)}, bf16[2,8,128,1024]{3,2,1,0:T(8,128)(2,1)}, f32[12,512]{1,0:T(8,128)}) custom-call(s32[3,34]{1,0:T(4,128)} %pad_add_fusion.refs_0_, bf16[192,1024]{1,0:T(8,128)(2,1)} %get-tuple-element.53.refs_1_, ...), custom_call_target="tpu_custom_call" | custom-call | tf_op jit(solution)/shard_map/backward/pallas_call | solution.py:1253
  260.6 0.0 copy-start
  260.6 0.0 copy-start.1
  260.6 14.0 %widen.1 = (f32[512,1024]{1,0:T(8,128)}, f32[512,1024]{1,0:T(8,128)}, f32[512,1024]{1,0:T(8,128)}, f32[512,1024]{1,0:T(8,128)}, f32[512,4096]{1,0:T(8,128)}, /*i...) custom-call(bf16[2,8,64,2048]{3,2,1,0:T(8,128)(2,1)} %get-tuple-elem, ...), custom_call_target="tpu_custom_call" | custom-call | tf_op jit(solution)/shard_map/widen/pallas_call | solution.py:1300
  274.6 0.0 copy-done
  274.6 0.7 copy.43
  275.4 0.0 copy-done.1
  275.4 0.7 copy.44
Async XLA Ops:
  260.6 14.0 %copy-start = (bf16[192,1024]{1,0:T(8,128)(2,1)S(1)}, bf16[192,1024]{1,0:T(8,128)(2,1)}, u32[]{:S(2)}) copy-start(bf16[192,1024]{1,0:T(8,128)(2,1)} %get-tuple-element.52) | copy-start | bytes 1179652
  260.6 14.8 %copy-start.1 = (bf16[192,1024]{1,0:T(8,128)(2,1)S(1)}, bf16[192,1024]{1,0:T(8,128)(2,1)}, u32[]{:S(2)}) copy-start(bf16[192,1024]{1,0:T(8,128)(2,1)} %get-tuple-element.67) | copy-start | bytes 1179652

commit v10 on v9

--- a/solution.py
+++ b/solution.py
@@ -410,7 +410,48 @@
     return copy
 
 
-SEQS = HEADS // BPS
+class Dealing:
+    def __init__(self, lengths_hbm, dealing_hbm, lengths, dealing, slots, sems):
+        self.lengths, self.dealing, self.slots = lengths, dealing, slots
+        self.copies = (
+            pltpu.make_async_copy(lengths_hbm, lengths, sems.at[0]),
+            pltpu.make_async_copy(dealing_hbm, dealing, sems.at[1]),
+        )
+        for copy in self.copies:
+            copy.start()
+
+    def invert(self):
+        for copy in self.copies:
+            copy.wait()
+        micros, _, count = self.dealing.shape
+
+        def find(number, carry):
+            m, block = lax.div(number, count), lax.rem(number, count)
+            slot = jnp.int32(0)
+            for t in range(count):
+                slot = jnp.where(self.dealing[m, 0, t] == block, jnp.int32(t), slot)
+            self.slots[m, block] = slot
+            return carry
+
+        lax.fori_loop(0, micros * count, find, 0)
+
+    def length(self, m, s):
+        return self.lengths[0, s, m]
+
+    def block(self, m, t):
+        return self.dealing[m, 0, t]
+
+    def slot(self, m, b):
+        return self.slots[m, b]
+
+
+def dealing_scratch(lengths, dealing):
+    return [
+        pltpu.SMEM(lengths.shape, jnp.int32),
+        pltpu.SMEM(dealing.shape, jnp.int32),
+        pltpu.SMEM((dealing.shape[0], dealing.shape[2]), jnp.int32),
+        pltpu.SemaphoreType.DMA((2,)),
+    ]
 
 
 def plane_peers(c, w, count):
@@ -493,13 +534,14 @@
 
 
 def forward_kernel(heads, plan, n_weights, n_vectors, *refs):
-    table_ref, x_ref, cot_ref = refs[:3]
-    refs = refs[3:]
+    integers, (x_ref, cot_ref), refs = refs[:2], refs[2:4], refs[4:]
     shards, vectors = refs[:n_weights], refs[n_weights : n_weights + n_vectors]
     refs = refs[n_weights + n_vectors :]
-    wholes, kept_ref, lse_ref, a_ref = refs[:3], *refs[3:6]
-    out_ref, n_ref, g_ref, do_ref, du_ref, dm_ref, dh_ref, da_ref, vec_ref = refs[6:15]
-    refs = refs[15:]
+    wholes, kept_ref, lse_ref = refs[:3], *refs[3:5]
+    results, refs = refs[5:15], refs[15:]
+    a_ref, out_ref, n_ref, g_ref, do_ref, du_ref, dm_ref, dh_ref, da_ref, vec_ref = refs[:10]
+    made, result_sem, refs = refs[:10], refs[10], refs[11:]
+    dealt, refs = Dealing(*integers, *refs[:4]), refs[4:]
     near, refs = refs[:n_weights], refs[n_weights:]
     small, small_in, small_whole, bias, q_ref, k_ref, v_ref = refs[:7]
     slope, n_full, unit, total = refs[7:11]
@@ -523,6 +565,14 @@
     by_x, by_y, by_z, by_core = (c, o), (flip(c, 2), w), (flip(c, 4), w), (flip(c, 1), w)
     core, y, z = bit_of(c, 1), bit_of(c, 2), bit_of(c, 4)
     peers = plane_peers(c, w, heads)
+    stores = []
+
+    def store(target):
+        index = [item is target for item in made].index(True)
+        copy = pltpu.make_async_copy(target, results[index], result_sem.at[index])
+        copy.start()
+        stores.append(copy)
+
     staged = []
     for index, shard in enumerate(shards):
         rows = shard.shape[0]
@@ -563,6 +613,7 @@
         size, mine = rows // way[0], own_piece(way)
         src = shards[tensor].at[pl.ds(pl.multiple_of(first + mine * size, 8), size)]
         steps[chunk, 0] = send(src, part(chunk, w, mine, 0, size), *sem(0, chunk), by_x)
+    dealt.invert()
 
     def second(chunk):
         _, _, rows, way = plan[chunk]
@@ -636,7 +687,7 @@
         all_bytes(in_buf[m], recv_sem.at[m], heads - 1).wait()
         pltpu.make_async_copy(in_buf[m], kept_ref.at[m], keep_sem.at[m]).start()
         for b in range(blocks):
-            got = in_buf[m][table_ref[m, SEQS + blocks + b]]
+            got = in_buf[m][dealt.slot(m, b)]
             q_s[b * BLK : (b + 1) * BLK, :] = got[:BLK, :HD]
             k_s[b * BLK : (b + 1) * BLK, :] = got[:BLK, HD:]
             v_s[b * BLK : (b + 1) * BLK, :] = unpack_fold(got[BLK:])
@@ -647,7 +698,7 @@
                 k_s[rows, :], q_s[rows, :], (((1,), (1,)), ((), ())), preferred_element_type=F32
             ) * (1.0 / math.sqrt(HD))
             place = lax.broadcasted_iota(jnp.int32, scores.shape, 0)
-            scores = jnp.where(place < table_ref[m, s], scores, NEG_FILL)
+            scores = jnp.where(place < dealt.length(m, s), scores, NEG_FILL)
             top = jnp.max(scores, axis=0, keepdims=True)
             weights = jnp.exp(scores - top)
             summed = jnp.sum(weights, axis=0, keepdims=True)
@@ -663,7 +714,7 @@
 
         lax.fori_loop(0, blocks // BPS, one_sequence, 0)
         for t in range(blocks):
-            back_out[m, t] = fold(a_s[table_ref[m, SEQS + t]]).astype(BF16)
+            back_out[m, t] = fold(a_s[dealt.block(m, t)]).astype(BF16)
         for peer in peers:
             send(
                 back_out.at[m, peer[0]], back_in.at[m, c], back_send.at[m], back_recv.at[m], peer
@@ -678,6 +729,7 @@
                     [unpack_fold(back_in[m, 2 * pair]), unpack_fold(back_in[m, 2 * pair + 1])],
                     axis=1,
                 )
+        store(a_ref)
 
     def line_of(row):
         return jnp.concatenate(
@@ -707,6 +759,7 @@
         n_one = unit_one * line_of(ROW_GAIN_ONE) + line_of(ROW_SHIFT_ONE)
         n_full[...] = n_one
         n_ref[...] = n_one.astype(BF16)
+        store(n_ref)
         total[...] = jnp.zeros_like(total)
         kept_scale.append(scale_one)
 
@@ -751,15 +804,18 @@
     for name, value in FORWARD_SCHEDULE:
         acts[name](value)
 
+    store(g_ref)
     h_two = n_full[...] + (total[...] + line_of(ROW_DOWN))
     unit_two, scale_two = norm_parts(h_two)
     out_ref[...] = (unit_two * line_of(ROW_GAIN_TWO) + line_of(ROW_SHIFT_TWO)).astype(BF16)
+    store(out_ref)
     cot = cot_ref[...].astype(F32)
     keep(ROW_GAIN_TWO, cot * unit_two)
     keep(ROW_SHIFT_TWO, cot)
     dh_two = norm_back(cot, unit_two, scale_two, line_of(ROW_GAIN_TWO))
     dm = dh_two.astype(BF16)
     dm_ref[...] = dm
+    store(dm_ref)
     keep(ROW_DOWN, dm.astype(F32))
     total[...] = dh_two
     for turn in range(hidden_steps):
@@ -768,17 +824,22 @@
         du_ref[:, cols] = du
         vec_ref[side, row, :] = jnp.sum(du.astype(F32), axis=0, keepdims=True)
         total[...] += dot_minor(du, up_w[:, cols])
+    store(du_ref)
     dn = total[...]
     keep(ROW_GAIN_ONE, dn * unit[...])
     keep(ROW_SHIFT_ONE, dn)
     dh_one = norm_back(dn, unit[...], kept_scale[0], line_of(ROW_GAIN_ONE))
     dh_ref[...] = dh_one
+    store(dh_ref)
     do = dh_one.astype(BF16)
     do_ref[...] = do
+    store(do_ref)
     keep(ROW_OUT, do.astype(F32))
-    da_ref[...] = dot_minor(do, out_w[...]).astype(BF16)
     for side in range(2):
         vec_ref[side, 0:ROW_OUT, :] = jnp.zeros((ROW_OUT, lanes), F32)
+    store(vec_ref)
+    da_ref[...] = dot_minor(do, out_w[...]).astype(BF16)
+    store(da_ref)
 
     for m in range(MB):
         all_bytes(out_buf.at[m], send_sem.at[m], heads - 1).wait()
@@ -786,15 +847,16 @@
         pltpu.make_async_copy(in_buf[m], kept_ref.at[m], keep_sem.at[m]).wait()
     for flight in steps.values():
         flight.wait_send()
+    for copy in stores:
+        copy.wait()
     for index in range(3):
         pltpu.make_async_copy(near[index], wholes[index], local_sem.at[index]).wait()
 
 
-def forward(table, x, cot, shards, vectors, heads):
+def forward(lengths, dealing, x, cot, shards, vectors, heads):
     plan = weight_plan(shards)
     count = len(shards)
     anywhere, vmem = pl.BlockSpec(memory_space=pl.ANY), pl.BlockSpec(memory_space=pltpu.VMEM)
-    smem = pl.BlockSpec(memory_space=pltpu.SMEM)
     rows, width = x.shape
     hidden = shards[4].shape[1]
     pack_rows = BLK + BLK // 2
@@ -805,26 +867,24 @@
     low = lambda cols: jax.ShapeDtypeStruct((rows, cols), BF16)
     full = lambda cols: pltpu.VMEM((rows, cols), F32)
     sems = lambda *dims: pltpu.SemaphoreType.DMA(dims)
+    kept_shapes = [
+        jax.ShapeDtypeStruct((MB, heads, pack_rows, 128), BF16),
+        jax.ShapeDtypeStruct((8, span), F32),
+    ]
+    results = [low(width)] * 3 + [low(hidden), low(width), low(hidden), low(width)]
+    results += [jax.ShapeDtypeStruct((rows, width), F32), low(width)]
+    results += [jax.ShapeDtypeStruct((2, lines, lanes), F32)]
     return pl.pallas_call(
         functools.partial(forward_kernel, heads, plan, count, len(vectors)),
         out_shape=[jax.ShapeDtypeStruct(whole(s), s.dtype) for s in shards[:3]]
-        + [
-            jax.ShapeDtypeStruct((MB, heads, pack_rows, 128), BF16),
-            jax.ShapeDtypeStruct((8, span), F32),
-            low(width),
-            low(width),
-            low(width),
-            low(hidden),
-            low(width),
-            low(hidden),
-            low(width),
-            jax.ShapeDtypeStruct((rows, width), F32),
-            low(width),
-            jax.ShapeDtypeStruct((2, lines, lanes), F32),
-        ],
-        in_specs=[smem, vmem, vmem] + [anywhere] * count + [vmem] * len(vectors),
-        out_specs=[anywhere] * 4 + [vmem] * 11,
-        scratch_shapes=[pltpu.VMEM(whole(s), s.dtype) for s in shards]
+        + kept_shapes
+        + results,
+        in_specs=[anywhere] * 2 + [vmem] * 2 + [anywhere] * count + [vmem] * len(vectors),
+        out_specs=[anywhere] * 4 + [vmem] + [anywhere] * 10,
+        scratch_shapes=[pltpu.VMEM(item.shape, item.dtype) for item in results]
+        + [sems(len(results))]
+        + dealing_scratch(lengths, dealing)
+        + [pltpu.VMEM(whole(s), s.dtype) for s in shards]
         + [pltpu.VMEM((lines, lanes), F32)] * 2
         + [pltpu.VMEM((2, lines, lanes), F32), pltpu.VMEM((2, width), F32)]
         + [pltpu.VMEM((rows, width), BF16)] * 3
@@ -845,25 +905,25 @@
             collective_id=1, has_side_effects=True, vmem_limit_bytes=VMEM_BYTES
         ),
         name="forward",
-    )(table, x, cot, *shards, *vectors)
+    )(lengths, dealing, x, cot, *shards, *vectors)
 
 
 ORDERS = (
-    ("yxzZ", "xyzZ", "xyzZ", "xyzZ"),
-    ("xzyZ", "xyzZ", "yxzZ", "zxyZ"),
-    ("yZz", "yzZ", "yZz", "zyZ"),
+    ("yxZz", "xyzZ", "xyzZ", "xyzZ"),
+    ("yxzZ", "zxyZ", "xyzZ", "xyzZ"),
+    ("yZz", "zyZ", "zyZ", "yzZ"),
 )
 PIECES = len(ORDERS[0])
 SCHEDULE = (
-    "up", 0, 1, (1, 2), 2, "down", "back", (2, 0), (1, 0), (2, 3), "qkv", (2, 1), (1, 3),
-    (2, 2), (1, 1), (1, 2), (2, 0), (2, 1), (1, 0), (2, 3), "vec", (2, 2), (2, 0), (2, 1),
-    (2, 2), (1, 2), (0, 1), (2, 1), (2, 3), (1, 2), (2, 2), (2, 1), (0, 0), "vec", (0, 2),
-    (1, 0), (2, 0), (1, 2), (2, 3), (0, 1), (1, 1), (0, 3), (2, 1), (0, 2), (0, 1), (1, 1),
-    "vec", (1, 3), (0, 2), (0, 3), (2, 0), (1, 1), (0, 2), (0, 0), (1, 2), (2, 2), (0, 3),
-    (1, 1), (1, 3), (0, 0), "vec", (0, 1), (1, 2), (0, 2), (0, 3), (1, 1), (1, 0), (0, 1),
-    (0, 0), (2, 0), (0, 2), (0, 3), (1, 3), (2, 3), (0, 1), (1, 3), "vec", (1, 1), (0, 0),
-    (0, 2), (1, 0), (0, 3), (1, 3), (1, 0), (2, 3), (0, 0), (0, 3), "rows", (1, 3), (0, 1),
-    (2, 2), (1, 0), (0, 0),
+    "up", 0, 1, 2, (1, 0), "down", (1, 2), "back", (2, 0), (2, 1), "qkv", (2, 3), (2, 0),
+    (2, 1), (2, 3), (1, 2), (1, 0), (2, 3), (2, 2), (1, 2), "vec", (2, 1), (1, 3), (2, 3),
+    (0, 1), (2, 0), (1, 2), (2, 2), (1, 3), (1, 0), (2, 3), (1, 2), (2, 0), "vec", (1, 3),
+    (2, 2), (0, 2), "rows", (0, 1), (2, 3), (2, 0), (1, 1), (0, 2), (1, 0), (0, 3), (0, 1),
+    "vec", (1, 3), (0, 0), (1, 1), (1, 2), (1, 0), (0, 1), (0, 3), (0, 2), (1, 1), (0, 1),
+    (2, 1), (0, 0), (2, 2), "vec", (1, 0), (1, 2), (0, 2), (0, 3), (0, 0), (0, 1), (1, 3),
+    (0, 2), (1, 1), (0, 3), (1, 3), (1, 0), (0, 0), (2, 2), (1, 1), "vec", (0, 2), (0, 3),
+    (0, 0), (1, 1), (2, 1), (2, 2), (0, 1), (2, 0), (0, 3), (0, 2), (0, 0), (1, 3), (0, 3),
+    (1, 1), (2, 1), (0, 0),
 )
 KEYS = tuple((part, piece) for part in range(3) for piece in range(PIECES))
 
@@ -888,11 +948,24 @@
 
 
 def backward_kernel(heads, *refs):
-    table_ref, da_ref, kept_ref, lse_ref = refs[:4]
-    x_ref, a_ref, n_ref, g_ref, do_ref, du_ref, dm_ref, vec_ref, dh_ref = refs[4:13]
-    weights = refs[13:16]
-    rows_out, o_a, o_b, o_c, vec_out = refs[16:21]
-    refs = refs[21:]
+    integers, operands, weights = refs[:2], refs[2:14], refs[14:17]
+    rows_out, o_a, o_b, o_c, vec_out = refs[17:22]
+    held, load_sem, refs = refs[22:34], refs[34], refs[35:]
+    dealt, refs = Dealing(*integers, *refs[:4]), refs[4:]
+    da_ref, g_ref, dm_ref, n_ref, du_ref, kept_ref = held[:6]
+    lse_ref, a_ref, do_ref, x_ref, vec_ref, dh_ref = held[6:]
+    loads = []
+    for index, (source, target) in enumerate(zip(operands, held)):
+        copy = pltpu.make_async_copy(source, target, load_sem.at[index])
+        copy.start()
+        loads.append((target, copy))
+
+    def ready(*targets):
+        for item in list(loads):
+            if any(item[0] is target for target in targets):
+                item[1].wait()
+                loads.remove(item)
+
     in_buf = refs[:MB]
     out_buf, back_out, back_in, q_s, k_s, v_s, a_s, dq_s, dk_s, dv_s = refs[MB : MB + 10]
     refs = refs[MB + 10 :]
@@ -933,6 +1006,7 @@
     by_cross = (flip(c, 1), 1 - x)
     greet(peers + [by["x"], by_cross])
 
+    ready(da_ref)
     for m in range(MB):
         row = slice(m * BLK, (m + 1) * BLK)
         for pair in range(heads // 2):
@@ -955,16 +1029,20 @@
     def hidden_rows(side, which):
         return g_ref.at[:, lanes_at(side * 2 * quarter + which * quarter, quarter)]
 
+    ready(g_ref, dm_ref)
     share("far_g", hidden_rows(1 - x, core), far_g, by["x"])
     share("far_dm", dm_ref, far_dm, by["x"])
     share("cross_g", hidden_rows(1 - x, other), cross_g, by_cross)
+    ready(n_ref, du_ref)
     share("n", n_ref, m_n)
     share("du", du_ref.at[:, lanes_at(other * (hidden // 2), hidden // 2)], m_du)
     share("g", hidden_rows(x, other), m_g)
     share("dm", dm_ref, m_dm)
+    ready(*held)
     share("a", a_ref, m_a)
     share("do", do_ref.at[:, lanes_at(other * (width // 2), width // 2)], m_do)
     share("x", x_ref, m_x)
+    dealt.invert()
 
     sums, outs = (s_a, s_b, s_c), (o_a, o_b, o_c)
     wide = 512
@@ -1006,7 +1084,7 @@
     def attention(m):
         all_bytes(in_buf[m], recv_sem.at[m], heads - 1).wait()
         for b in range(blocks):
-            slot = table_ref[m, SEQS + blocks + b]
+            slot = dealt.slot(m, b)
             got = kept_ref[m, slot]
             rows = slice(b * BLK, (b + 1) * BLK)
             q_s[rows, :] = got[:BLK, :HD]
@@ -1022,7 +1100,7 @@
             scores = lax.dot_general(kk, qq, minor, preferred_element_type=F32) * scale
             spot = lax.broadcasted_iota(jnp.int32, scores.shape, 0)
             total = lse_ref[pl.ds(m * (blocks // BPS) + s, 1), :]
-            probs = jnp.exp(jnp.where(spot < table_ref[m, s], scores - total, NEG_FILL))
+            probs = jnp.exp(jnp.where(spot < dealt.length(m, s), scores - total, NEG_FILL))
             dp = lax.dot_general(vv, dd, minor, preferred_element_type=F32)
             both = probs * dp
             delta = jnp.sum(both, axis=0, keepdims=True)
@@ -1036,7 +1114,7 @@
 
         lax.fori_loop(0, blocks // BPS, one_sequence, 0)
         for t in range(blocks):
-            at = table_ref[m, SEQS + t]
+            at = dealt.block(m, t)
             back_out[m, t, 0:BLK, :] = jnp.concatenate([dq_s[at], dk_s[at]], axis=1).astype(BF16)
             back_out[m, t, BLK:, :] = fold(dv_s[at]).astype(BF16)
         for peer in peers:
@@ -1223,16 +1301,19 @@
         flight.wait_send()
 
 
-def backward(table, da, kept, lse, x, a, n1, g, do, du, dm, vec, dh, weights, heads):
-    vmem, smem = pl.BlockSpec(memory_space=pltpu.VMEM), pl.BlockSpec(memory_space=pltpu.SMEM)
-    anywhere = pl.BlockSpec(memory_space=pl.ANY)
+def backward(lengths, dealing, da, kept, lse, x, a, n1, g, do, du, dm, vec, dh, weights, heads):
+    vmem, anywhere = pl.BlockSpec(memory_space=pltpu.VMEM), pl.BlockSpec(memory_space=pl.ANY)
     rows, width = da.shape
     hidden = g.shape[1]
     pack_rows = BLK + BLK // 2
     low = lambda *dims: pltpu.VMEM(dims, BF16)
+    operands = (da, g, dm, n1, du, kept, lse, a, do, x, vec, dh)
     a_shape, b_shape = (2, 8, width // 16, 2 * width), (2, 8, width // 16, hidden // 2)
     c_shape = (1, 8, hidden // 32, width)
-    scratch = [low(heads, BLK // 2, 128)] * MB
+    scratch = [pltpu.VMEM(item.shape, item.dtype) for item in operands]
+    scratch += [pltpu.SemaphoreType.DMA((len(operands),))]
+    scratch += dealing_scratch(lengths, dealing)
+    scratch += [low(heads, BLK // 2, 128)] * MB
     scratch += [low(MB, heads, BLK // 2, 128)]
     scratch += [low(MB, heads, pack_rows, 128)] * 2
     scratch += [low(heads * BLK, HD)] * 4
@@ -1259,17 +1340,20 @@
             jax.ShapeDtypeStruct((2,) + c_shape[1:], BF16),
             jax.ShapeDtypeStruct(vec.shape[1:], F32),
         ],
-        in_specs=[smem] + [vmem] * 12 + [anywhere] * 3,
+        in_specs=[anywhere] * 17,
         out_specs=[vmem] + [anywhere] * 3 + [vmem],
         scratch_shapes=scratch,
         compiler_params=pltpu.CompilerParams(
             collective_id=2, has_side_effects=True, vmem_limit_bytes=VMEM_BYTES
         ),
         name="backward",
-    )(table, da, kept, lse, x, a, n1, g, do, du, dm, vec, dh, *weights)
-
-
-def widen_kernel(a_ref, b_ref, c_ref, vec_ref, *outs):
+    )(lengths, dealing, *operands, *weights)
+
+
+def widen_kernel(a_ref, b_ref, c_ref, vec_ref, one_ref, two_ref, one_out, two_out, *outs):
+    one_out[...] = one_ref[...]
+    two_out[...] = two_ref[...]
+
     @pl.when(pl.program_id(0) == 0)
     def _():
         line, lanes = 0, vec_ref.shape[1]
@@ -1291,25 +1375,29 @@
         down[core, 0] = c_ref[core, 0].astype(F32)
 
 
-def widen(o_a, o_b, o_c, vec, sizes):
+def widen(o_a, o_b, o_c, vec, sizes, one, two):
     shards = o_a.shape[1]
     block = lambda item: pl.BlockSpec((2, 1) + item.shape[2:], lambda i: (0, i, 0, 0))
     rows = o_a.shape[2]
     square = (shards * rows, o_a.shape[3] // 2)
     wide = (shards * rows, 2 * o_b.shape[3])
+    strip = pl.BlockSpec((one.shape[0] // shards, one.shape[1]), lambda i: (i, 0))
     return pl.pallas_call(
         widen_kernel,
         grid=(shards,),
-        out_shape=[jax.ShapeDtypeStruct(square, F32)] * 4
+        out_shape=[jax.ShapeDtypeStruct(one.shape, one.dtype)] * 2
+        + [jax.ShapeDtypeStruct(square, F32)] * 4
         + [jax.ShapeDtypeStruct(wide, F32), jax.ShapeDtypeStruct(o_c.shape, F32)]
         + [jax.ShapeDtypeStruct((size,), F32) for size in sizes],
-        in_specs=[block(o_a), block(o_b), block(o_c), pl.BlockSpec(vec.shape, lambda i: (0, 0))],
-        out_specs=[pl.BlockSpec((rows, square[1]), lambda i: (i, 0))] * 4
+        in_specs=[block(o_a), block(o_b), block(o_c), pl.BlockSpec(vec.shape, lambda i: (0, 0))]
+        + [strip] * 2,
+        out_specs=[strip] * 2
+        + [pl.BlockSpec((rows, square[1]), lambda i: (i, 0))] * 4
         + [pl.BlockSpec((rows, wide[1]), lambda i: (i, 0)), block(o_c)]
         + [pl.BlockSpec((size,), lambda i: (0,)) for size in sizes],
         compiler_params=pltpu.CompilerParams(vmem_limit_bytes=VMEM_BYTES),
         name="widen",
-    )(o_a, o_b, o_c, vec)
+    )(o_a, o_b, o_c, vec, one, two)
 
 
 def per_device_heads(tokens, cotangent, lengths, dealing, *params):
@@ -1319,15 +1407,13 @@
     weights, vectors = params[:6], params[6:]
     sizes = [item.shape[0] for item in vectors]
     x = tokens.reshape(rows, width)
-    blocks = jnp.arange(HEADS, dtype=jnp.int32)
-    at_block = dealing[0][:, :, None] == blocks[None, None, :]
-    slot_of = jnp.sum(jnp.where(at_block, blocks[None, :, None], 0), axis=1)
-    table = jnp.concatenate([lengths[0], dealing[0], slot_of], axis=1)
+    lengths, dealing = lengths.transpose(0, 2, 1), dealing.transpose(1, 0, 2)
     query_w, key_w, value_w, kept, lse, a, output, n_low, g, do, du, dm, dh_one, da, vec = forward(
-        table, x, cotangent.reshape(rows, width), weights, vectors, HEADS
+        lengths, dealing, x, cotangent.reshape(rows, width), weights, vectors, HEADS
     )
     grad_tokens, o_a, o_b, o_c, vec_sum = backward(
-        table,
+        lengths,
+        dealing,
         da,
         kept,
         lse,
@@ -1343,7 +1429,7 @@
         (query_w, key_w, value_w),
         HEADS,
     )
-    grads = list(widen(o_a, o_b, o_c, vec_sum, sizes))
+    output, grad_tokens, *grads = widen(o_a, o_b, o_c, vec_sum, sizes, output, grad_tokens)
     grads[5] = grads[5].reshape(-1, width)
     shape = (1, MB, rows_in, width)
     return (

time: 277 us -> 270 us (0.975)
  Pallas kernels: 272 us -> 269 us
  local copies, waits for them, and re-layouts: 2.95 us -> 0 us
where the time goes in v10:
time: 270 us
  Pallas kernels  269 us (100%)
    pallas_call x1, Pallas kernels, backward(): pl.pallas_call(functools.partial(backward_kernel, heads), out_shape=[jax....  166 us
    pallas_call x1, Pallas kernels, forward(): pl.pallas_call(functools.partial(forward_kernel, heads, plan, count, len(...  88.4 us
    pallas_call x1, Pallas kernels, widen(): pl.pallas_call(widen_kernel, grid=(shards,), out_shape=[jax.ShapeDtypeStr...  14.7 us

profile of v10, /device:TPU:0, one launch (start us, length us, event | category | flops | bytes accessed | tf_op | source)
XLA Modules:
  0.0 269.9 jit_solution(15279045376333941744)
XLA Ops:
  0.7 88.4 %forward.1 = (bf16[1024,1024]{1,0:T(8,128)(2,1)}, bf16[1024,1024]{1,0:T(8,128)(2,1)}, bf16[1024,1024]{1,0:T(8,128)(2,1)}, bf16[3,16,96,128]{3,2,1,0:T(8,128)(2,1...) custom-call(s32[1,2,3]{2,1,0:T(2,128)} %bitcast.12, ...), custom_call_target="tpu_custom_call" | custom-call | tf_op jit(solution)/shard_map/forward/pallas_call | solution.py:877
  89.0 166.0 %backward.1 = (bf16[192,1024]{1,0:T(8,128)(2,1)}, bf16[2,8,64,2048]{3,2,1,0:T(8,128)(2,1)}, bf16[2,8,64,2048]{3,2,1,0:T(8,128)(2,1)}, bf16[2,8,128,1024]{3,2,1,0:T(8,128)(2,1)}, f32[12,512]{1,0:T(8,128)}) custom-call(s32[1,2,3]{2,1,0:T(2,128)} %bitcast.13, s32[3,1,16]{2,1,0:T(1,128)} %bitcast.11, bf16[192,1024]{1,0:T(8,128)(2,1)} %get-tuple-element.54.refs_2_, ...), custom_call_target="tpu_custom_call" | custom-call | tf_op jit(solution)/shard_map/backward/pallas_call | solution.py:1334
  255.1 14.7 %widen.1 = (bf16[192,1024]{1,0:T(8,128)(2,1)}, bf16[192,1024]{1,0:T(8,128)(2,1)}, f32[512,1024]{1,0:T(8,128)}, f32[512,1024]{1,0:T(8,128)}, f32[512,1024]{1,0:T(...) custom-call(bf16[2,8,64,2048]{3,2,1,0:T(8,128)(2,1)} %get-tuple-elem, ...), custom_call_target="tpu_custom_call" | custom-call | tf_op jit(solution)/shard_map/widen/pallas_call | solution.py:1385

commit v11 on v10

--- a/solution.py
+++ b/solution.py
@@ -458,16 +458,19 @@
     return [(lax.rem(c + step, count), w) for step in range(1, count)]
 
 
-def pack_three(first, second, third, row, pair, out):
+def pack_two(first, second, row, pair, out):
     cols = pl.ds(pair * 128, 128)
-    a, b, d = (ref[pl.ds(row, BLK), cols] for ref in (first, second, third))
-    half = BLK // 2
+    a, b = first[pl.ds(row, BLK), cols], second[pl.ds(row, BLK), cols]
     for head in range(2):
         lane = slice(head * HD, head * HD + HD)
         out[2 * pair + head, 0:BLK, :] = jnp.concatenate([a[:, lane], b[:, lane]], axis=1)
-        out[2 * pair + head, BLK : BLK + half, :] = jnp.concatenate(
-            [d[:half, lane], d[half:, lane]], axis=1
-        )
+
+
+def pack_one(source, row, pair, out):
+    both = source[pl.ds(row, BLK), pl.ds(pair * 128, 128)]
+    for head in range(2):
+        lane = slice(head * HD, head * HD + HD)
+        out[2 * pair + head, BLK : BLK + BLK // 2, :] = fold(both[:, lane])
 
 
 def unpack_fold(block):
@@ -508,18 +511,19 @@
 
 SQUARE, PAIR_Y, PAIR_Z, ALONE = (8, "yz"), (4, "y"), (4, "z"), (2, "")
 WAYS = (
-    SQUARE, SQUARE, SQUARE, SQUARE, PAIR_Y, SQUARE, PAIR_Z, PAIR_Y, ALONE, PAIR_Z, PAIR_Y, ALONE,
+    SQUARE, SQUARE, SQUARE, ALONE, PAIR_Y, PAIR_Y, SQUARE, SQUARE, SQUARE, PAIR_Z, ALONE, PAIR_Y,
 )
-SEND_ORDER = (2, 0, 1, 3, 5, 7, 4, 6, 9, 10, 8, 11)
+SEND_ORDER = (1, 0, 2, 7, 6, 5, 11, 9, 4, 8, 3, 10)
 FORWARD_SCHEDULE = (
-    ("second", 2), ("second", 0), ("third", 2), ("second", 1), ("third", 0), ("fourth", 2),
-    ("third", 1), ("second", 3), ("second", 5), ("fourth", 0), ("project", 2), ("fourth", 1),
-    ("project", 0), ("project", 1), ("pack", 0), ("second", 7), ("third", 3), ("second", 4),
-    ("second", 6), ("att", 0), ("fourth", 7), ("third", 5), ("fourth", 3), ("att", 1), ("att",
-    2), ("fourth", 5), ("fourth", 8), ("second", 10), ("second", 9), ("fourth", 6), ("fourth",
-    4), ("rows", 0), ("out", 0), ("hidden", 0), ("fourth", 10), ("hidden", 1), ("hidden", 2),
-    ("fourth", 9), ("hidden", 3), ("hidden", 4), ("fourth", 11), ("hidden", 5), ("hidden", 6),
-    ("hidden", 7),
+    ("own", 0), ("own", 1), ("own", 2), ("second", 1), ("second", 0), ("third", 1), ("third",
+    0), ("second", 2), ("fourth", 1), ("project", 1), ("second", 7), ("fourth", 0), ("third",
+    2), ("project", 0), ("keys", 0), ("keys", 1), ("third", 7), ("second", 6), ("fourth", 2),
+    ("project", 2), ("values", 0), ("values", 1), ("keys", 2), ("second", 5), ("values", 2),
+    ("att", 0), ("second", 8), ("att", 1), ("second", 4), ("fourth", 7), ("att", 2), ("fourth",
+    5), ("fourth", 3), ("third", 6), ("third", 8), ("second", 9), ("fourth", 4), ("rows", 0),
+    ("second", 11), ("fourth", 6), ("out", 0), ("hidden", 0), ("hidden", 1), ("fourth", 8),
+    ("hidden", 2), ("fourth", 9), ("hidden", 3), ("fourth", 10), ("hidden", 4), ("fourth", 11),
+    ("hidden", 5), ("hidden", 6), ("hidden", 7),
 )
 
 
@@ -544,8 +548,8 @@
     dealt, refs = Dealing(*integers, *refs[:4]), refs[4:]
     near, refs = refs[:n_weights], refs[n_weights:]
     small, small_in, small_whole, bias, q_ref, k_ref, v_ref = refs[:7]
-    slope, n_full, unit, total = refs[7:11]
-    refs = refs[11:]
+    begun, slope, n_full, unit, total = refs[7:12]
+    refs = refs[12:]
     in_buf = refs[:MB]
     out_buf, back_out, back_in, q_s, k_s, v_s, a_s = refs[MB : 7 + MB]
     (
@@ -644,6 +648,23 @@
     step = 256
     projected = []
 
+    def half_product(index, side, cols):
+        rows = shards[index].shape[0]
+        lanes_in = pl.ds(pl.multiple_of(side * rows, rows), rows)
+        return jnp.dot(
+            x_ref[:, lanes_in], near[index][lanes_in, cols], preferred_element_type=F32
+        )
+
+    def own_half(index):
+        staged[index].wait()
+
+        def some_columns(turn, carry):
+            cols = pl.ds(pl.multiple_of(turn * step, step), step)
+            begun[index, :, cols] = half_product(index, w, cols)
+            return carry
+
+        lax.fori_loop(0, width // step, some_columns, 0)
+
     def project(index):
         if not projected:
             small_sent.wait()
@@ -655,13 +676,12 @@
                         side, row : row + 1, :
                     ]
         projected.append(index)
-        staged[index].wait()
         steps[index, 5].wait_recv()
-        weight, out = near[index], (q_ref, k_ref, v_ref)[index]
+        out = (q_ref, k_ref, v_ref)[index]
 
         def some_columns(turn, carry):
             cols = pl.ds(pl.multiple_of(turn * step, step), step)
-            product = jnp.dot(x_ref[...], weight[:, cols], preferred_element_type=F32)
+            product = begun[index, :, cols] + half_product(index, o, cols)
             if index != 1:
                 product = product + bias[index // 2 : index // 2 + 1, cols]
             out[:, cols] = product.astype(BF16)
@@ -670,15 +690,25 @@
         lax.fori_loop(0, width // step, some_columns, 0)
         pltpu.make_async_copy(near[index], wholes[index], local_sem.at[index]).start()
 
-    def pack(_):
-        for m in range(MB):
-            for pair in range(heads // 2):
-                pack_three(q_ref, k_ref, v_ref, m * BLK, pair, out_buf.at[m])
-            for peer in peers:
-                send(
-                    out_buf.at[m, peer[0]], in_buf[m].at[c], send_sem.at[m], recv_sem.at[m], peer
-                )
-            in_buf[m][c] = out_buf[m, c]
+    def pack(item, first, count, fill):
+        for pair in range(heads // 2):
+            fill(item, pair)
+        rows = pl.ds(first, count)
+        for peer in peers:
+            send(
+                out_buf.at[item, peer[0], rows],
+                in_buf[item].at[c, rows],
+                send_sem.at[item],
+                recv_sem.at[item],
+                peer,
+            )
+        in_buf[item][c, rows] = out_buf[item, c, rows]
+
+    def pack_keys(m):
+        pack(m, 0, BLK, lambda m, pair: pack_two(q_ref, k_ref, m * BLK, pair, out_buf.at[m]))
+
+    def pack_values(m):
+        pack(m, BLK, BLK // 2, lambda m, pair: pack_one(v_ref, m * BLK, pair, out_buf.at[m]))
 
     blocks = heads
     span = BPS * BLK
@@ -795,7 +825,9 @@
         "third": third,
         "fourth": fourth,
         "project": project,
-        "pack": pack,
+        "own": own_half,
+        "keys": pack_keys,
+        "values": pack_values,
         "att": attention,
         "rows": come_back,
         "out": out_project,
@@ -888,6 +920,7 @@
         + [pltpu.VMEM((lines, lanes), F32)] * 2
         + [pltpu.VMEM((2, lines, lanes), F32), pltpu.VMEM((2, width), F32)]
         + [pltpu.VMEM((rows, width), BF16)] * 3
+        + [pltpu.VMEM((3, rows, width), F32)]
         + [full(hidden), full(width), full(width), full(width)]
         + [pltpu.VMEM((heads, pack_rows, 128), BF16)] * MB
         + [
@@ -1365,26 +1398,28 @@
     half = outs[0].shape[1] // 2
     for index, out in enumerate(outs[:4]):
         for core in range(2):
-            out[:, core * half : (core + 1) * half] = a_ref[
-                core, 0, :, index * half : (index + 1) * half
-            ].astype(F32)
+            part = a_ref[core, :, :, index * half : (index + 1) * half]
+            out[:, core * half : (core + 1) * half] = part.astype(F32).reshape(-1, half)
     up, down = outs[4:6]
     half = up.shape[1] // 2
     for core in range(2):
-        up[:, core * half : (core + 1) * half] = b_ref[core, 0].astype(F32)
-        down[core, 0] = c_ref[core, 0].astype(F32)
+        part = b_ref[core].astype(F32)
+        up[:, core * half : (core + 1) * half] = part.reshape(-1, half)
+        down[core] = c_ref[core].astype(F32)
 
 
 def widen(o_a, o_b, o_c, vec, sizes, one, two):
     shards = o_a.shape[1]
-    block = lambda item: pl.BlockSpec((2, 1) + item.shape[2:], lambda i: (0, i, 0, 0))
-    rows = o_a.shape[2]
-    square = (shards * rows, o_a.shape[3] // 2)
-    wide = (shards * rows, 2 * o_b.shape[3])
-    strip = pl.BlockSpec((one.shape[0] // shards, one.shape[1]), lambda i: (i, 0))
+    turns = 2
+    share = shards // turns
+    block = lambda item: pl.BlockSpec((2, share) + item.shape[2:], lambda i: (0, i, 0, 0))
+    rows = o_a.shape[2] * share
+    square = (turns * rows, o_a.shape[3] // 2)
+    wide = (turns * rows, 2 * o_b.shape[3])
+    strip = pl.BlockSpec((one.shape[0] // turns, one.shape[1]), lambda i: (i, 0))
     return pl.pallas_call(
         widen_kernel,
-        grid=(shards,),
+        grid=(turns,),
         out_shape=[jax.ShapeDtypeStruct(one.shape, one.dtype)] * 2
         + [jax.ShapeDtypeStruct(square, F32)] * 4
         + [jax.ShapeDtypeStruct(wide, F32), jax.ShapeDtypeStruct(o_c.shape, F32)]

time: 270 us -> 266 us (0.985)
  Pallas kernels: 269 us -> 265 us
where the time goes in v11:
time: 266 us
  Pallas kernels  265 us (100%)
    pallas_call x1, Pallas kernels, backward(): pl.pallas_call(functools.partial(backward_kernel, heads), out_shape=[jax....  165 us
    pallas_call x1, Pallas kernels, forward(): pl.pallas_call(functools.partial(forward_kernel, heads, plan, count, len(...  88.3 us
    pallas_call x1, Pallas kernels, widen(): pl.pallas_call(widen_kernel, grid=(turns,), out_shape=[jax.ShapeDtypeStru...  12.1 us

profile of v11, /device:TPU:0, one launch (start us, length us, event | category | flops | bytes accessed | tf_op | source)
XLA Modules:
  0.0 266.3 jit_solution(13844882578791228904)
XLA Ops:
  0.7 88.3 %forward.1 = (bf16[1024,1024]{1,0:T(8,128)(2,1)}, bf16[1024,1024]{1,0:T(8,128)(2,1)}, bf16[1024,1024]{1,0:T(8,128)(2,1)}, bf16[3,16,96,128]{3,2,1,0:T(8,128)(2,1...) custom-call(s32[1,2,3]{2,1,0:T(2,128)} %bitcast.12, ...), custom_call_target="tpu_custom_call" | custom-call | tf_op jit(solution)/shard_map/forward/pallas_call | solution.py:909
  88.9 165.0 %backward.1 = (bf16[192,1024]{1,0:T(8,128)(2,1)}, bf16[2,8,64,2048]{3,2,1,0:T(8,128)(2,1)}, bf16[2,8,64,2048]{3,2,1,0:T(8,128)(2,1)}, bf16[2,8,128,1024]{3,2,1,0:T(8,128)(2,1)}, f32[12,512]{1,0:T(8,128)}) custom-call(s32[1,2,3]{2,1,0:T(2,128)} %bitcast.13, s32[3,1,16]{2,1,0:T(1,128)} %bitcast.11, bf16[192,1024]{1,0:T(8,128)(2,1)} %get-tuple-element.54.refs_2_, ...), custom_call_target="tpu_custom_call" | custom-call | tf_op jit(solution)/shard_map/backward/pallas_call | solution.py:1367
  254.0 12.1 %widen.1 = (bf16[192,1024]{1,0:T(8,128)(2,1)}, bf16[192,1024]{1,0:T(8,128)(2,1)}, f32[512,1024]{1,0:T(8,128)}, f32[512,1024]{1,0:T(8,128)}, f32[512,1024]{1,0:T(...) custom-call(bf16[2,8,64,2048]{3,2,1,0:T(8,128)(2,1)} %get-tuple-elem, ...), custom_call_target="tpu_custom_call" | custom-call | tf_op jit(solution)/shard_map/widen/pallas_call | solution.py:1420

commit v12 on v11

--- a/solution.py
+++ b/solution.py
@@ -942,21 +942,21 @@
 
 
 ORDERS = (
-    ("yxZz", "xyzZ", "xyzZ", "xyzZ"),
-    ("yxzZ", "zxyZ", "xyzZ", "xyzZ"),
-    ("yZz", "zyZ", "zyZ", "yzZ"),
+    ("xyzZ", "xyzZ", "yxzZ", "xyzZ"),
+    ("zxyZ", "yxzZ", "xyzZ", "xzyZ"),
+    ("yzZ", "zyZ", "yzZ", "yzZ"),
 )
 PIECES = len(ORDERS[0])
 SCHEDULE = (
-    "up", 0, 1, 2, (1, 0), "down", (1, 2), "back", (2, 0), (2, 1), "qkv", (2, 3), (2, 0),
-    (2, 1), (2, 3), (1, 2), (1, 0), (2, 3), (2, 2), (1, 2), "vec", (2, 1), (1, 3), (2, 3),
-    (0, 1), (2, 0), (1, 2), (2, 2), (1, 3), (1, 0), (2, 3), (1, 2), (2, 0), "vec", (1, 3),
-    (2, 2), (0, 2), "rows", (0, 1), (2, 3), (2, 0), (1, 1), (0, 2), (1, 0), (0, 3), (0, 1),
-    "vec", (1, 3), (0, 0), (1, 1), (1, 2), (1, 0), (0, 1), (0, 3), (0, 2), (1, 1), (0, 1),
-    (2, 1), (0, 0), (2, 2), "vec", (1, 0), (1, 2), (0, 2), (0, 3), (0, 0), (0, 1), (1, 3),
-    (0, 2), (1, 1), (0, 3), (1, 3), (1, 0), (0, 0), (2, 2), (1, 1), "vec", (0, 2), (0, 3),
-    (0, 0), (1, 1), (2, 1), (2, 2), (0, 1), (2, 0), (0, 3), (0, 2), (0, 0), (1, 3), (0, 3),
-    (1, 1), (2, 1), (0, 0),
+    "up", 0, 1, 2, "down", (1, 0), (2, 0), "back", (1, 2), (2, 2), (2, 0), (1, 1), (1, 3),
+    (2, 2), (2, 1), (2, 3), (2, 0), "qkv", (1, 1), (2, 3), (2, 2), (1, 3), (2, 0), (2, 3),
+    (1, 2), (0, 0), "vec", (2, 1), (1, 1), (2, 0), (1, 2), (1, 0), (2, 2), "rows", (0, 0),
+    (1, 3), (1, 2), (0, 1), "vec", (0, 0), (1, 1), (2, 3), (1, 3), (2, 2), (0, 2), (2, 1),
+    (0, 1), (0, 3), (1, 1), (0, 1), "vec", (1, 0), (2, 3), (0, 0), (1, 3), (0, 3), (0, 2),
+    (2, 0), (1, 1), (1, 0), (0, 3), (0, 2), (0, 0), "vec", (2, 1), (0, 1), (1, 2), (1, 0),
+    (0, 2), (0, 3), (0, 0), (0, 1), (1, 2), (2, 2), (0, 2), (0, 3), (2, 1), (0, 0), "vec",
+    (1, 1), (0, 1), (1, 0), (1, 3), (0, 2), (0, 3), (2, 3), (0, 1), (1, 0), (1, 2), (0, 2),
+    (2, 1), (0, 3), (1, 3),
 )
 KEYS = tuple((part, piece) for part in range(3) for piece in range(PIECES))
 

time: 266 us -> 264 us (level)
  no operation moved by 1% of the time
where the time goes in v12:
time: 264 us
  Pallas kernels  263 us (100%)
    pallas_call x1, Pallas kernels, backward(): pl.pallas_call(functools.partial(backward_kernel, heads), out_shape=[jax....  162 us
    pallas_call x1, Pallas kernels, forward(): pl.pallas_call(functools.partial(forward_kernel, heads, plan, count, len(...  88.3 us
    pallas_call x1, Pallas kernels, widen(): pl.pallas_call(widen_kernel, grid=(turns,), out_shape=[jax.ShapeDtypeStru...  12.1 us

profile of v12, /device:TPU:0, one launch (start us, length us, event | category | flops | bytes accessed | tf_op | source)
XLA Modules:
  0.0 263.6 jit_solution(6893138902051456797)
XLA Ops:
  0.7 88.3 %forward.1 = (bf16[1024,1024]{1,0:T(8,128)(2,1)}, bf16[1024,1024]{1,0:T(8,128)(2,1)}, bf16[1024,1024]{1,0:T(8,128)(2,1)}, bf16[3,16,96,128]{3,2,1,0:T(8,128)(2,1...) custom-call(s32[1,2,3]{2,1,0:T(2,128)} %bitcast.12, ...), custom_call_target="tpu_custom_call" | custom-call | tf_op jit(solution)/shard_map/forward/pallas_call | solution.py:909
  88.9 162.4 %backward.1 = (bf16[192,1024]{1,0:T(8,128)(2,1)}, bf16[2,8,64,2048]{3,2,1,0:T(8,128)(2,1)}, bf16[2,8,64,2048]{3,2,1,0:T(8,128)(2,1)}, bf16[2,8,128,1024]{3,2,1,0:T(8,128)(2,1)}, f32[12,512]{1,0:T(8,128)}) custom-call(s32[1,2,3]{2,1,0:T(2,128)} %bitcast.13, s32[3,1,16]{2,1,0:T(1,128)} %bitcast.11, bf16[192,1024]{1,0:T(8,128)(2,1)} %get-tuple-element.54.refs_2_, ...), custom_call_target="tpu_custom_call" | custom-call | tf_op jit(solution)/shard_map/backward/pallas_call | solution.py:1367
  251.3 12.1 %widen.1 = (bf16[192,1024]{1,0:T(8,128)(2,1)}, bf16[192,1024]{1,0:T(8,128)(2,1)}, f32[512,1024]{1,0:T(8,128)}, f32[512,1024]{1,0:T(8,128)}, f32[512,1024]{1,0:T(...) custom-call(bf16[2,8,64,2048]{3,2,1,0:T(8,128)(2,1)} %get-tuple-elem, ...), custom_call_target="tpu_custom_call" | custom-call | tf_op jit(solution)/shard_map/widen/pallas_call | solution.py:1420

commit v13 on v12

--- a/solution.py
+++ b/solution.py
@@ -394,7 +394,10 @@
     barrier = pltpu.get_barrier_semaphore()
     for peer in peers:
         pl.semaphore_signal(barrier, inc=1, device_id=peer, device_id_type=MESH_IDS)
-    pl.semaphore_wait(barrier, len(peers))
+
+
+def wait_for_all(peers):
+    pl.semaphore_wait(pltpu.get_barrier_semaphore(), len(peers))
 
 
 def send(src, dst, send_sem, recv_sem, peer):
@@ -577,6 +580,7 @@
         copy.start()
         stores.append(copy)
 
+    greet(peers + [by_x])
     staged = []
     for index, shard in enumerate(shards):
         rows = shard.shape[0]
@@ -590,7 +594,7 @@
             piece = vector[pl.ds(first, lanes)].astype(F32)
             small[line : line + 1, :] = piece.reshape(1, lanes)
             line += 1
-    greet(peers + [by_x])
+    wait_for_all(peers + [by_x])
     small_sent = send(small, small_in, small_sems.at[0], small_sems.at[1], by_x)
 
     def part(chunk, side, piece, start, count):
@@ -1032,13 +1036,12 @@
     by = {"x": (c, 1 - x), "y": (flip(c, 2), x), "z": (flip(c, 4), x), "Z": (flip(c, 8), x)}
     bits = {"y": y, "z": z, "Z": zz}
     peers = plane_peers(c, x, heads)
+    by_cross = (flip(c, 1), 1 - x)
+    greet(peers + [by["x"], by_cross])
     blocks, span = heads, BPS * BLK
     width, hidden = da_ref.shape[1], g_ref.shape[1]
     for index, weight in enumerate(weights):
         pltpu.make_async_copy(weight, near[index], near_sem.at[index]).start()
-    by_cross = (flip(c, 1), 1 - x)
-    greet(peers + [by["x"], by_cross])
-
     ready(da_ref)
     for m in range(MB):
         row = slice(m * BLK, (m + 1) * BLK)
@@ -1046,9 +1049,11 @@
             both = da_ref[row, pair * 128 : (pair + 1) * 128]
             for head in range(2):
                 out_buf[m, 2 * pair + head] = fold(both[:, head * HD : (head + 1) * HD])
+        in_buf[m][c] = out_buf[m, c]
+    wait_for_all(peers + [by["x"], by_cross])
+    for m in range(MB):
         for peer in peers:
             send(out_buf.at[m, peer[0]], in_buf[m].at[c], send_sem.at[m], recv_sem.at[m], peer)
-        in_buf[m][c] = out_buf[m, c]
 
     shared = {}
 

time: 264 us -> 264 us (level)
  no operation moved by 1% of the time
where the time goes in v13:
time: 264 us
  Pallas kernels  263 us (100%)
    pallas_call x1, Pallas kernels, backward(): pl.pallas_call(functools.partial(backward_kernel, heads), out_shape=[jax....  163 us
    pallas_call x1, Pallas kernels, forward(): pl.pallas_call(functools.partial(forward_kernel, heads, plan, count, len(...  88.2 us
    pallas_call x1, Pallas kernels, widen(): pl.pallas_call(widen_kernel, grid=(turns,), out_shape=[jax.ShapeDtypeStru...  12.1 us

profile of v13, /device:TPU:0, one launch (start us, length us, event | category | flops | bytes accessed | tf_op | source)
XLA Modules:
  0.0 264.2 jit_solution(4513627733745912597)
XLA Ops:
  0.7 88.2 %forward.1 = (bf16[1024,1024]{1,0:T(8,128)(2,1)}, bf16[1024,1024]{1,0:T(8,128)(2,1)}, bf16[1024,1024]{1,0:T(8,128)(2,1)}, bf16[3,16,96,128]{3,2,1,0:T(8,128)(2,1...) custom-call(s32[1,2,3]{2,1,0:T(2,128)} %bitcast.12, ...), custom_call_target="tpu_custom_call" | custom-call | tf_op jit(solution)/shard_map/forward/pallas_call | solution.py:913
  88.9 163.0 %backward.1 = (bf16[192,1024]{1,0:T(8,128)(2,1)}, bf16[2,8,64,2048]{3,2,1,0:T(8,128)(2,1)}, bf16[2,8,64,2048]{3,2,1,0:T(8,128)(2,1)}, bf16[2,8,128,1024]{3,2,1,0:T(8,128)(2,1)}, f32[12,512]{1,0:T(8,128)}) custom-call(s32[1,2,3]{2,1,0:T(2,128)} %bitcast.13, s32[3,1,16]{2,1,0:T(1,128)} %bitcast.11, bf16[192,1024]{1,0:T(8,128)(2,1)} %get-tuple-element.54.refs_2_, ...), custom_call_target="tpu_custom_call" | custom-call | tf_op jit(solution)/shard_map/backward/pallas_call | solution.py:1372
  251.9 12.1 %widen.1 = (bf16[192,1024]{1,0:T(8,128)(2,1)}, bf16[192,1024]{1,0:T(8,128)(2,1)}, f32[512,1024]{1,0:T(8,128)}, f32[512,1024]{1,0:T(8,128)}, f32[512,1024]{1,0:T(...) custom-call(bf16[2,8,64,2048]{3,2,1,0:T(8,128)(2,1)} %get-tuple-elem, ...), custom_call_target="tpu_custom_call" | custom-call | tf_op jit(solution)/shard_map/widen/pallas_call | solution.py:1425
